TPU v7x, 32 devices: a whole 2x2x4 slice. The times are simulated.
32 devices in a mesh: recv: 8 (over z, x), src: 4 (over y, core).
Axes of the slice: x: 2, y: 2, z: 4, core: 2. Of those that a mesh axis runs over, the one named last changes fastest.
Arguments:
- interactions: int32 [3, 3072], P(None, ('recv', 'src')), may hold values from 0 to 255, as said below
- list_lengths: int32 [32], P(('recv', 'src')), may hold values from 48 to 96, as said below
- kernels: float32 [128, 128, 16, 128], P(('recv', 'src')), may hold values from -0.0210316469 to 0.0210316469
- prestress: float32 [256, 128], P(('recv', 'src')), may hold values from 2 to 3
- friction: float32 [256, 128], P(('recv', 'src')), may hold values from 0.2 to 0.5
- load_rate: float32 [256, 128], P(('recv', 'src')), may hold values from 0.04 to 0.08
Outputs:
- slip_rates: float32 [256, 96, 128], P(('recv', 'src'))
Inputs may be any that keep to these rules, and one draw needn't show every extreme that they name: `interactions`: column e belongs to device block g = e // 96, g = i * 4 + j. Its receiver patch lies in [i * 4 * 8, (i + 1) * 4 * 8); its source patch p satisfies (p // 8) mod 4 == j; its owner is p // 32; its lag offset lies in [32, 48]. The entries of one block name at most 1 distinct source patches of one owner, and in every draw some owner supplies exactly that many distinct source patches to every block. `list_lengths`: some device's list is full and some device's list holds exactly half, in every draw.
All inputs are finite; a program needn't handle non-finite values.
Results may differ from a plain program's by a relative error of at most 0.0003.
Values sent between devices are 32-bit elements; how exact they have to be, the bound alone decides.
No kernel may reach another device: no remote copies, remote signals or barrier semaphores. Data moves between devices by JAX's collectives and lax.ppermute only.
A program may use at most 128 MiB of HBM per device.

v0:
```python
import functools

import jax
import jax.numpy as jnp
from jax import lax
from jax.experimental import pallas as pl
from jax.experimental.pallas import tpu as pltpu
from jax.sharding import PartitionSpec as P

BLOCK = 32
BLOCKS = 3
NEWTON = 4
damping = 0.5
VMEM = pl.BlockSpec(memory_space=pltpu.VMEM)
SMEM = pl.BlockSpec(memory_space=pltpu.SMEM)


def friction_solve(drive, friction):
    rates = drive / (damping + friction)
    for newton_step in range(NEWTON - 1):
        squares = 1.0 + rates * rates
        inverse_root = lax.rsqrt(squares)
        magnitude = jnp.log(jnp.abs(rates) + squares * inverse_root)
        inverse_sinh = jnp.where(rates < 0, -magnitude, magnitude)
        misfit = damping * rates + friction * inverse_sinh - drive
        rates = rates - misfit / (damping + friction * inverse_root)
    return rates


def times_of(block_idx, width):
    steps = lax.broadcasted_iota(jnp.int32, (BLOCK, width), 0)
    return (steps + (block_idx * BLOCK + 1)).astype(jnp.float32)


def split(values):
    high = values.astype(jnp.bfloat16)
    return high, (values - high.astype(jnp.float32)).astype(jnp.bfloat16)


def weights_kernel(kernel_ref, high_ref, low_ref):
    lag_count, width = kernel_ref.shape[2], kernel_ref.shape[3]
    for lag in range(lag_count):
        high, low = split(kernel_ref[0, :, lag, :].T)
        high_ref[lag * width : (lag + 1) * width, :] = high
        low_ref[lag * width : (lag + 1) * width, :] = low


def first_block_kernel(prestress_ref, friction_ref, load_ref, out_ref):
    patch_count, width = prestress_ref.shape
    times = times_of(0, width)
    for patch in range(patch_count):
        row = pl.ds(patch, 1)
        drive = prestress_ref[row, :] + load_ref[row, :] * times
        out_ref[patch] = friction_solve(drive, jnp.broadcast_to(friction_ref[row, :], drive.shape))


def convolve_and_route(
    window, stacked, responses, sums, high_ref, low_ref, table_ref, keep_ref, send_ref
):
    slots, span, width = window.shape
    history = span - BLOCK
    ker_count = responses.shape[0]
    lag_count = high_ref.shape[0] // width
    chunk = stacked.shape[0] // (2 * BLOCK)
    rows = chunk * BLOCK

    def one_chunk(chunk_idx, carry):
        first = chunk_idx * chunk
        for lag in range(lag_count):
            for slot in range(chunk):
                high, low = split(window[first + slot, history - lag : history - lag + BLOCK, :])
                cols = slice(lag * width, (lag + 1) * width)
                stacked[slot * BLOCK : (slot + 1) * BLOCK, cols] = high
                stacked[rows + slot * BLOCK : rows + (slot + 1) * BLOCK, cols] = low
        both = jnp.dot(stacked[...], high_ref[...], preferred_element_type=jnp.float32)
        rest = jnp.dot(stacked[:rows, :], low_ref[...], preferred_element_type=jnp.float32)
        total = both[:rows] + both[rows:] + rest
        for ker in range(ker_count):
            for slot in range(chunk):
                responses[ker, first + slot, history:, :] = total[
                    slot * BLOCK : (slot + 1) * BLOCK, ker * width : (ker + 1) * width
                ]
        return carry

    chunks = slots // chunk
    if chunks == 1:
        one_chunk(0, 0)
    else:
        lax.fori_loop(0, chunks, one_chunk, 0)

    per_kernel = table_ref.shape[1] // ker_count
    for ker in range(ker_count):
        sums[ker][...] = jnp.zeros_like(sums[ker])
    for entry in range(per_kernel):
        for ker in range(ker_count):
            idx = ker * per_kernel + entry
            place = table_ref[0, idx]
            sums[ker][place] = (
                sums[ker][place]
                + responses[ker, table_ref[1, idx], pl.ds(table_ref[2, idx], BLOCK), :]
            )
    half = keep_ref.shape[0]
    for place in range(2 * half):
        total = sums[0][place]
        for ker in range(1, ker_count):
            total = total + sums[ker][place]
        if place < half:
            keep_ref[place] = total
        else:
            send_ref[place - half] = total


def first_stress_kernel(
    wanted_ref, table_ref, params_ref, high_ref, low_ref,
    keep_ref, send_ref, rates_tail_ref, responses_tail_ref,
    window, stacked, responses, *sums,
):
    slots, span, width = window.shape
    history = span - BLOCK
    patch_count = (params_ref.shape[1] - 1) // 3
    times = times_of(0, width)
    for ker in range(responses.shape[0]):
        responses[ker, :, :history, :] = jnp.zeros((slots, history, width), jnp.float32)

    def one_slot(slot):
        patch = wanted_ref[slot]
        drive = (
            params_ref[slot, pl.ds(patch, 1), :]
            + params_ref[slot, pl.ds(2 * patch_count + patch, 1), :] * times
        )
        friction = jnp.broadcast_to(
            params_ref[slot, pl.ds(patch_count + patch, 1), :], drive.shape
        )
        window[slot, :history, :] = jnp.zeros((history, width), jnp.float32)
        window[slot, history:, :] = friction_solve(drive, friction)

    if slots <= 8:
        for slot in range(slots):
            one_slot(slot)
    else:
        pl.loop(0, slots)(one_slot)
    convolve_and_route(
        window, stacked, responses, sums, high_ref, low_ref, table_ref, keep_ref, send_ref
    )
    rates_tail_ref[...] = window[:, BLOCK:, :]
    responses_tail_ref[...] = responses[:, :, BLOCK:, :]


def next_stress_kernel(
    table_ref, rates_ref, rates_tail_ref, responses_tail_ref, high_ref, low_ref,
    keep_ref, send_ref,
    window, stacked, responses, *sums,
):
    history = window.shape[1] - BLOCK
    window[:, :history, :] = rates_tail_ref[...]
    window[:, history:, :] = rates_ref[...]
    responses[:, :, :history, :] = responses_tail_ref[...]
    convolve_and_route(
        window, stacked, responses, sums, high_ref, low_ref, table_ref, keep_ref, send_ref
    )


def solve_patch(block_idx, patch, prestress_ref, friction_ref, load_ref, kept_ref, came_ref):
    width = prestress_ref.shape[1]
    row = pl.ds(patch, 1)
    stress = kept_ref[patch] + came_ref[patch]
    drive = prestress_ref[row, :] + load_ref[row, :] * times_of(block_idx, width) + stress
    return friction_solve(drive, jnp.broadcast_to(friction_ref[row, :], drive.shape))


def middle_block_kernel(
    asked_ref, prestress_ref, friction_ref, load_ref, kept_ref, came_ref, rates_ref, outgoing_ref
):
    for patch in range(prestress_ref.shape[0]):
        rates_ref[patch] = solve_patch(
            1, patch, prestress_ref, friction_ref, load_ref, kept_ref, came_ref
        )

    def one_slot(slot):
        outgoing_ref[slot] = rates_ref[asked_ref[slot]]

    slots = outgoing_ref.shape[0]
    if slots <= 8:
        for slot in range(slots):
            one_slot(slot)
    else:
        pl.loop(0, slots)(one_slot)


def last_block_kernel(
    prestress_ref, friction_ref, load_ref, kept_ref, came_ref, first_ref, second_ref, out_ref
):
    for patch in range(prestress_ref.shape[0]):
        out_ref[patch, :BLOCK, :] = first_ref[patch]
        out_ref[patch, BLOCK : 2 * BLOCK, :] = second_ref[patch]
        out_ref[patch, 2 * BLOCK :, :] = solve_patch(
            2, patch, prestress_ref, friction_ref, load_ref, kept_ref, came_ref
        )


def local(interactions, list_lengths, kernels, prestress, friction, load_rate):
    n_recv = lax.axis_size("recv")
    n_src = lax.axis_size("src")
    recv_idx = lax.axis_index("recv")
    src_idx = lax.axis_index("src")
    ent_count = interactions.shape[1]
    ker_count, width, lag_count, _ = kernels.shape
    patch_count = prestress.shape[0]
    group_rows = n_src * patch_count
    bits = n_src.bit_length() - 1
    assert n_src == 1 << bits and bits > 0

    owners = interactions[1] // group_rows
    local_patch = interactions[1] % patch_count
    slot_ids = jnp.arange(n_recv, dtype=jnp.int32)
    wanted = jnp.max(jnp.where(slot_ids[:, None] == owners[None, :], local_patch[None, :], 0), axis=1)
    params = jnp.concatenate([prestress, friction, load_rate], axis=0)
    outgoing = jnp.concatenate(
        [
            jnp.broadcast_to(params[None], (n_recv,) + params.shape),
            jnp.broadcast_to(wanted.astype(jnp.float32)[:, None, None], (n_recv, 1, width)),
        ],
        axis=1,
    )
    received = lax.all_to_all(outgoing, "recv", split_axis=0, concat_axis=0, tiled=True)
    asked = received[:, -1, 0].astype(jnp.int32)

    receivers = interactions[0] - recv_idx * group_rows
    distance = (receivers // patch_count) ^ src_idx
    place = jnp.zeros_like(distance)
    for bit in range(bits):
        place = place | (((distance >> bit) & 1) << (bits - 1 - bit))
    entry_numbers = jnp.arange(ent_count, dtype=jnp.int32)
    place = jnp.where(
        entry_numbers < list_lengths[0], place * patch_count + receivers % patch_count, group_rows
    )
    table = jnp.stack([place, owners, BLOCK + lag_count - interactions[2]])

    f32, bf16 = jnp.float32, jnp.bfloat16
    taps = lag_count * width
    high, low = pl.pallas_call(
        weights_kernel,
        grid=(ker_count,),
        in_specs=[pl.BlockSpec((1, width, lag_count, width), lambda k: (k, 0, 0, 0))],
        out_specs=[pl.BlockSpec((taps, width), lambda k: (0, k))] * 2,
        out_shape=[jax.ShapeDtypeStruct((taps, ker_count * width), bf16)] * 2,
        name="weights",
    )(kernels)
    first_rates = pl.pallas_call(
        first_block_kernel,
        in_specs=[VMEM] * 3,
        out_specs=VMEM,
        out_shape=jax.ShapeDtypeStruct((patch_count, BLOCK, width), f32),
        name="first_block",
    )(prestress, friction, load_rate)

    half = jax.ShapeDtypeStruct((group_rows // 2, BLOCK, width), f32)
    rates_tail = jax.ShapeDtypeStruct((n_recv, lag_count, width), f32)
    responses_tail = jax.ShapeDtypeStruct((ker_count, n_recv, lag_count, width), f32)
    chunk = min(8, n_recv)
    scratch = [
        pltpu.VMEM((n_recv, lag_count + BLOCK, width), f32),
        pltpu.VMEM((2 * chunk * BLOCK, taps), bf16),
        pltpu.VMEM((ker_count, n_recv, lag_count + BLOCK, width), f32),
    ] + [pltpu.VMEM((group_rows + 1, BLOCK, width), f32)] * ker_count

    def reduce_scatter(kept, sent):
        for bit in range(bits):
            pairs = [(i, i ^ (1 << bit)) for i in range(n_src)]
            came = lax.ppermute(sent, "src", pairs)
            if bit == bits - 1:
                return kept, came
            quarter = kept.shape[0] // 2
            sent = kept[quarter:] + came[quarter:]
            kept = kept[:quarter] + came[:quarter]

    kept, sent, rates_tail, responses_tail = pl.pallas_call(
        first_stress_kernel,
        in_specs=[SMEM, SMEM, VMEM, VMEM, VMEM],
        out_specs=[VMEM] * 4,
        out_shape=[half, half, rates_tail, responses_tail],
        scratch_shapes=scratch,
        name="first_stress",
    )(wanted, table, received, high, low)
    kept, came = reduce_scatter(kept, sent)
    second_rates, outgoing = pl.pallas_call(
        middle_block_kernel,
        in_specs=[SMEM] + [VMEM] * 5,
        out_specs=[VMEM] * 2,
        out_shape=[
            jax.ShapeDtypeStruct((patch_count, BLOCK, width), f32),
            jax.ShapeDtypeStruct((n_recv, BLOCK, width), f32),
        ],
        name="middle_block",
    )(asked, prestress, friction, load_rate, kept, came)
    rates = lax.all_to_all(outgoing, "recv", split_axis=0, concat_axis=0, tiled=True)
    kept, sent = pl.pallas_call(
        next_stress_kernel,
        in_specs=[SMEM] + [VMEM] * 5,
        out_specs=[VMEM] * 2,
        out_shape=[half, half],
        scratch_shapes=scratch,
        name="next_stress",
    )(table, rates, rates_tail, responses_tail, high, low)
    kept, came = reduce_scatter(kept, sent)
    return pl.pallas_call(
        last_block_kernel,
        in_specs=[VMEM] * 7,
        out_specs=VMEM,
        out_shape=jax.ShapeDtypeStruct((patch_count, BLOCKS * BLOCK, width), f32),
        name="last_block",
    )(prestress, friction, load_rate, kept, came, first_rates, second_rates)


def solution(mesh):
    in_specs = (
        P(None, ("recv", "src")),
        P(("recv", "src")),
        P(("recv", "src"), None, None, None),
        P(("recv", "src"), None),
        P(("recv", "src"), None),
        P(("recv", "src"), None),
    )
    out_specs = P(("recv", "src"), None, None)
    return jax.shard_map(local, mesh=mesh, in_specs=in_specs, out_specs=out_specs, check_vma=False)
```

profile of v0, /device:TPU:0, one launch (start us, length us, event | category | flops | bytes accessed | tf_op | source)
XLA Modules:
  0.0 65.3 jit_solution(30449546445197676)
XLA Ops:
  0.7 0.8 %fusion.2 = (s32[96]{0:T(128)S(1)}, s32[1,96]{1,0:T(1,128)S(1)}, s32[1,96]{1,0:T(1,128)S(1)}, s32[1,96]{1,0:T(1,128)S(1)}) fusion(s32[3,96]{1,0:T(4,128)} %param.6, s32[]{:T(128)S(6)} %axis_index.25, s32[]{:T(128)S(6)} %mul.8, s32[]{:T(128)} %bitcast.4), kind=kLoop, calls=%fused_computation.24 | loop fusion | flops 5376 | bytes 2700 | tf_op jit(solution)/shard_map/jit(_where)/broadcast_in_dim | solution.py:216
  1.6 0.7 %pad_maximum_fusion.1 = f32[24,128]{1,0:T(8,128)S(1)} fusion(f32[8,128]{1,0:T(8,128)} %load_ref.5, f32[8,128]{1,0:T(8,128)} %friction_ref.5, f32[8,128]{1,0:T(8,128)} %prestress_ref.5), kind=kLoop, calls=%fused_computation.5 | loop fusion | flops 6144 | bytes 24576 | tf_op jit(solution)/shard_map/concatenate | solution.py:217
  2.4 0.7 %pad_maximum_fusion = f32[8,25,128]{2,1,0:T(8,128)} fusion(f32[8,1,128]{2,1,0:T(1,128)S(1)} %broadcast_in_dim.38, f32[8,24,128]{2,1,0:T(8,128)S(1)} %broadcast_in_dim.34), kind=kLoop, calls=%fused_computation.4 | loop fusion | flops 25600 | bytes 204800 | tf_op jit(solution)/shard_map/concatenate | solution.py:218
  3.1 7.3 %all-to-all-start = ((f32[8,25,128]{2,1,0:T(8,128)}), f32[8,25,128]{2,1,0:T(8,128)S(1)}, u32[]{:S(2)}, u32[]{:S(2)}) async-start(f32[8,25,128]{2,1,0:T(8,128)} %pad_maximum_fusion), calls=%async_computation | async-start | bytes 262144 | tf_op jit(solution)/shard_map/all_to_all | solution.py:225
  10.4 5.9 %weights.1 = (bf16[2048,512]{1,0:T(8,128)(2,1)}, bf16[2048,512]{1,0:T(8,128)(2,1)}) custom-call(f32[4,128,16,128]{3,2,1,0:T(8,128)} %kernel_ref.1), custom_call_target="tpu_custom_call" | custom-call | tf_op jit(solution)/shard_map/weights/pallas_call | solution.py:241
  16.8 0.9 %all-to-all-done.params_ref = f32[8,25,128]{2,1,0:T(8,128)S(1)} async-done(((f32[8,25,128]{2,1,0:T(8,128)}), f32[8,25,128]{2,1,0:T(8,128)S(1)}, u32[]{:S(2)}, u32[]{:S(2)}) %all-to-all-start) | async-done | bytes 102432 | tf_op jit(solution)/shard_map/all_to_all | solution.py:225
  17.7 0.6 copy-done
  18.4 5.6 %first_stress.1 = (f32[16,32,128]{2,1,0:T(8,128)}, f32[16,32,128]{2,1,0:T(8,128)}, f32[8,16,128]{2,1,0:T(8,128)}, f32[4,8,16,128]{3,2,1,0:T(8,128)}) custom-call(s32[8]{0:T(128)} %copy-done.3, s32[3,96]{1,0:T(4,128)} %pad_add_fusion.table_ref, f32[8,25,128]{2,1,0:T(8,128)} %copy-done, bf16[2048,512]{1,0:T(8,128)(2,1)} %get-tuple-element.15.high_ref, ...), custom_call_target="tpu_custom_call" | custom-call | tf_op jit(solution)/shard_map/first_stress/pallas_call | solution.py:277
  24.0 1.7 %collective-permute-done = f32[16,32,128]{2,1,0:T(8,128)S(1)} collective-permute-done((f32[16,32,128]{2,1,0:T(8,128)}, f32[16,32,128]{2,1,0:T(8,128)S(1)}, u32[]{:S(2)}, u32[]{:S(2)}) %collective-permute-start) | collective-permute-done | bytes 262176 | tf_op jit(solution)/shard_map/ppermute | solution.py:270
  25.7 1.7 %slice_add_fusion.2 = (f32[8,32,128]{2,1,0:T(8,128)S(1)}, f32[8,32,128]{2,1,0:T(8,128)}) fusion(f32[16,32,128]{2,1,0:T(8,128)S(1)} %collective-permute-done, f32[16,32,128]{2,1,0:T(8,128)} %get-tuple-element.17), kind=kLoop, calls=%fused_computation.2 | loop fusion | flops 65536 | bytes 786432 | tf_op jit(solution)/shard_map/add | solution.py:274
  27.4 1.5 %collective-permute-start.1 = (f32[8,32,128]{2,1,0:T(8,128)S(1)}, f32[8,32,128]{2,1,0:T(8,128)S(1)}, u32[]{:S(2)}, u32[]{:S(2)}) collective-permute-start(f32[8,32,128]{2,1,0:T(8,128)S(1)} %get-tuple-element.27), channel_id=1, source_target_pairs={{0,2},{1,3},{2,0},{3,1},{4,6},{5,7},{6,4},{7,5},{8,10},{9,11},{10,... | collective-permute-start | bytes 393224 | tf_op jit(solution)/shard_map/ppermute | solution.py:270
  28.9 1.6 %fusion.asked_ref = s32[8]{0:T(128)} fusion(f32[8,25,128]{2,1,0:T(8,128)} %copy-done), kind=kLoop, calls=%fused_computation.7 | loop fusion | flops 8 | bytes 64 | tf_op jit(solution)/shard_map/convert_element_type | solution.py:226
  30.5 2.4 %collective-permute-done.1.came_ref = f32[8,32,128]{2,1,0:T(8,128)S(1)} collective-permute-done((f32[8,32,128]{2,1,0:T(8,128)S(1)}, f32[8,32,128]{2,1,0:T(8,128)S(1)}, u32[]{:S(2)}, u32[]{:S(2)}) %collective-permute-start.1) | collective-permute-done | bytes 131104 | tf_op jit(solution)/shard_map/ppermute | solution.py:270
  32.9 0.7 %copy-done.2 = f32[8,32,128]{2,1,0:T(8,128)} copy-done((f32[8,32,128]{2,1,0:T(8,128)}, f32[8,32,128]{2,1,0:T(8,128)S(1)}, u32[]{:S(2)}) %copy-start.2) | copy-done | bytes 131096
  33.6 2.0 %middle_block.1 = (f32[8,32,128]{2,1,0:T(8,128)}, f32[8,32,128]{2,1,0:T(8,128)}) custom-call(s32[8]{0:T(128)} %fusion.asked_ref, f32[8,128]{1,0:T(8,128)} %prestress_ref.5, f32[8,128]{1,0:T(8,128)} %friction_ref.5, f32[8,128]{1,0:T(8,128)} %load_ref.5, f32[8,32,128]{2,1,0:T(8,128)} %get-tuple-element.28.kept_ref, f32[8,32,128]{2,1,0:T(8,128)} %copy-done.2), custom_call_target="tpu_custom_call" | custom-call | tf_op jit(solution)/shard_map/middle_block/pallas_call | solution.py:286
  35.6 12.6 %all_to_all.10.rates_ref = f32[8,32,128]{2,1,0:T(8,128)} all-to-all(f32[8,32,128]{2,1,0:T(8,128)} %get-tuple-element.19), channel_id=1, replica_groups=mesh['recv'=8,'src'=4] {'recv'}, dimensions={0} | all-to-all | bytes 262144 | tf_op jit(solution)/shard_map/all_to_all | solution.py:296
  48.2 5.3 %next_stress.1 = (f32[16,32,128]{2,1,0:T(8,128)}, f32[16,32,128]{2,1,0:T(8,128)}) custom-call(s32[3,96]{1,0:T(4,128)} %pad_add_fusion.table_ref, f32[8,32,128]{2,1,0:T(8,128)} %all_to_all.10.rates_ref, f32[8,16,128]{2,1,0:T(8,128)} %get-tuple-element.20.rates_tail_ref, f32[4,8,16,128]{3,2,1,0:T(8,128)} %get-tuple-element.21.responses_tail_ref, ...), custom_call_target="tpu_custom_call" | custom-call | tf_op jit(solution)/shard_map/next_stress/pallas_call | solution.py:297
  53.5 1.7 %collective-permute-done.2 = f32[16,32,128]{2,1,0:T(8,128)S(1)} collective-permute-done((f32[16,32,128]{2,1,0:T(8,128)}, f32[16,32,128]{2,1,0:T(8,128)S(1)}, u32[]{:S(2)}, u32[]{:S(2)}) %collective-permute-start.2) | collective-permute-done | bytes 262176 | tf_op jit(solution)/shard_map/ppermute | solution.py:270
  55.3 1.6 %slice_add_fusion = (f32[8,32,128]{2,1,0:T(8,128)S(1)}, f32[8,32,128]{2,1,0:T(8,128)}) fusion(f32[16,32,128]{2,1,0:T(8,128)S(1)} %collective-permute-done.2, f32[16,32,128]{2,1,0:T(8,128)} %get-tuple-element.22), kind=kLoop, calls=%fused_computation | loop fusion | flops 65536 | bytes 786432 | tf_op jit(solution)/shard_map/add | solution.py:274
  56.9 1.5 %collective-permute-start.3 = (f32[8,32,128]{2,1,0:T(8,128)S(1)}, f32[8,32,128]{2,1,0:T(8,128)S(1)}, u32[]{:S(2)}, u32[]{:S(2)}) collective-permute-start(f32[8,32,128]{2,1,0:T(8,128)S(1)} %get-tuple-element.25), channel_id=1, source_target_pairs={{0,2},{1,3},{2,0},{3,1},{4,6},{5,7},{6,4},{7,5},{8,10},{9,11},{10,... | collective-permute-start | bytes 393224 | tf_op jit(solution)/shard_map/ppermute | solution.py:270
  58.4 1.7 %first_block.1.first_ref = f32[8,32,128]{2,1,0:T(8,128)} custom-call(f32[8,128]{1,0:T(8,128)} %prestress_ref.5, f32[8,128]{1,0:T(8,128)} %friction_ref.5, f32[8,128]{1,0:T(8,128)} %load_ref.5), custom_call_target="tpu_custom_call" | custom-call | tf_op jit(solution)/shard_map/first_block/pallas_call | solution.py:249
  60.1 2.3 %collective-permute-done.3.came_ref = f32[8,32,128]{2,1,0:T(8,128)S(1)} collective-permute-done((f32[8,32,128]{2,1,0:T(8,128)S(1)}, f32[8,32,128]{2,1,0:T(8,128)S(1)}, u32[]{:S(2)}, u32[]{:S(2)}) %collective-permute-start.3) | collective-permute-done | bytes 131104 | tf_op jit(solution)/shard_map/ppermute | solution.py:270
  62.4 0.7 copy-done.1
  63.1 2.2 %last_block.1 = f32[8,96,128]{2,1,0:T(8,128)} custom-call(f32[8,128]{1,0:T(8,128)} %prestress_ref.5, f32[8,128]{1,0:T(8,128)} %friction_ref.5, f32[8,128]{1,0:T(8,128)} %load_ref.5, f32[8,32,128]{2,1,0:T(8,128)} %get-tuple-element.26.kept_ref, f32[8,32,128]{2,1,0:T(8,128)} %copy-done.1, f32[8,32,128]{2,1,0:T(8,128)} %first_block.1.first_ref, ...), custom_call_target="tpu_custom_call" | custom-call | tf_op jit(solution)/shard_map/last_block/pallas_call | solution.py:306
  (12 shorter events, 0.8 us)
Async XLA Ops:
  1.6 14.7 %copy-start.3 = (s32[8]{0:T(128)}, s32[8]{0:T(128)S(1)}, u32[]{:S(2)}) copy-start(s32[8]{0:T(128)S(1)} %select_reduce_fusion.wanted_ref) | copy-start | bytes 100
  3.1 14.6 %all-to-all-start = ((f32[8,25,128]{2,1,0:T(8,128)}), f32[8,25,128]{2,1,0:T(8,128)S(1)}, u32[]{:S(2)}, u32[]{:S(2)}) async-start(f32[8,25,128]{2,1,0:T(8,128)} %pad_maximum_fusion), calls=%async_computation | async-start | bytes 262144 | tf_op jit(solution)/shard_map/all_to_all | solution.py:225
  17.7 0.7 copy-start
  24.0 1.7 %collective-permute-start = (f32[16,32,128]{2,1,0:T(8,128)}, f32[16,32,128]{2,1,0:T(8,128)S(1)}, u32[]{:S(2)}, u32[]{:S(2)}) collective-permute-start(f32[16,32,128]{2,1,0:T(8,128)} %get-tuple-element.18), channel_id=1, source_target_pairs={{0,1},{1,0},{2,3},{3,2},{4,5},{5,4},{6,7},{7,6},{8,9},{9,8},{10,11... | collective-permute-start | bytes 786440 | tf_op jit(solution)/shard_map/ppermute | solution.py:270
  27.4 5.5 %collective-permute-start.1 = (f32[8,32,128]{2,1,0:T(8,128)S(1)}, f32[8,32,128]{2,1,0:T(8,128)S(1)}, u32[]{:S(2)}, u32[]{:S(2)}) collective-permute-start(f32[8,32,128]{2,1,0:T(8,128)S(1)} %get-tuple-element.27), channel_id=1, source_target_pairs={{0,2},{1,3},{2,0},{3,1},{4,6},{5,7},{6,4},{7,5},{8,10},{9,11},{10,... | collective-permute-start | bytes 393224 | tf_op jit(solution)/shard_map/ppermute | solution.py:270
  32.9 0.7 %copy-start.2 = (f32[8,32,128]{2,1,0:T(8,128)}, f32[8,32,128]{2,1,0:T(8,128)S(1)}, u32[]{:S(2)}) copy-start(f32[8,32,128]{2,1,0:T(8,128)S(1)} %collective-permute-done.1.came_ref) | copy-start | bytes 393220
  53.5 1.7 %collective-permute-start.2 = (f32[16,32,128]{2,1,0:T(8,128)}, f32[16,32,128]{2,1,0:T(8,128)S(1)}, u32[]{:S(2)}, u32[]{:S(2)}) collective-permute-start(f32[16,32,128]{2,1,0:T(8,128)} %get-tuple-element.23), channel_id=1, source_target_pairs={{0,1},{1,0},{2,3},{3,2},{4,5},{5,4},{6,7},{7,6},{8,9},{9,8},{10,11... | collective-permute-start | bytes 786440 | tf_op jit(solution)/shard_map/ppermute | solution.py:270
  56.9 5.5 %collective-permute-start.3 = (f32[8,32,128]{2,1,0:T(8,128)S(1)}, f32[8,32,128]{2,1,0:T(8,128)S(1)}, u32[]{:S(2)}, u32[]{:S(2)}) collective-permute-start(f32[8,32,128]{2,1,0:T(8,128)S(1)} %get-tuple-element.25), channel_id=1, source_target_pairs={{0,2},{1,3},{2,0},{3,1},{4,6},{5,7},{6,4},{7,5},{8,10},{9,11},{10,... | collective-permute-start | bytes 393224 | tf_op jit(solution)/shard_map/ppermute | solution.py:270
  62.4 0.7 %copy-start.1 = (f32[8,32,128]{2,1,0:T(8,128)}, f32[8,32,128]{2,1,0:T(8,128)S(1)}, u32[]{:S(2)}) copy-start(f32[8,32,128]{2,1,0:T(8,128)S(1)} %collective-permute-done.3.came_ref) | copy-start | bytes 393220
where the time goes:
time: 65.9 us; the launch traced here: 65.3 us
  Pallas kernels  22.7 us (34%)
  blocking collectives  12.6 us (19%)
  starting transfers between devices  10.3 us (16%)
  waiting for transfers between devices  9.11 us (14%)
  other arithmetic  7.81 us (12%)
  local copies, waits for them, and re-layouts  2.04 us (3%)
  between operations  0.69 us (1%)
    all_to_all x1, blocking collectives, local(): lax.all_to_all(outgoing, 'recv', split_axis=0, concat_axis=0, tiled=True)  12.6 us
    ppermute x4, waiting for transfers between devices, reduce_scatter(): came = lax.ppermute(sent, 'src', pairs)  8.25 us
    all_to_all x1, starting transfers between devices, local(): lax.all_to_all(outgoing, 'recv', split_axis=0, concat_axis=0, tiled=True)  7.28 us
    pallas_call x1, Pallas kernels, local(): pl.pallas_call(weights_kernel, grid=(ker_count,), in_specs=[pl.BlockSpec(...  5.9 us
    pallas_call x1, Pallas kernels, local(): pl.pallas_call(first_stress_kernel, in_specs=[SMEM, SMEM, VMEM, VMEM, VME...  5.64 us
    pallas_call x1, Pallas kernels, local(): pl.pallas_call(next_stress_kernel, in_specs=[SMEM] + [VMEM] * 5, out_spec...  5.28 us
    add x2, other arithmetic, reduce_scatter(): sent = kept[quarter:] + came[quarter:]  3.31 us
    ppermute x4, starting transfers between devices, reduce_scatter(): came = lax.ppermute(sent, 'src', pairs)  3.04 us
  transfers between devices with their start and end apart: 5, of which 5 were waited for; matrix products, arithmetic and copies ran while one was open for 3% of the time, Pallas kernels for 12%

commit v1 on v0

v1 whole, which is shorter than its diff:
```python
import functools

import jax
import jax.numpy as jnp
from jax import lax
from jax.experimental import pallas as pl
from jax.experimental.pallas import tpu as pltpu
from jax.sharding import PartitionSpec as P

BLOCK = 32
BLOCKS = 3
NEWTON = 4
damping = 0.5
def grant(mib):
    return pltpu.CompilerParams(vmem_limit_bytes=mib * 2**20)


VMEM = pl.BlockSpec(memory_space=pltpu.VMEM)
SMEM = pl.BlockSpec(memory_space=pltpu.SMEM)
HBM = pl.BlockSpec(memory_space=pltpu.HBM)


def friction_solve(drive, friction):
    rates = drive / (damping + friction)
    for newton_step in range(NEWTON - 1):
        squares = 1.0 + rates * rates
        inverse_root = lax.rsqrt(squares)
        magnitude = jnp.log(jnp.abs(rates) + squares * inverse_root)
        inverse_sinh = jnp.where(rates < 0, -magnitude, magnitude)
        misfit = damping * rates + friction * inverse_sinh - drive
        rates = rates - misfit / (damping + friction * inverse_root)
    return rates


def times_of(block_idx, width):
    steps = lax.broadcasted_iota(jnp.int32, (BLOCK, width), 0)
    return (steps + (block_idx * BLOCK + 1)).astype(jnp.float32)


def split(values):
    high = values.astype(jnp.bfloat16)
    return high, (values - high.astype(jnp.float32)).astype(jnp.bfloat16)


def wanted_patches(interactions_ref, slots, patch_count):
    sources = interactions_ref[pl.ds(1, 1), :]
    owners = lax.broadcasted_iota(jnp.int32, (slots, sources.shape[1]), 0)
    first = (owners * lax.axis_size("src") + lax.axis_index("src")) * patch_count
    offset = sources - first
    inside = (offset >= 0) & (offset < patch_count)
    wanted = jnp.max(jnp.where(inside, offset, 0).astype(jnp.float32), axis=1, keepdims=True)
    return owners, inside, wanted


def pack_kernel(interactions_ref, prestress_ref, friction_ref, load_ref, out_ref):
    slots, rows, width = out_ref.shape
    patch_count = prestress_ref.shape[0]
    wanted = wanted_patches(interactions_ref, slots, patch_count)[2]
    wanted = jnp.broadcast_to(wanted, (slots, width))
    for field, ref in enumerate((prestress_ref, friction_ref, load_ref)):
        out_ref[:, field * patch_count : (field + 1) * patch_count, :] = jnp.broadcast_to(
            ref[...][None], (slots, patch_count, width)
        )
    for slot in range(slots):
        out_ref[slot, rows - 1 :, :] = wanted[slot : slot + 1, :]


def split_lag(lag, raw, first, halves):
    ker_count, width = raw.shape[0], raw.shape[3]
    rows = slice(lag * width, (lag + 1) * width)
    for ker in range(ker_count):
        split_tile(raw[ker, :, first + lag, :], ker, rows, halves)


def split_tile(tile, ker, rows, halves):
    halves[ker, rows, :], halves[halves.shape[0] // 2 + ker, rows, :] = split(tile.T)


def prepare_kernel(
    patch_count, lengths_ref, interactions_ref, kernel_ref, halves, table_ref, wanted_ref,
    interactions, raw, list_sem, sems,
):
    ker_count, _, lag_count, width = raw.shape
    early = halves.shape[1] // width
    loads = [
        pltpu.make_async_copy(kernel_ref.at[ker], raw.at[ker], sems.at[ker])
        for ker in range(ker_count)
    ]
    list_load = pltpu.make_async_copy(interactions_ref, interactions, list_sem)
    list_load.start()
    for copy in loads:
        copy.start()
    list_load.wait()

    slots = wanted_ref.shape[0]
    owners, inside, wanted = wanted_patches(interactions, slots, patch_count)
    wanted_ref[...] = jnp.broadcast_to(wanted, wanted_ref.shape)
    n_src = lax.axis_size("src")
    group_rows = n_src * patch_count
    receivers = interactions[pl.ds(0, 1), :] - lax.axis_index("recv") * group_rows
    strips = jnp.zeros_like(receivers)
    for other in range(1, n_src):
        strips = strips + (receivers >= other * patch_count).astype(jnp.int32)
    distance = strips ^ lax.axis_index("src")
    bits = n_src.bit_length() - 1
    order = jnp.zeros_like(distance)
    for bit in range(bits):
        order = order | (((distance >> bit) & 1) << (bits - 1 - bit))
    place = order * patch_count + receivers - strips * patch_count
    live = lax.broadcasted_iota(jnp.int32, place.shape, 1) < lengths_ref[0]
    table_ref[pl.ds(0, 1), :] = jnp.where(live, place, group_rows)
    table_ref[pl.ds(1, 1), :] = jnp.max(
        jnp.where(inside, owners, 0).astype(jnp.float32), axis=0, keepdims=True
    ).astype(jnp.int32)
    table_ref[pl.ds(2, 1), :] = BLOCK + lag_count - interactions[pl.ds(2, 1), :]

    for ker in range(ker_count):
        loads[ker].wait()
        for lag in range(early):
            split_tile(
                raw[ker, :, lag, :], ker, slice(lag * width, (lag + 1) * width), halves
            )


def first_block_kernel(prestress_ref, friction_ref, load_ref, out_ref):
    patch_count, width = prestress_ref.shape
    times = times_of(0, width)
    for patch in range(patch_count):
        row = pl.ds(patch, 1)
        drive = prestress_ref[row, :] + load_ref[row, :] * times
        out_ref[patch] = friction_solve(drive, jnp.broadcast_to(friction_ref[row, :], drive.shape))


def product(left, halves, parts):
    right = jnp.concatenate([halves[part] for part in parts], axis=1)
    return jnp.dot(left, right, preferred_element_type=jnp.float32)


def convolve_and_route(
    window, stacked, responses, sums, early, late, table_ref, keep_ref, send_ref, late_ready=None
):
    slots, span, width = window.shape
    history = span - BLOCK
    ker_count = responses.shape[0]
    early_lags, late_lags = early.shape[1] // width, late.shape[1] // width
    chunk = stacked.shape[0] // (2 * BLOCK)
    rows = chunk * BLOCK
    chunks = slots // chunk
    if late_ready is not None and chunks > 1:
        late_ready()

    def one_chunk(chunk_idx, carry):
        first = chunk_idx * chunk

        def part(halves, lags):
            for lag in lags:
                cols = slice(lag * width, (lag + 1) * width)
                for slot in range(chunk):
                    upper, lower = split(
                        window[first + slot, history - lag : history - lag + BLOCK, :]
                    )
                    stacked[slot * BLOCK : (slot + 1) * BLOCK, cols] = upper
                    stacked[rows + slot * BLOCK : rows + (slot + 1) * BLOCK, cols] = lower
            taps = slice(lags[0] * width, (lags[-1] + 1) * width)
            both = product(stacked[:, taps], halves, range(ker_count))
            rest = product(stacked[:rows, taps], halves, range(ker_count, 2 * ker_count))
            return both[:rows] + both[rows:] + rest

        total = part(early, range(early_lags))
        if late_ready is not None and chunks == 1:
            late_ready()
        total = total + part(late, range(early_lags, early_lags + late_lags))
        for ker in range(ker_count):
            for slot in range(chunk):
                responses[ker, first + slot, history:, :] = total[
                    slot * BLOCK : (slot + 1) * BLOCK, ker * width : (ker + 1) * width
                ]
        return carry

    if chunks == 1:
        one_chunk(0, 0)
    else:
        lax.fori_loop(0, chunks, one_chunk, 0)

    per_kernel = table_ref.shape[1] // ker_count
    for ker in range(ker_count):
        sums[ker][...] = jnp.zeros_like(sums[ker])
    for entry in range(per_kernel):
        for ker in range(ker_count):
            idx = ker * per_kernel + entry
            place = table_ref[0, idx]
            sums[ker][place] = (
                sums[ker][place]
                + responses[ker, table_ref[1, idx], pl.ds(table_ref[2, idx], BLOCK), :]
            )
    half = keep_ref.shape[0]
    for place in range(2 * half):
        total = sums[0][place]
        for ker in range(1, ker_count):
            total = total + sums[ker][place]
        if place < half:
            keep_ref[place] = total
        else:
            send_ref[place - half] = total


def first_stress_kernel(
    table_ref, wanted_ref, params_ref, early, kernel_ref,
    keep_ref, send_ref, rates_tail_ref, responses_tail_ref, late,
    window, stacked, responses, raw, sem, *sums,
):
    slots, span, width = window.shape
    loaded = raw.shape[2]
    lag_count = kernel_ref.shape[2]
    load = pltpu.make_async_copy(
        kernel_ref.at[:, :, lag_count - loaded :, :], raw, sem
    )
    load.start()

    def late_ready():
        load.wait()
        late_lags = late.shape[1] // width
        for lag in range(late_lags):
            split_lag(lag, raw, loaded - late_lags, late)

    history = span - BLOCK
    patch_count = (params_ref.shape[1] - 1) // 3
    times = times_of(0, width)
    for ker in range(responses.shape[0]):
        responses[ker, :, :history, :] = jnp.zeros((slots, history, width), jnp.float32)

    patches = lax.broadcasted_iota(jnp.int32, (patch_count, width), 0).astype(jnp.float32)

    def one_slot(slot):
        chosen = patches == wanted_ref[pl.ds(slot, 1), :]

        def field(number):
            rows = params_ref[slot, number * patch_count : (number + 1) * patch_count, :]
            return jnp.sum(jnp.where(chosen, rows, 0.0), axis=0, keepdims=True)

        drive = field(0) + field(2) * times
        friction = jnp.broadcast_to(field(1), drive.shape)
        window[slot, :history, :] = jnp.zeros((history, width), jnp.float32)
        window[slot, history:, :] = friction_solve(drive, friction)

    if slots <= 8:
        for slot in range(slots):
            one_slot(slot)
    else:
        pl.loop(0, slots)(one_slot)
    convolve_and_route(
        window, stacked, responses, sums, early, late, table_ref, keep_ref, send_ref, late_ready
    )
    rates_tail_ref[...] = window[:, BLOCK:, :]
    responses_tail_ref[...] = responses[:, :, BLOCK:, :]


def next_stress_kernel(
    table_ref, rates_ref, rates_tail_ref, responses_tail_ref, early, late,
    keep_ref, send_ref,
    window, stacked, responses, *sums,
):
    history = window.shape[1] - BLOCK
    window[:, :history, :] = rates_tail_ref[...]
    window[:, history:, :] = rates_ref[...]
    responses[:, :, :history, :] = responses_tail_ref[...]
    convolve_and_route(
        window, stacked, responses, sums, early, late, table_ref, keep_ref, send_ref
    )


def solve_patch(block_idx, patch, prestress_ref, friction_ref, load_ref, kept_ref, came_ref):
    width = prestress_ref.shape[1]
    row = pl.ds(patch, 1)
    stress = kept_ref[patch] + came_ref[patch]
    drive = prestress_ref[row, :] + load_ref[row, :] * times_of(block_idx, width) + stress
    return friction_solve(drive, jnp.broadcast_to(friction_ref[row, :], drive.shape))


def middle_block_kernel(
    asked_ref, prestress_ref, friction_ref, load_ref, kept_ref, came_ref, rates_ref, outgoing_ref
):
    for patch in range(prestress_ref.shape[0]):
        rates_ref[patch] = solve_patch(
            1, patch, prestress_ref, friction_ref, load_ref, kept_ref, came_ref
        )

    def one_slot(slot):
        outgoing_ref[slot] = rates_ref[asked_ref[slot]]

    slots = outgoing_ref.shape[0]
    if slots <= 8:
        for slot in range(slots):
            one_slot(slot)
    else:
        pl.loop(0, slots)(one_slot)


def last_block_kernel(
    prestress_ref, friction_ref, load_ref, kept_ref, came_ref, first_ref, second_ref, out_ref
):
    for patch in range(prestress_ref.shape[0]):
        out_ref[patch, :BLOCK, :] = first_ref[patch]
        out_ref[patch, BLOCK : 2 * BLOCK, :] = second_ref[patch]
        out_ref[patch, 2 * BLOCK :, :] = solve_patch(
            2, patch, prestress_ref, friction_ref, load_ref, kept_ref, came_ref
        )


def local(interactions, list_lengths, kernels, prestress, friction, load_rate):
    n_recv = lax.axis_size("recv")
    n_src = lax.axis_size("src")
    ker_count, width, lag_count, _ = kernels.shape
    patch_count = prestress.shape[0]
    group_rows = n_src * patch_count
    bits = n_src.bit_length() - 1
    assert n_src == 1 << bits and bits > 0

    f32, bf16 = jnp.float32, jnp.bfloat16
    packed = pl.pallas_call(
        pack_kernel,
        in_specs=[VMEM] * 4,
        out_specs=VMEM,
        out_shape=jax.ShapeDtypeStruct((n_recv, 3 * patch_count + 1, width), f32),
        name="pack",
    )(interactions, prestress, friction, load_rate)
    received = lax.all_to_all(packed, "recv", split_axis=0, concat_axis=0, tiled=True)
    asked = received[:, -1, 0].astype(jnp.int32)

    late_lags = lag_count // 4
    early = jax.ShapeDtypeStruct((2 * ker_count, (lag_count - late_lags) * width, width), bf16)
    late = jax.ShapeDtypeStruct((2 * ker_count, late_lags * width, width), bf16)
    kernels = pltpu.with_memory_space_constraint(kernels, pltpu.HBM)
    early, table, wanted = pl.pallas_call(
        functools.partial(prepare_kernel, patch_count),
        in_specs=[SMEM, HBM, HBM],
        out_specs=[VMEM] * 3,
        out_shape=[
            early,
            jax.ShapeDtypeStruct(interactions.shape, jnp.int32),
            jax.ShapeDtypeStruct((n_recv, width), f32),
        ],
        scratch_shapes=[
            pltpu.VMEM(interactions.shape, jnp.int32),
            pltpu.VMEM(kernels.shape, f32),
            pltpu.SemaphoreType.DMA,
            pltpu.SemaphoreType.DMA((ker_count,)),
        ],
        compiler_params=grant(12),
        name="prepare",
    )(list_lengths, pltpu.with_memory_space_constraint(interactions, pltpu.HBM), kernels)
    first_rates = pl.pallas_call(
        first_block_kernel,
        in_specs=[VMEM] * 3,
        out_specs=VMEM,
        out_shape=jax.ShapeDtypeStruct((patch_count, BLOCK, width), f32),
        compiler_params=grant(2),
        name="first_block",
    )(prestress, friction, load_rate)

    half = jax.ShapeDtypeStruct((group_rows // 2, BLOCK, width), f32)
    rates_tail = jax.ShapeDtypeStruct((n_recv, lag_count, width), f32)
    responses_tail = jax.ShapeDtypeStruct((ker_count, n_recv, lag_count, width), f32)
    chunk = min(8, n_recv)
    stress_mib = 16 + 8 * ker_count * n_recv * (lag_count + BLOCK) * width // 2**20
    scratch = [
        pltpu.VMEM((n_recv, lag_count + BLOCK, width), f32),
        pltpu.VMEM((2 * chunk * BLOCK, lag_count * width), bf16),
        pltpu.VMEM((ker_count, n_recv, lag_count + BLOCK, width), f32),
    ] + [pltpu.VMEM((group_rows + 1, BLOCK, width), f32)] * ker_count

    def reduce_scatter(kept, sent):
        for bit in range(bits):
            pairs = [(i, i ^ (1 << bit)) for i in range(n_src)]
            came = lax.ppermute(sent, "src", pairs)
            if bit == bits - 1:
                return kept, came
            quarter = kept.shape[0] // 2
            sent = kept[quarter:] + came[quarter:]
            kept = kept[:quarter] + came[:quarter]

    loaded = min(lag_count, -(-late_lags // 8) * 8)
    kept, sent, rates_tail, responses_tail, late = pl.pallas_call(
        first_stress_kernel,
        in_specs=[SMEM] + [VMEM] * 3 + [HBM],
        out_specs=[VMEM] * 5,
        out_shape=[half, half, rates_tail, responses_tail, late],
        scratch_shapes=scratch[:3]
        + [pltpu.VMEM((ker_count, width, loaded, width), f32), pltpu.SemaphoreType.DMA]
        + scratch[3:],
        compiler_params=grant(stress_mib),
        name="first_stress",
    )(table, wanted, received, early, kernels)
    kept, came = reduce_scatter(kept, sent)
    second_rates, outgoing = pl.pallas_call(
        middle_block_kernel,
        in_specs=[SMEM] + [VMEM] * 5,
        out_specs=[VMEM] * 2,
        out_shape=[
            jax.ShapeDtypeStruct((patch_count, BLOCK, width), f32),
            jax.ShapeDtypeStruct((n_recv, BLOCK, width), f32),
        ],
        compiler_params=grant(4),
        name="middle_block",
    )(asked, prestress, friction, load_rate, kept, came)
    rates = lax.all_to_all(outgoing, "recv", split_axis=0, concat_axis=0, tiled=True)
    kept, sent = pl.pallas_call(
        next_stress_kernel,
        in_specs=[SMEM] + [VMEM] * 5,
        out_specs=[VMEM] * 2,
        out_shape=[half, half],
        scratch_shapes=scratch,
        compiler_params=grant(stress_mib),
        name="next_stress",
    )(table, rates, rates_tail, responses_tail, early, late)
    kept, came = reduce_scatter(kept, sent)
    return pl.pallas_call(
        last_block_kernel,
        in_specs=[VMEM] * 7,
        out_specs=VMEM,
        out_shape=jax.ShapeDtypeStruct((patch_count, BLOCKS * BLOCK, width), f32),
        compiler_params=grant(4),
        name="last_block",
    )(prestress, friction, load_rate, kept, came, first_rates, second_rates)


def solution(mesh):
    in_specs = (
        P(None, ("recv", "src")),
        P(("recv", "src")),
        P(("recv", "src"), None, None, None),
        P(("recv", "src"), None),
        P(("recv", "src"), None),
        P(("recv", "src"), None),
    )
    out_specs = P(("recv", "src"), None, None)
    return jax.shard_map(local, mesh=mesh, in_specs=in_specs, out_specs=out_specs, check_vma=False)
```

time: 65.9 us -> 49.8 us (0.76)
  Pallas kernels: 22.7 us -> 14.1 us
  other arithmetic: 7.81 us -> 0.32 us
  waiting for transfers between devices: 9.11 us -> 13.5 us
  blocking collectives: 12.6 us -> 10.2 us
  local copies, waits for them, and re-layouts: 2.04 us -> 0.02 us
    add x2, other arithmetic: 3.31 us -> 0.08 us  [reduce_scatter(): sent = kept[quarter:] + came[quarter:]]
    pallas_call x1, Pallas kernels: 5.28 us -> 2.75 us  [local(): pl.pallas_call(next_stress_kernel, in_specs=[SMEM] + [VMEM] * 5, out_spec...]
    pallas_call x2 -> x3, Pallas kernels: 11.5 us -> 9.1 us  [the longest x1 3.89 us: local(): pl.pallas_call(first_stress_kernel, in_specs=[SMEM] + [VMEM] * 3 + [HBM],...]
    all_to_all x1, blocking collectives: 12.6 us -> 10.2 us  [local(): lax.all_to_all(outgoing, 'recv', split_axis=0, concat_axis=0, tiled=True)]
    ppermute x4, waiting for transfers between devices: 8.25 us -> 10.5 us  [reduce_scatter(): came = lax.ppermute(sent, 'src', pairs)]
    all_to_all x1, waiting for transfers between devices: 0.86 us -> 2.92 us  [local(): lax.all_to_all(packed, 'recv', split_axis=0, concat_axis=0, tiled=True)]
    unnamed x8 -> x6, local copies, waits for them, and re-layouts: 1.96 us -> 0.02 us
    concatenate x2 -> x0, other arithmetic: 1.39 us -> none  [the longest x1 0.72 us: local(): params = jnp.concatenate([prestress, friction, load_rate], axis=0)]
  transfers between devices with their start and end apart: 5 -> 5, of which waited for: 5 -> 5; matrix products, arithmetic and copies ran while one was open for 3% -> 0% of each run, Pallas kernels for 12% -> 8%
where the time goes in v1:
time: 49.8 us; the launch traced here: 49.4 us
  Pallas kernels  14.1 us (28%)
  waiting for transfers between devices  13.5 us (27%)
  starting transfers between devices  10.6 us (21%)
  blocking collectives  10.2 us (20%)
  between operations  0.74 us (1%)
    ppermute x4, waiting for transfers between devices, reduce_scatter(): came = lax.ppermute(sent, 'src', pairs)  10.5 us
    all_to_all x1, blocking collectives, local(): lax.all_to_all(outgoing, 'recv', split_axis=0, concat_axis=0, tiled=True)  10.2 us
    all_to_all x1, starting transfers between devices, local(): lax.all_to_all(packed, 'recv', split_axis=0, concat_axis=0, tiled=True)  7.28 us
    pallas_call x1, Pallas kernels, local(): pl.pallas_call(first_stress_kernel, in_specs=[SMEM] + [VMEM] * 3 + [HBM],...  3.89 us
    pallas_call x1, Pallas kernels, local(): pl.pallas_call(functools.partial(prepare_kernel, patch_count), in_specs=[...  3.73 us
    ppermute x4, starting transfers between devices, reduce_scatter(): came = lax.ppermute(sent, 'src', pairs)  3.3 us
    all_to_all x1, waiting for transfers between devices, local(): lax.all_to_all(packed, 'recv', split_axis=0, concat_axis=0, tiled=True)  2.92 us
    pallas_call x1, Pallas kernels, local(): pl.pallas_call(next_stress_kernel, in_specs=[SMEM] + [VMEM] * 5, out_spec...  2.75 us
  transfers between devices with their start and end apart: 5, of which 5 were waited for; matrix products, arithmetic and copies ran while one was open for 0% of the time, Pallas kernels for 8%

profile of v1, /device:TPU:0, one launch (start us, length us, event | category | flops | bytes accessed | tf_op | source)
XLA Modules:
  0.0 49.4 jit_solution(2282671483260985168)
XLA Ops:
  0.0 1.5 %pack.1 = f32[8,25,128]{2,1,0:T(8,128)} custom-call(s32[3,96]{1,0:T(4,128)} %interactions_ref.3, f32[8,128]{1,0:T(8,128)} %prestress_ref.7, f32[8,128]{1,0:T(8,128)} %friction_ref.7, f32[8,128]{1,0:T(8,128)} %load_ref.7), custom_call_target="tpu_custom_call" | custom-call | tf_op jit(solution)/shard_map/pack/pallas_call | solution.py:320
  1.5 7.3 %all-to-all-start = ((f32[8,25,128]{2,1,0:T(8,128)}), f32[8,25,128]{2,1,0:T(8,128)S(1)}, u32[]{:S(2)}, u32[]{:S(2)}) async-start(f32[8,25,128]{2,1,0:T(8,128)} %pack.1), calls=%async_computation | async-start | bytes 262144 | tf_op jit(solution)/shard_map/all_to_all | solution.py:327
  9.4 3.7 %prepare.1 = (bf16[8,1536,128]{2,1,0:T(8,128)(2,1)S(1)}, s32[3,96]{1,0:T(4,128)S(1)}, f32[8,128]{1,0:T(8,128)S(1)}) custom-call(s32[1]{0:T(128)S(6)} %copy.7.lengths_ref, s32[3,96]{1,0:T(4,128)} %interactions_ref.3, f32[4,128,16,128]{3,2,1,0:T(8,128)} %kernel_ref.3), custom_call_target="tpu_custom_call" | custom-call | tf_op jit(solution)/shard_map/prepare/pallas_call | solution.py:334
  13.2 0.0 copy-start
  13.2 0.0 copy-start.1
  13.2 0.0 copy-start.2
  13.2 2.9 %all-to-all-done.params_ref = f32[8,25,128]{2,1,0:T(8,128)S(1)} async-done(((f32[8,25,128]{2,1,0:T(8,128)}), f32[8,25,128]{2,1,0:T(8,128)S(1)}, u32[]{:S(2)}, u32[]{:S(2)}) %all-to-all-start) | async-done | bytes 102432 | tf_op jit(solution)/shard_map/all_to_all | solution.py:327
  16.1 3.9 %first_stress.1 = (f32[16,32,128]{2,1,0:T(8,128)S(1)}, f32[16,32,128]{2,1,0:T(8,128)S(1)}, f32[8,16,128]{2,1,0:T(8,128)S(1)}, f32[4,8,16,128]{3,2,1,0:T(8,128)S(1)}, bf16[8,512,128]{2,1,0:T(8,128)(2,1)S(1)}) custom-call(s32[3,96]{1,0:T(4,128)S(1)} %get-tuple-element.17.table_ref, f32[8,128]{1,0:T(8,128)S(1)} %get-tuple-element.18.wanted_ref, ...), custom_call_target="tpu_custom_call" | custom-call | tf_op jit(solution)/shard_map/first_stress/pallas_call | solution.py:383
  20.0 0.1 collective-permute-start
  20.1 1.5 %collective-permute-done = f32[16,32,128]{2,1,0:T(8,128)S(1)} collective-permute-done((f32[16,32,128]{2,1,0:T(8,128)S(1)}, f32[16,32,128]{2,1,0:T(8,128)S(1)}, u32[]{:S(2)}, u32[]{:S(2)}) %collective-permute-start) | collective-permute-done | bytes 262176 | tf_op jit(solution)/shard_map/ppermute | solution.py:375
  21.6 1.6 %collective-permute-start.1 = (f32[8,32,128]{2,1,0:T(8,128)S(1)}, f32[8,32,128]{2,1,0:T(8,128)S(1)}, u32[]{:S(2)}, u32[]{:S(2)}) collective-permute-start(f32[8,32,128]{2,1,0:T(8,128)S(1)} %get-tuple-element.31), channel_id=1, source_target_pairs={{0,2},{1,3},{2,0},{3,1},{4,6},{5,7},{6,4},{7,5},{8,10},{9,11},{10,... | collective-permute-start | bytes 393224 | tf_op jit(solution)/shard_map/ppermute | solution.py:375
  23.2 0.2 fusion.asked_ref
  23.5 3.8 %collective-permute-done.1.came_ref = f32[8,32,128]{2,1,0:T(8,128)S(1)} collective-permute-done((f32[8,32,128]{2,1,0:T(8,128)S(1)}, f32[8,32,128]{2,1,0:T(8,128)S(1)}, u32[]{:S(2)}, u32[]{:S(2)}) %collective-permute-start.1) | collective-permute-done | bytes 131104 | tf_op jit(solution)/shard_map/ppermute | solution.py:375
  27.3 0.0 copy-done
  27.3 0.0 copy-done.1
  27.3 0.9 %middle_block.1 = (f32[8,32,128]{2,1,0:T(8,128)S(1)}, f32[8,32,128]{2,1,0:T(8,128)S(1)}) custom-call(s32[8]{0:T(128)S(1)} %fusion.asked_ref, f32[8,128]{1,0:T(8,128)S(1)} %copy-done, f32[8,128]{1,0:T(8,128)S(1)} %copy-done.1, f32[8,128]{1,0:T(8,128)S(1)} %copy-done.2, f32[8,32,128]{2,1,0:T(8,128)S(1)} %get-tuple-element.32.kept_ref, ...), custom_call_target="tpu_custom_call" | custom-call | tf_op jit(solution)/shard_map/middle_block/pallas_call | solution.py:395
  28.1 10.2 %all_to_all.10.rates_ref = f32[8,32,128]{2,1,0:T(8,128)S(1)} all-to-all(f32[8,32,128]{2,1,0:T(8,128)S(1)} %get-tuple-element.22), channel_id=1, replica_groups=mesh['recv'=8,'src'=4] {'recv'}, dimensions={0} | all-to-all | bytes 262144 | tf_op jit(solution)/shard_map/all_to_all | solution.py:406
  38.4 2.8 %next_stress.1 = (f32[16,32,128]{2,1,0:T(8,128)S(1)}, f32[16,32,128]{2,1,0:T(8,128)S(1)}) custom-call(s32[3,96]{1,0:T(4,128)S(1)} %get-tuple-element.17.table_ref, f32[8,32,128]{2,1,0:T(8,128)S(1)} %all_to_all.10.rates_ref, f32[8,16,128]{2,1,0:T(8,128)S(1)} %get-tuple-element.23.rates_tail_ref, f32[4,8,16,128]{3,2,1,0:T(8,128)S(1)} %get-tuple-element.24.responses_tail_ref, ...), custom_call_target="tpu_custom_call" | custom-call | tf_op jit(solution)/shard_map/next_stress/pallas_call | solution.py:407
  41.1 0.1 collective-permute-start.2
  41.2 1.5 %collective-permute-done.2 = f32[16,32,128]{2,1,0:T(8,128)S(1)} collective-permute-done((f32[16,32,128]{2,1,0:T(8,128)S(1)}, f32[16,32,128]{2,1,0:T(8,128)S(1)}, u32[]{:S(2)}, u32[]{:S(2)}) %collective-permute-start.2) | collective-permute-done | bytes 262176 | tf_op jit(solution)/shard_map/ppermute | solution.py:375
  42.8 1.6 %collective-permute-start.3 = (f32[8,32,128]{2,1,0:T(8,128)S(1)}, f32[8,32,128]{2,1,0:T(8,128)S(1)}, u32[]{:S(2)}, u32[]{:S(2)}) collective-permute-start(f32[8,32,128]{2,1,0:T(8,128)S(1)} %get-tuple-element.29), channel_id=1, source_target_pairs={{0,2},{1,3},{2,0},{3,1},{4,6},{5,7},{6,4},{7,5},{8,10},{9,11},{10,... | collective-permute-start | bytes 393224 | tf_op jit(solution)/shard_map/ppermute | solution.py:375
  44.3 0.3 first_block.1.first_ref
  44.7 3.7 %collective-permute-done.3.came_ref = f32[8,32,128]{2,1,0:T(8,128)S(1)} collective-permute-done((f32[8,32,128]{2,1,0:T(8,128)S(1)}, f32[8,32,128]{2,1,0:T(8,128)S(1)}, u32[]{:S(2)}, u32[]{:S(2)}) %collective-permute-start.3) | collective-permute-done | bytes 131104 | tf_op jit(solution)/shard_map/ppermute | solution.py:375
  48.4 1.1 %last_block.1 = f32[8,96,128]{2,1,0:T(8,128)} custom-call(f32[8,128]{1,0:T(8,128)S(1)} %copy-done, f32[8,128]{1,0:T(8,128)S(1)} %copy-done.1, f32[8,128]{1,0:T(8,128)S(1)} %copy-done.2, f32[8,32,128]{2,1,0:T(8,128)S(1)} %get-tuple-element.30.kept_ref, f32[8,32,128]{2,1,0:T(8,128)S(1)} %collective-permute-done.3.came_ref, ...), custom_call_target="tpu_custom_call" | custom-call | tf_op jit(solution)/shard_map/last_block/pallas_call | solution.py:417
  (3 shorter events, 0.1 us)
Async XLA Ops:
  1.5 14.6 %all-to-all-start = ((f32[8,25,128]{2,1,0:T(8,128)}), f32[8,25,128]{2,1,0:T(8,128)S(1)}, u32[]{:S(2)}, u32[]{:S(2)}) async-start(f32[8,25,128]{2,1,0:T(8,128)} %pack.1), calls=%async_computation | async-start | bytes 262144 | tf_op jit(solution)/shard_map/all_to_all | solution.py:327
  13.2 14.1 %copy-start = (f32[8,128]{1,0:T(8,128)S(1)}, f32[8,128]{1,0:T(8,128)}, u32[]{:S(2)}) copy-start(f32[8,128]{1,0:T(8,128)} %prestress_ref.7) | copy-start | bytes 12292
  13.2 14.1 %copy-start.1 = (f32[8,128]{1,0:T(8,128)S(1)}, f32[8,128]{1,0:T(8,128)}, u32[]{:S(2)}) copy-start(f32[8,128]{1,0:T(8,128)} %friction_ref.7) | copy-start | bytes 12292
  13.2 14.1 %copy-start.2 = (f32[8,128]{1,0:T(8,128)S(1)}, f32[8,128]{1,0:T(8,128)}, u32[]{:S(2)}) copy-start(f32[8,128]{1,0:T(8,128)} %load_ref.7) | copy-start | bytes 12292
  20.0 1.6 %collective-permute-start = (f32[16,32,128]{2,1,0:T(8,128)S(1)}, f32[16,32,128]{2,1,0:T(8,128)S(1)}, u32[]{:S(2)}, u32[]{:S(2)}) collective-permute-start(f32[16,32,128]{2,1,0:T(8,128)S(1)} %get-tuple-element.21), channel_id=1, source_target_pairs={{0,1},{1,0},{2,3},{3,2},{4,5},{5,4},{6,7},{7,6},{8,9},{9,8},{10,11... | collective-permute-start | bytes 786440 | tf_op jit(solution)/shard_map/ppermute | solution.py:375
  21.6 5.6 %collective-permute-start.1 = (f32[8,32,128]{2,1,0:T(8,128)S(1)}, f32[8,32,128]{2,1,0:T(8,128)S(1)}, u32[]{:S(2)}, u32[]{:S(2)}) collective-permute-start(f32[8,32,128]{2,1,0:T(8,128)S(1)} %get-tuple-element.31), channel_id=1, source_target_pairs={{0,2},{1,3},{2,0},{3,1},{4,6},{5,7},{6,4},{7,5},{8,10},{9,11},{10,... | collective-permute-start | bytes 393224 | tf_op jit(solution)/shard_map/ppermute | solution.py:375
  41.1 1.6 %collective-permute-start.2 = (f32[16,32,128]{2,1,0:T(8,128)S(1)}, f32[16,32,128]{2,1,0:T(8,128)S(1)}, u32[]{:S(2)}, u32[]{:S(2)}) collective-permute-start(f32[16,32,128]{2,1,0:T(8,128)S(1)} %get-tuple-element.27), channel_id=1, source_target_pairs={{0,1},{1,0},{2,3},{3,2},{4,5},{5,4},{6,7},{7,6},{8,9},{9,8},{10,11... | collective-permute-start | bytes 786440 | tf_op jit(solution)/shard_map/ppermute | solution.py:375
  42.8 5.6 %collective-permute-start.3 = (f32[8,32,128]{2,1,0:T(8,128)S(1)}, f32[8,32,128]{2,1,0:T(8,128)S(1)}, u32[]{:S(2)}, u32[]{:S(2)}) collective-permute-start(f32[8,32,128]{2,1,0:T(8,128)S(1)} %get-tuple-element.29), channel_id=1, source_target_pairs={{0,2},{1,3},{2,0},{3,1},{4,6},{5,7},{6,4},{7,5},{8,10},{9,11},{10,... | collective-permute-start | bytes 393224 | tf_op jit(solution)/shard_map/ppermute | solution.py:375

commit v2 on v1

v2 whole, which is shorter than its diff:
```python
import functools

import jax
import jax.numpy as jnp
from jax import lax
from jax.experimental import pallas as pl
from jax.experimental.pallas import tpu as pltpu
from jax.sharding import PartitionSpec as P

BLOCK = 32
BLOCKS = 3
NEWTON = 4
PAD = 8
damping = 0.5
def grant(mib):
    return pltpu.CompilerParams(vmem_limit_bytes=mib * 2**20)


VMEM = pl.BlockSpec(memory_space=pltpu.VMEM)
SMEM = pl.BlockSpec(memory_space=pltpu.SMEM)
HBM = pl.BlockSpec(memory_space=pltpu.HBM)


def in_hbm(array):
    return pltpu.with_memory_space_constraint(array, pltpu.HBM)


def friction_solve(drive, friction):
    rates = drive / (damping + friction)
    for newton_step in range(NEWTON - 1):
        squares = 1.0 + rates * rates
        inverse_root = lax.rsqrt(squares)
        magnitude = jnp.log(jnp.abs(rates) + squares * inverse_root)
        inverse_sinh = jnp.where(rates < 0, -magnitude, magnitude)
        misfit = damping * rates + friction * inverse_sinh - drive
        rates = rates - misfit / (damping + friction * inverse_root)
    return rates


def times_of(block_idx, width):
    steps = lax.broadcasted_iota(jnp.int32, (BLOCK, width), 0)
    return (steps + (block_idx * BLOCK + 1)).astype(jnp.float32)


def split(values):
    high = values.astype(jnp.bfloat16)
    return high, (values - high.astype(jnp.float32)).astype(jnp.bfloat16)


def wanted_patches(interactions_ref, slots, patch_count):
    sources = interactions_ref[pl.ds(1, 1), :]
    owners = lax.broadcasted_iota(jnp.int32, (slots, sources.shape[1]), 0)
    first = (owners * lax.axis_size("src") + lax.axis_index("src")) * patch_count
    offset = sources - first
    inside = (offset >= 0) & (offset < patch_count)
    wanted = jnp.max(jnp.where(inside, offset, 0).astype(jnp.float32), axis=1, keepdims=True)
    return owners, inside, wanted


def pack_kernel(interactions_ref, prestress_ref, friction_ref, load_ref, out_ref):
    slots, rows, width = out_ref.shape
    patch_count = prestress_ref.shape[0]
    wanted = wanted_patches(interactions_ref, slots, patch_count)[2]
    wanted = jnp.broadcast_to(wanted, (slots, width))
    for field, ref in enumerate((prestress_ref, friction_ref, load_ref)):
        out_ref[:, field * patch_count : (field + 1) * patch_count, :] = jnp.broadcast_to(
            ref[...][None], (slots, patch_count, width)
        )
    for slot in range(slots):
        out_ref[slot, rows - 1 :, :] = wanted[slot : slot + 1, :]


def split_lag(lag, raw, ker, halves, number):
    width = raw.shape[3]
    rows = raw.reshape(raw.shape[0], width * raw.shape[2], width)
    tile = rows[ker, pl.ds(lag, width, stride=raw.shape[2]), :]
    cols = slice(number * width, (number + 1) * width)
    halves[ker, :, cols], halves[halves.shape[0] // 2 + ker, :, cols] = split(tile)


def prepare_kernel(
    patch_count, lengths_ref, interactions_ref, kernel_ref, early, late_ref, table_ref, wanted_ref,
    interactions, lengths, raw, late, list_sems, load_sems, store_sems,
):
    ker_count, _, lag_count, width = kernel_ref.shape
    early_lags = early.shape[2] // width
    loads = [
        pltpu.make_async_copy(kernel_ref.at[ker], raw.at[ker, :, :lag_count, :], load_sems.at[ker])
        for ker in range(ker_count)
    ]
    list_loads = [
        pltpu.make_async_copy(interactions_ref, interactions, list_sems.at[0]),
        pltpu.make_async_copy(lengths_ref, lengths, list_sems.at[1]),
    ]
    for copy in list_loads + loads:
        copy.start()
    for copy in list_loads:
        copy.wait()

    slots = wanted_ref.shape[0]
    owners, inside, wanted = wanted_patches(interactions, slots, patch_count)
    wanted_ref[...] = jnp.broadcast_to(wanted, wanted_ref.shape)
    n_src = lax.axis_size("src")
    group_rows = n_src * patch_count
    receivers = interactions[pl.ds(0, 1), :] - lax.axis_index("recv") * group_rows
    strips = jnp.zeros_like(receivers)
    for other in range(1, n_src):
        strips = strips + (receivers >= other * patch_count).astype(jnp.int32)
    distance = strips ^ lax.axis_index("src")
    bits = n_src.bit_length() - 1
    order = jnp.zeros_like(distance)
    for bit in range(bits):
        order = order | (((distance >> bit) & 1) << (bits - 1 - bit))
    place = order * patch_count + receivers - strips * patch_count
    entry_numbers = lax.broadcasted_iota(jnp.int32, place.shape, 1)
    place = jnp.where(entry_numbers < lengths[0], place, group_rows)
    table_ref[pl.ds(0, 1), :] = place * BLOCK
    owner = jnp.max(
        jnp.where(inside, owners, 0).astype(jnp.float32), axis=0, keepdims=True
    ).astype(jnp.int32)
    ker_of = jnp.zeros_like(place)
    per_kernel = place.shape[1] // ker_count
    for ker in range(1, ker_count):
        ker_of = ker_of + (entry_numbers >= ker * per_kernel).astype(jnp.int32)
    span = lag_count + BLOCK
    table_ref[pl.ds(1, 1), :] = (
        (ker_of * slots + owner) * span + span - interactions[pl.ds(2, 1), :]
    )

    stores = [
        pltpu.make_async_copy(late.at[part], late_ref.at[part], store_sems.at[part])
        for part in range(2 * ker_count)
    ]
    for ker in range(ker_count):
        loads[ker].wait()
        for lag in range(early_lags, lag_count):
            split_lag(lag, raw, ker, late, lag - early_lags)
        stores[ker].start()
        stores[ker_count + ker].start()
        for lag in range(early_lags):
            split_lag(lag, raw, ker, early, lag)
    for copy in stores:
        copy.wait()


def first_block_kernel(prestress_ref, friction_ref, load_ref, out_ref):
    patch_count, width = prestress_ref.shape
    times = times_of(0, width)
    for patch in range(patch_count):
        row = pl.ds(patch, 1)
        drive = prestress_ref[row, :] + load_ref[row, :] * times
        out_ref[patch] = friction_solve(drive, jnp.broadcast_to(friction_ref[row, :], drive.shape))


def product(left, halves, parts):
    right = jnp.concatenate([halves[part] for part in parts], axis=0)
    return lax.dot_general(
        left, right, (((1,), (1,)), ((), ())), preferred_element_type=jnp.float32
    )


def convolve_and_route(
    window, stacked, responses, sums, early, late, late_copy, table_ref, totals
):
    slots, span, width = window.shape
    history = span - BLOCK
    ker_count = responses.shape[0]
    early_lags, late_lags = early.shape[2] // width, late.shape[2] // width
    chunk = stacked.shape[0] // (2 * BLOCK)
    rows = chunk * BLOCK
    chunks = slots // chunk

    def clear():
        for ker in range(ker_count):
            sums[ker][...] = jnp.zeros_like(sums[ker])

    if chunks > 1:
        clear()
        if late_copy is not None:
            late_copy.wait()

    def one_chunk(chunk_idx, carry):
        first = chunk_idx * chunk

        for lag in range(early_lags + late_lags):
            cols = slice(lag * width, (lag + 1) * width)
            for slot in range(chunk):
                upper, lower = split(
                    window[first + slot, history - lag : history - lag + BLOCK, :]
                )
                stacked[slot * BLOCK : (slot + 1) * BLOCK, cols] = upper
                stacked[rows + slot * BLOCK : rows + (slot + 1) * BLOCK, cols] = lower
        if chunks == 1:
            clear()

        def part(halves, taps):
            both = product(stacked[:, taps], halves, range(ker_count))
            rest = product(stacked[:rows, taps], halves, range(ker_count, 2 * ker_count))
            return both[:rows] + both[rows:] + rest

        total = part(early, slice(0, early_lags * width))
        if chunks == 1 and late_copy is not None:
            late_copy.wait()
        total = total + part(late, slice(early_lags * width, (early_lags + late_lags) * width))
        for ker in range(ker_count):
            for slot in range(chunk):
                responses[ker, first + slot, history:, :] = total[
                    slot * BLOCK : (slot + 1) * BLOCK, ker * width : (ker + 1) * width
                ]
        return carry

    if chunks == 1:
        one_chunk(0, 0)
    else:
        lax.fori_loop(0, chunks, one_chunk, 0)

    per_kernel = table_ref.shape[1] // ker_count
    every = responses.reshape(ker_count * slots * span, width)
    for entry in range(per_kernel):
        for ker in range(ker_count):
            idx = ker * per_kernel + entry
            place = pl.ds(pl.multiple_of(table_ref[0, idx], BLOCK), BLOCK)
            sums[ker][place, :] = sums[ker][place, :] + every[pl.ds(table_ref[1, idx], BLOCK), :]
    strips = totals[0].shape[0]
    patches = totals[0].shape[1]
    for group in range(2):
        for place in range(2 * strips * patches):
            part, strip, patch = place // (strips * patches), place // patches % strips, place % patches
            first = (part * strips + strip) * 2 * patches + group * patches + patch
            rows = slice(first * BLOCK, (first + 1) * BLOCK)
            total = sums[0][rows, :]
            for ker in range(1, ker_count):
                total = total + sums[ker][rows, :]
            totals[2 * group + part][strip, patch] = total


def first_stress_kernel(
    table_ref, wanted_ref, params_ref, early, late_ref,
    *refs,
):
    totals, (rates_tail_ref, responses_tail_ref, late) = refs[:4], refs[4:7]
    window, stacked, responses, late_sem, *sums = refs[7:]
    late_copy = pltpu.make_async_copy(late_ref.at[: late.shape[0]], late, late_sem)
    late_copy.start()
    slots, span, width = window.shape
    history = span - BLOCK
    patch_count = (params_ref.shape[1] - 1) // 3
    times = times_of(0, width)
    for ker in range(responses.shape[0]):
        responses[ker, :, :history, :] = jnp.zeros((slots, history, width), jnp.float32)

    patches = lax.broadcasted_iota(jnp.int32, (patch_count, width), 0).astype(jnp.float32)

    def one_slot(slot):
        chosen = patches == wanted_ref[pl.ds(slot, 1), :]

        def field(number):
            rows = params_ref[slot, number * patch_count : (number + 1) * patch_count, :]
            return jnp.sum(jnp.where(chosen, rows, 0.0), axis=0, keepdims=True)

        drive = field(0) + field(2) * times
        friction = jnp.broadcast_to(field(1), drive.shape)
        window[slot, :history, :] = jnp.zeros((history, width), jnp.float32)
        window[slot, history:, :] = friction_solve(drive, friction)

    if slots <= 8:
        for slot in range(slots):
            one_slot(slot)
    else:
        pl.loop(0, slots)(one_slot)
    convolve_and_route(
        window, stacked, responses, sums, early, late, late_copy, table_ref, totals
    )
    rates_tail_ref[...] = window[:, BLOCK:, :]
    responses_tail_ref[...] = responses[:, :, BLOCK:, :]


def next_stress_kernel(
    table_ref, rates_ref, rates_tail_ref, responses_tail_ref, early, late,
    *refs,
):
    totals, (window, stacked, responses, *sums) = refs[:4], refs[4:]
    history = window.shape[1] - BLOCK
    window[:, :history, :] = rates_tail_ref[...]
    window[:, history:, :] = rates_ref[...]
    responses[:, :, :history, :] = responses_tail_ref[...]
    convolve_and_route(
        window, stacked, responses, sums, early, late, None, table_ref, totals
    )


def solve_patch(
    block_idx, patch, first, prestress_ref, friction_ref, load_ref, kept_ref, came_ref
):
    width = prestress_ref.shape[1]
    row = pl.ds(first + patch, 1)
    stress = kept_ref[0, patch] + came_ref[0, patch]
    drive = prestress_ref[row, :] + load_ref[row, :] * times_of(block_idx, width) + stress
    return friction_solve(drive, jnp.broadcast_to(friction_ref[row, :], drive.shape))


def solve_group_kernel(
    block_idx, group, prestress_ref, friction_ref, load_ref, kept_ref, came_ref, rates_ref
):
    patches = rates_ref.shape[0]
    for patch in range(patches):
        rates_ref[patch] = solve_patch(
            block_idx, patch, group * patches, prestress_ref, friction_ref, load_ref,
            kept_ref, came_ref,
        )


def middle_block_kernel(
    asked_ref, prestress_ref, friction_ref, load_ref, kept_ref, came_ref, others_ref,
    rates_ref, outgoing_ref,
):
    patches = others_ref.shape[0]
    for patch in range(patches):
        rates_ref[patch] = others_ref[patch]
        rates_ref[patches + patch] = solve_patch(
            1, patch, patches, prestress_ref, friction_ref, load_ref, kept_ref, came_ref
        )

    def one_slot(slot):
        outgoing_ref[slot] = rates_ref[asked_ref[slot]]

    slots = outgoing_ref.shape[0]
    if slots <= 8:
        for slot in range(slots):
            one_slot(slot)
    else:
        pl.loop(0, slots)(one_slot)


def last_block_kernel(
    prestress_ref, friction_ref, load_ref, kept_ref, came_ref, others_ref, first_ref, second_ref,
    out_ref,
):
    patches = others_ref.shape[0]
    for patch in range(2 * patches):
        out_ref[patch, :BLOCK, :] = first_ref[patch]
        out_ref[patch, BLOCK : 2 * BLOCK, :] = second_ref[patch]
    for patch in range(patches):
        out_ref[patch, 2 * BLOCK :, :] = others_ref[patch]
        out_ref[patches + patch, 2 * BLOCK :, :] = solve_patch(
            2, patch, patches, prestress_ref, friction_ref, load_ref, kept_ref, came_ref
        )


def local(interactions, list_lengths, kernels, prestress, friction, load_rate):
    n_recv = lax.axis_size("recv")
    n_src = lax.axis_size("src")
    ker_count, width, lag_count, _ = kernels.shape
    patch_count = prestress.shape[0]
    group_rows = n_src * patch_count
    bits = n_src.bit_length() - 1
    assert n_src == 1 << bits and bits > 0

    f32, bf16 = jnp.float32, jnp.bfloat16
    packed = pl.pallas_call(
        pack_kernel,
        in_specs=[VMEM] * 4,
        out_specs=VMEM,
        out_shape=jax.ShapeDtypeStruct((n_recv, 3 * patch_count + 1, width), f32),
        compiler_params=grant(2 + n_recv // 8),
        name="pack",
    )(*map(in_hbm, (interactions, prestress, friction, load_rate)))
    received = lax.all_to_all(packed, "recv", split_axis=0, concat_axis=0, tiled=True)
    asked = received[:, -1, 0].astype(jnp.int32)

    late_lags = lag_count // 4
    early = jax.ShapeDtypeStruct((2 * ker_count, width, (lag_count - late_lags) * width), bf16)
    late_shape = (2 * ker_count, width, late_lags * width)
    late_halves = pltpu.VMEM(late_shape, bf16)
    kernels = in_hbm(kernels)
    early, late, table, wanted = pl.pallas_call(
        functools.partial(prepare_kernel, patch_count),
        in_specs=[HBM] * 3,
        out_specs=[VMEM, HBM, VMEM, VMEM],
        out_shape=[
            early,
            jax.ShapeDtypeStruct((24 * ker_count,) + late_shape[1:], bf16),
            jax.ShapeDtypeStruct((2, interactions.shape[1]), jnp.int32),
            jax.ShapeDtypeStruct((n_recv, width), f32),
        ],
        scratch_shapes=[
            pltpu.VMEM(interactions.shape, jnp.int32),
            pltpu.SMEM(list_lengths.shape, jnp.int32),
            pltpu.VMEM((ker_count, width, lag_count + PAD, width), f32),
            late_halves,
            pltpu.SemaphoreType.DMA((2,)),
            pltpu.SemaphoreType.DMA((ker_count,)),
            pltpu.SemaphoreType.DMA((2 * ker_count,)),
        ],
        compiler_params=grant(46),
        name="prepare",
    )(list_lengths, in_hbm(interactions), kernels)
    late_shape, late = jax.ShapeDtypeStruct(late_shape, bf16), in_hbm(late)
    first_rates = pl.pallas_call(
        first_block_kernel,
        in_specs=[VMEM] * 3,
        out_specs=VMEM,
        out_shape=jax.ShapeDtypeStruct((patch_count, BLOCK, width), f32),
        compiler_params=grant(2),
        name="first_block",
    )(prestress, friction, load_rate)

    group_patches = patch_count // 2
    half = jax.ShapeDtypeStruct((n_src // 2, group_patches, BLOCK, width), f32)
    rates_tail = jax.ShapeDtypeStruct((n_recv, lag_count, width), f32)
    responses_tail = jax.ShapeDtypeStruct((ker_count, n_recv, lag_count, width), f32)
    chunk = min(8, n_recv)
    stress_mib = 16 + 8 * ker_count * n_recv * (lag_count + BLOCK) * width // 2**20
    scratch = [
        pltpu.VMEM((n_recv, lag_count + BLOCK, width), f32),
        pltpu.VMEM((2 * chunk * BLOCK, lag_count * width), bf16),
        pltpu.VMEM((ker_count, n_recv, lag_count + BLOCK, width), f32),
    ] + [pltpu.VMEM(((group_rows + 1) * BLOCK, width), f32)] * ker_count

    def reduce_scatter(kept, sent):
        for bit in range(bits):
            pairs = [(i, i ^ (1 << bit)) for i in range(n_src)]
            came = lax.ppermute(sent, "src", pairs)
            if bit == bits - 1:
                return kept, came
            quarter = kept.shape[0] // 2
            sent = kept[quarter:] + came[quarter:]
            kept = kept[:quarter] + came[:quarter]

    rates_group = jax.ShapeDtypeStruct((group_patches, BLOCK, width), f32)

    def solve_first_group(block_idx, terms):
        return pl.pallas_call(
            functools.partial(solve_group_kernel, block_idx, 0),
            in_specs=[VMEM] * 5,
            out_specs=VMEM,
            out_shape=rates_group,
            compiler_params=grant(2),
            name="solve_group",
        )(prestress, friction, load_rate, *terms)

    *totals, rates_tail, responses_tail, late = pl.pallas_call(
        first_stress_kernel,
        in_specs=[SMEM] + [VMEM] * 3 + [HBM],
        out_specs=[VMEM] * 7,
        out_shape=[half] * 4 + [rates_tail, responses_tail, late_shape],
        scratch_shapes=scratch[:3] + [pltpu.SemaphoreType.DMA] + scratch[3:],
        compiler_params=grant(stress_mib),
        name="first_stress",
    )(table, wanted, received, early, late)
    terms = [reduce_scatter(*totals[:2]), reduce_scatter(*totals[2:])]
    second_rates, outgoing = pl.pallas_call(
        middle_block_kernel,
        in_specs=[SMEM] + [VMEM] * 6,
        out_specs=[VMEM] * 2,
        out_shape=[
            jax.ShapeDtypeStruct((patch_count, BLOCK, width), f32),
            jax.ShapeDtypeStruct((n_recv, BLOCK, width), f32),
        ],
        compiler_params=grant(4),
        name="middle_block",
    )(asked, prestress, friction, load_rate, *terms[1], solve_first_group(1, terms[0]))
    rates = lax.all_to_all(outgoing, "recv", split_axis=0, concat_axis=0, tiled=True)
    totals = pl.pallas_call(
        next_stress_kernel,
        in_specs=[SMEM] + [VMEM] * 5,
        out_specs=[VMEM] * 4,
        out_shape=[half] * 4,
        scratch_shapes=scratch,
        compiler_params=grant(stress_mib),
        name="next_stress",
    )(table, rates, rates_tail, responses_tail, early, late)
    terms = [reduce_scatter(*totals[:2]), reduce_scatter(*totals[2:])]
    return pl.pallas_call(
        last_block_kernel,
        in_specs=[VMEM] * 8,
        out_specs=VMEM,
        out_shape=jax.ShapeDtypeStruct((patch_count, BLOCKS * BLOCK, width), f32),
        compiler_params=grant(4),
        name="last_block",
    )(
        prestress, friction, load_rate, *terms[1], solve_first_group(2, terms[0]),
        first_rates, second_rates,
    )


def solution(mesh):
    in_specs = (
        P(None, ("recv", "src")),
        P(("recv", "src")),
        P(("recv", "src"), None, None, None),
        P(("recv", "src"), None),
        P(("recv", "src"), None),
        P(("recv", "src"), None),
    )
    out_specs = P(("recv", "src"), None, None)
    return jax.shard_map(local, mesh=mesh, in_specs=in_specs, out_specs=out_specs, check_vma=False)
```

time: 49.8 us -> 48.5 us (0.974)
  starting transfers between devices: 10.6 us -> 12.7 us
  waiting for transfers between devices: 13.5 us -> 11.5 us
  Pallas kernels: 14.1 us -> 13 us
    ppermute x4 -> x8, waiting for transfers between devices: 10.5 us -> 8.05 us  [reduce_scatter(): came = lax.ppermute(sent, 'src', pairs)]
    ppermute x4 -> x8, starting transfers between devices: 3.3 us -> 5.45 us  [reduce_scatter(): came = lax.ppermute(sent, 'src', pairs)]
    pallas_call x1, Pallas kernels: 3.89 us -> 3.28 us  [local(): pl.pallas_call(first_stress_kernel, in_specs=[SMEM] + [VMEM] * 3 + [HBM],...]
    all_to_all x1, waiting for transfers between devices: 2.92 us -> 3.49 us  [local(): lax.all_to_all(packed, 'recv', split_axis=0, concat_axis=0, tiled=True)]
    pallas_call x1, Pallas kernels: 3.73 us -> 3.2 us  [local(): pl.pallas_call(functools.partial(prepare_kernel, patch_count), in_specs=[...]
    all_to_all x1, blocking collectives: 10.2 us -> 9.74 us  [local(): lax.all_to_all(outgoing, 'recv', split_axis=0, concat_axis=0, tiled=True)]
    pallas_call x2 -> x4, Pallas kernels: 1.93 us -> 2.04 us  [the longest x1 0.94 us: local(): pl.pallas_call(last_block_kernel, in_specs=[VMEM] * 8, out_specs=VMEM, ou...]
  transfers between devices with their start and end apart: 5 -> 9, of which waited for: 5 -> 7; matrix products, arithmetic and copies ran while one was open for 0% -> 1% of each run, Pallas kernels for 8% -> 8%
where the time goes in v2:
time: 48.5 us; the launch traced here: 48.1 us
  Pallas kernels  13 us (27%)
  starting transfers between devices  12.7 us (26%)
  waiting for transfers between devices  11.5 us (24%)
  blocking collectives  9.74 us (20%)
  between operations  0.73 us (2%)
    all_to_all x1, blocking collectives, local(): lax.all_to_all(outgoing, 'recv', split_axis=0, concat_axis=0, tiled=True)  9.74 us
    ppermute x8, waiting for transfers between devices, reduce_scatter(): came = lax.ppermute(sent, 'src', pairs)  8.05 us
    all_to_all x1, starting transfers between devices, local(): lax.all_to_all(packed, 'recv', split_axis=0, concat_axis=0, tiled=True)  7.28 us
    ppermute x8, starting transfers between devices, reduce_scatter(): came = lax.ppermute(sent, 'src', pairs)  5.45 us
    all_to_all x1, waiting for transfers between devices, local(): lax.all_to_all(packed, 'recv', split_axis=0, concat_axis=0, tiled=True)  3.49 us
    pallas_call x1, Pallas kernels, local(): pl.pallas_call(first_stress_kernel, in_specs=[SMEM] + [VMEM] * 3 + [HBM],...  3.28 us
    pallas_call x1, Pallas kernels, local(): pl.pallas_call(functools.partial(prepare_kernel, patch_count), in_specs=[...  3.2 us
    pallas_call x1, Pallas kernels, local(): pl.pallas_call(next_stress_kernel, in_specs=[SMEM] + [VMEM] * 5, out_spec...  2.74 us
  transfers between devices with their start and end apart: 9, of which 7 were waited for; matrix products, arithmetic and copies ran while one was open for 1% of the time, Pallas kernels for 8%

profile of v2, /device:TPU:0, one launch (start us, length us, event | category | flops | bytes accessed | tf_op | source)
XLA Modules:
  0.0 48.1 jit_solution(15478424323099369392)
XLA Ops:
  0.0 1.5 %pack.1 = f32[8,25,128]{2,1,0:T(8,128)} custom-call(s32[3,96]{1,0:T(4,128)} %interactions_ref.3, f32[8,128]{1,0:T(8,128)} %prestress_ref.11, f32[8,128]{1,0:T(8,128)} %friction_ref.11, f32[8,128]{1,0:T(8,128)} %load_ref.11), custom_call_target="tpu_custom_call" | custom-call | tf_op jit(solution)/shard_map/pack/pallas_call | solution.py:360
  1.5 7.3 %all-to-all-start = ((f32[8,25,128]{2,1,0:T(8,128)}), f32[8,25,128]{2,1,0:T(8,128)S(1)}, u32[]{:S(2)}, u32[]{:S(2)}) async-start(f32[8,25,128]{2,1,0:T(8,128)} %pack.1), calls=%async_computation | async-start | bytes 262144 | tf_op jit(solution)/shard_map/all_to_all | solution.py:368
  9.4 3.2 %prepare.1 = (bf16[8,128,1536]{2,1,0:T(8,128)(2,1)S(1)}, bf16[96,128,512]{2,1,0:T(8,128)(2,1)}, s32[2,96]{1,0:T(2,128)S(1)}, f32[8,128]{1,0:T(8,128)S(1)}) custom-call(s32[1]{0:T(128)S(6)} %copy.7.lengths_ref, s32[3,96]{1,0:T(4,128)} %interactions_ref.3, f32[4,128,16,128]{3,2,1,0:T(8,128)} %kernel_ref.1), custom_call_target="tpu_custom_call" | custom-call | tf_op jit(solution)/shard_map/prepare/pallas_call | solution.py:376
  12.6 3.5 %all-to-all-done.params_ref = f32[8,25,128]{2,1,0:T(8,128)S(1)} async-done(((f32[8,25,128]{2,1,0:T(8,128)}), f32[8,25,128]{2,1,0:T(8,128)S(1)}, u32[]{:S(2)}, u32[]{:S(2)}) %all-to-all-start) | async-done | bytes 102432 | tf_op jit(solution)/shard_map/all_to_all | solution.py:368
  16.1 3.3 %first_stress.1 = (f32[2,4,32,128]{3,2,1,0:T(8,128)S(1)}, f32[2,4,32,128]{3,2,1,0:T(8,128)S(1)}, f32[2,4,32,128]{3,2,1,0:T(8,128)S(1)}, f32[2,4,32,128]{3,2,1,0:...) custom-call(s32[2,96]{1,0:T(2,128)S(1)} %get-tuple-element.22.table_ref, ...), custom_call_target="tpu_custom_call" | custom-call | tf_op jit(solution)/shard_map/first_stress/pallas_call | solution.py:442
  19.5 0.5 %collective-permute-start = (f32[2,4,32,128]{3,2,1,0:T(8,128)S(1)}, f32[2,4,32,128]{3,2,1,0:T(8,128)S(1)}, u32[]{:S(2)}, u32[]{:S(2)}) collective-permute-start(f32[2,4,32,128]{3,2,1,0:T(8,128)S(1)} %get-tuple-element.27), channel_id=1, source_target_pairs={{0,1},{1,0},{2,3},{3,2},{4,5},{5,4},{6,7},{7,6},{8,9},{9,8},{10,11... | collective-permute-start | bytes 393224 | tf_op jit(solution)/shard_map/ppermute | solution.py:423
  20.0 0.8 %collective-permute-done.2 = f32[2,4,32,128]{3,2,1,0:T(8,128)S(1)} collective-permute-done((f32[2,4,32,128]{3,2,1,0:T(8,128)S(1)}, f32[2,4,32,128]{3,2,1,0:T(8,128)S(1)}, u32[]{:S(2)}, u32[]{:S(2)}) %collective-permute-start.2) | collective-permute-done | bytes 131104 | tf_op jit(solution)/shard_map/ppermute | solution.py:423
  20.8 1.6 %collective-permute-start.3 = (f32[1,4,32,128]{3,2,1,0:T(8,128)S(1)}, f32[1,4,32,128]{3,2,1,0:T(8,128)S(1)}, u32[]{:S(2)}, u32[]{:S(2)}) collective-permute-start(f32[1,4,32,128]{3,2,1,0:T(8,128)S(1)} %get-tuple-element.43), channel_id=1, source_target_pairs={{0,2},{1,3},{2,0},{3,1},{4,6},{5,7},{6,4},{7,5},{8,10},{9,11},{10,... | collective-permute-start | bytes 196616 | tf_op jit(solution)/shard_map/ppermute | solution.py:423
  22.4 0.6 %collective-permute-start.1 = (f32[1,4,32,128]{3,2,1,0:T(8,128)S(1)}, f32[1,4,32,128]{3,2,1,0:T(8,128)S(1)}, u32[]{:S(2)}, u32[]{:S(2)}) collective-permute-start(f32[1,4,32,128]{3,2,1,0:T(8,128)S(1)} %get-tuple-element.45), channel_id=1, source_target_pairs={{0,2},{1,3},{2,0},{3,1},{4,6},{5,7},{6,4},{7,5},{8,10},{9,11},{10,... | collective-permute-start | bytes 196616 | tf_op jit(solution)/shard_map/ppermute | solution.py:423
  23.0 0.2 fusion.asked_ref
  23.3 2.1 %collective-permute-done.3.came_ref = f32[1,4,32,128]{3,2,1,0:T(8,128)S(1)} collective-permute-done((f32[1,4,32,128]{3,2,1,0:T(8,128)S(1)}, f32[1,4,32,128]{3,2,1,0:T(8,128)S(1)}, u32[]{:S(2)}, u32[]{:S(2)}) %collective-permute-start.3) | collective-permute-done | bytes 65568 | tf_op jit(solution)/shard_map/ppermute | solution.py:423
  25.4 0.2 solve_group.2.others_ref
  25.6 1.2 %collective-permute-done.1.came_ref = f32[1,4,32,128]{3,2,1,0:T(8,128)S(1)} collective-permute-done((f32[1,4,32,128]{3,2,1,0:T(8,128)S(1)}, f32[1,4,32,128]{3,2,1,0:T(8,128)S(1)}, u32[]{:S(2)}, u32[]{:S(2)}) %collective-permute-start.1) | collective-permute-done | bytes 65568 | tf_op jit(solution)/shard_map/ppermute | solution.py:423
  26.8 0.7 %middle_block.1 = (f32[8,32,128]{2,1,0:T(8,128)S(1)}, f32[8,32,128]{2,1,0:T(8,128)S(1)}) custom-call(s32[8]{0:T(128)S(1)} %fusion.asked_ref, f32[8,128]{1,0:T(8,128)S(1)} %copy-done, f32[8,128]{1,0:T(8,128)S(1)} %copy-done.1, f32[8,128]{1,0:T(8,128)S(1)} %copy-done.2, f32[1,4,32,128]{3,2,1,0:T(8,128)S(1)} %get-tuple-element.46.kept_ref, ...), custom_call_target="tpu_custom_call" | custom-call | tf_op jit(solution)/shard_map/middle_block/pallas_call | solution.py:452
  27.5 9.7 %all_to_all.10.rates_ref = f32[8,32,128]{2,1,0:T(8,128)S(1)} all-to-all(f32[8,32,128]{2,1,0:T(8,128)S(1)} %get-tuple-element.30), channel_id=1, replica_groups=mesh['recv'=8,'src'=4] {'recv'}, dimensions={0} | all-to-all | bytes 262144 | tf_op jit(solution)/shard_map/all_to_all | solution.py:463
  37.2 2.7 %next_stress.1 = (f32[2,4,32,128]{3,2,1,0:T(8,128)S(1)}, f32[2,4,32,128]{3,2,1,0:T(8,128)S(1)}, f32[2,4,32,128]{3,2,1,0:T(8,128)S(1)}, f32[2,4,32,128]{3,2,1,0:T(8,128)S(1)}) custom-call(s32[2,96]{1,0:T(2,128)S(1)} %get-tuple-element.22.table_ref, f32[8,32,128]{2,1,0:T(8,128)S(1)} %all_to_all.10.rates_ref, ...), custom_call_target="tpu_custom_call" | custom-call | tf_op jit(solution)/shard_map/next_stress/pallas_call | solution.py:464
  40.1 0.5 %collective-permute-start.4 = (f32[2,4,32,128]{3,2,1,0:T(8,128)S(1)}, f32[2,4,32,128]{3,2,1,0:T(8,128)S(1)}, u32[]{:S(2)}, u32[]{:S(2)}) collective-permute-start(f32[2,4,32,128]{3,2,1,0:T(8,128)S(1)} %get-tuple-element.35), channel_id=1, source_target_pairs={{0,1},{1,0},{2,3},{3,2},{4,5},{5,4},{6,7},{7,6},{8,9},{9,8},{10,11... | collective-permute-start | bytes 393224 | tf_op jit(solution)/shard_map/ppermute | solution.py:423
  40.6 0.8 %collective-permute-done.6 = f32[2,4,32,128]{3,2,1,0:T(8,128)S(1)} collective-permute-done((f32[2,4,32,128]{3,2,1,0:T(8,128)S(1)}, f32[2,4,32,128]{3,2,1,0:T(8,128)S(1)}, u32[]{:S(2)}, u32[]{:S(2)}) %collective-permute-start.6) | collective-permute-done | bytes 131104 | tf_op jit(solution)/shard_map/ppermute | solution.py:423
  41.4 1.2 %collective-permute-start.7 = (f32[1,4,32,128]{3,2,1,0:T(8,128)S(1)}, f32[1,4,32,128]{3,2,1,0:T(8,128)S(1)}, u32[]{:S(2)}, u32[]{:S(2)}) collective-permute-start(f32[1,4,32,128]{3,2,1,0:T(8,128)S(1)} %get-tuple-element.39), channel_id=1, source_target_pairs={{0,2},{1,3},{2,0},{3,1},{4,6},{5,7},{6,4},{7,5},{8,10},{9,11},{10,... | collective-permute-start | bytes 196616 | tf_op jit(solution)/shard_map/ppermute | solution.py:423
  42.7 0.9 %collective-permute-start.5 = (f32[1,4,32,128]{3,2,1,0:T(8,128)S(1)}, f32[1,4,32,128]{3,2,1,0:T(8,128)S(1)}, u32[]{:S(2)}, u32[]{:S(2)}) collective-permute-start(f32[1,4,32,128]{3,2,1,0:T(8,128)S(1)} %get-tuple-element.41), channel_id=1, source_target_pairs={{0,2},{1,3},{2,0},{3,1},{4,6},{5,7},{6,4},{7,5},{8,10},{9,11},{10,... | collective-permute-start | bytes 196616 | tf_op jit(solution)/shard_map/ppermute | solution.py:423
  43.6 0.3 first_block.1.first_ref
  43.9 2.4 %collective-permute-done.7.came_ref = f32[1,4,32,128]{3,2,1,0:T(8,128)S(1)} collective-permute-done((f32[1,4,32,128]{3,2,1,0:T(8,128)S(1)}, f32[1,4,32,128]{3,2,1,0:T(8,128)S(1)}, u32[]{:S(2)}, u32[]{:S(2)}) %collective-permute-start.7) | collective-permute-done | bytes 65568 | tf_op jit(solution)/shard_map/ppermute | solution.py:423
  46.5 0.7 %collective-permute-done.5.came_ref = f32[1,4,32,128]{3,2,1,0:T(8,128)S(1)} collective-permute-done((f32[1,4,32,128]{3,2,1,0:T(8,128)S(1)}, f32[1,4,32,128]{3,2,1,0:T(8,128)S(1)}, u32[]{:S(2)}, u32[]{:S(2)}) %collective-permute-start.5) | collective-permute-done | bytes 65568 | tf_op jit(solution)/shard_map/ppermute | solution.py:423
  47.2 0.9 %last_block.1 = f32[8,96,128]{2,1,0:T(8,128)} custom-call(f32[8,128]{1,0:T(8,128)S(1)} %copy-done, f32[8,128]{1,0:T(8,128)S(1)} %copy-done.1, f32[8,128]{1,0:T(8,128)S(1)} %copy-done.2, f32[1,4,32,128]{3,2,1,0:T(8,128)S(1)} %get-tuple-element.42.kept_ref, f32[1,4,32,128]{3,2,1,0:T(8,128)S(1)} %collective-permute-done.5.came_ref, ...), custom_call_target="tpu_custom_call" | custom-call | tf_op jit(solution)/shard_map/last_block/pallas_call | solution.py:474
  (15 shorter events, 0.4 us)
Async XLA Ops:
  1.5 14.6 %all-to-all-start = ((f32[8,25,128]{2,1,0:T(8,128)}), f32[8,25,128]{2,1,0:T(8,128)S(1)}, u32[]{:S(2)}, u32[]{:S(2)}) async-start(f32[8,25,128]{2,1,0:T(8,128)} %pack.1), calls=%async_computation | async-start | bytes 262144 | tf_op jit(solution)/shard_map/all_to_all | solution.py:368
  16.1 9.3 %copy-start = (f32[8,128]{1,0:T(8,128)S(1)}, f32[8,128]{1,0:T(8,128)}, u32[]{:S(2)}) copy-start(f32[8,128]{1,0:T(8,128)} %prestress_ref.11) | copy-start | bytes 12292
  16.1 9.3 %copy-start.1 = (f32[8,128]{1,0:T(8,128)S(1)}, f32[8,128]{1,0:T(8,128)}, u32[]{:S(2)}) copy-start(f32[8,128]{1,0:T(8,128)} %friction_ref.11) | copy-start | bytes 12292
  16.1 9.3 %copy-start.2 = (f32[8,128]{1,0:T(8,128)S(1)}, f32[8,128]{1,0:T(8,128)}, u32[]{:S(2)}) copy-start(f32[8,128]{1,0:T(8,128)} %load_ref.11) | copy-start | bytes 12292
  19.4 1.4 %collective-permute-start.2 = (f32[2,4,32,128]{3,2,1,0:T(8,128)S(1)}, f32[2,4,32,128]{3,2,1,0:T(8,128)S(1)}, u32[]{:S(2)}, u32[]{:S(2)}) collective-permute-start(f32[2,4,32,128]{3,2,1,0:T(8,128)S(1)} %get-tuple-element.29), channel_id=1, source_target_pairs={{0,1},{1,0},{2,3},{3,2},{4,5},{5,4},{6,7},{7,6},{8,9},{9,8},{10,11... | collective-permute-start | bytes 393224 | tf_op jit(solution)/shard_map/ppermute | solution.py:423
  19.5 2.9 %collective-permute-start = (f32[2,4,32,128]{3,2,1,0:T(8,128)S(1)}, f32[2,4,32,128]{3,2,1,0:T(8,128)S(1)}, u32[]{:S(2)}, u32[]{:S(2)}) collective-permute-start(f32[2,4,32,128]{3,2,1,0:T(8,128)S(1)} %get-tuple-element.27), channel_id=1, source_target_pairs={{0,1},{1,0},{2,3},{3,2},{4,5},{5,4},{6,7},{7,6},{8,9},{9,8},{10,11... | collective-permute-start | bytes 393224 | tf_op jit(solution)/shard_map/ppermute | solution.py:423
  20.8 4.5 %collective-permute-start.3 = (f32[1,4,32,128]{3,2,1,0:T(8,128)S(1)}, f32[1,4,32,128]{3,2,1,0:T(8,128)S(1)}, u32[]{:S(2)}, u32[]{:S(2)}) collective-permute-start(f32[1,4,32,128]{3,2,1,0:T(8,128)S(1)} %get-tuple-element.43), channel_id=1, source_target_pairs={{0,2},{1,3},{2,0},{3,1},{4,6},{5,7},{6,4},{7,5},{8,10},{9,11},{10,... | collective-permute-start | bytes 196616 | tf_op jit(solution)/shard_map/ppermute | solution.py:423
  22.4 4.3 %collective-permute-start.1 = (f32[1,4,32,128]{3,2,1,0:T(8,128)S(1)}, f32[1,4,32,128]{3,2,1,0:T(8,128)S(1)}, u32[]{:S(2)}, u32[]{:S(2)}) collective-permute-start(f32[1,4,32,128]{3,2,1,0:T(8,128)S(1)} %get-tuple-element.45), channel_id=1, source_target_pairs={{0,2},{1,3},{2,0},{3,1},{4,6},{5,7},{6,4},{7,5},{8,10},{9,11},{10,... | collective-permute-start | bytes 196616 | tf_op jit(solution)/shard_map/ppermute | solution.py:423
  40.0 1.4 %collective-permute-start.6 = (f32[2,4,32,128]{3,2,1,0:T(8,128)S(1)}, f32[2,4,32,128]{3,2,1,0:T(8,128)S(1)}, u32[]{:S(2)}, u32[]{:S(2)}) collective-permute-start(f32[2,4,32,128]{3,2,1,0:T(8,128)S(1)} %get-tuple-element.37), channel_id=1, source_target_pairs={{0,1},{1,0},{2,3},{3,2},{4,5},{5,4},{6,7},{7,6},{8,9},{9,8},{10,11... | collective-permute-start | bytes 393224 | tf_op jit(solution)/shard_map/ppermute | solution.py:423
  40.1 2.6 %collective-permute-start.4 = (f32[2,4,32,128]{3,2,1,0:T(8,128)S(1)}, f32[2,4,32,128]{3,2,1,0:T(8,128)S(1)}, u32[]{:S(2)}, u32[]{:S(2)}) collective-permute-start(f32[2,4,32,128]{3,2,1,0:T(8,128)S(1)} %get-tuple-element.35), channel_id=1, source_target_pairs={{0,1},{1,0},{2,3},{3,2},{4,5},{5,4},{6,7},{7,6},{8,9},{9,8},{10,11... | collective-permute-start | bytes 393224 | tf_op jit(solution)/shard_map/ppermute | solution.py:423
  41.4 4.9 %collective-permute-start.7 = (f32[1,4,32,128]{3,2,1,0:T(8,128)S(1)}, f32[1,4,32,128]{3,2,1,0:T(8,128)S(1)}, u32[]{:S(2)}, u32[]{:S(2)}) collective-permute-start(f32[1,4,32,128]{3,2,1,0:T(8,128)S(1)} %get-tuple-element.39), channel_id=1, source_target_pairs={{0,2},{1,3},{2,0},{3,1},{4,6},{5,7},{6,4},{7,5},{8,10},{9,11},{10,... | collective-permute-start | bytes 196616 | tf_op jit(solution)/shard_map/ppermute | solution.py:423
  42.7 4.5 %collective-permute-start.5 = (f32[1,4,32,128]{3,2,1,0:T(8,128)S(1)}, f32[1,4,32,128]{3,2,1,0:T(8,128)S(1)}, u32[]{:S(2)}, u32[]{:S(2)}) collective-permute-start(f32[1,4,32,128]{3,2,1,0:T(8,128)S(1)} %get-tuple-element.41), channel_id=1, source_target_pairs={{0,2},{1,3},{2,0},{3,1},{4,6},{5,7},{6,4},{7,5},{8,10},{9,11},{10,... | collective-permute-start | bytes 196616 | tf_op jit(solution)/shard_map/ppermute | solution.py:423

commit v3 on v2

--- a/solution.py
+++ b/solution.py
@@ -143,13 +143,21 @@
         copy.wait()
 
 
-def first_block_kernel(prestress_ref, friction_ref, load_ref, out_ref):
+def first_blocks_kernel(
+    prestress_ref, friction_ref, load_ref, second_ref, out_ref, rates, sems
+):
     patch_count, width = prestress_ref.shape
+    second = pltpu.make_async_copy(second_ref, out_ref.at[:, BLOCK : 2 * BLOCK], sems.at[0])
+    second.start()
     times = times_of(0, width)
     for patch in range(patch_count):
         row = pl.ds(patch, 1)
         drive = prestress_ref[row, :] + load_ref[row, :] * times
-        out_ref[patch] = friction_solve(drive, jnp.broadcast_to(friction_ref[row, :], drive.shape))
+        rates[patch] = friction_solve(drive, jnp.broadcast_to(friction_ref[row, :], drive.shape))
+    first = pltpu.make_async_copy(rates, out_ref.at[:, :BLOCK], sems.at[1])
+    first.start()
+    second.wait()
+    first.wait()
 
 
 def product(left, halves, parts):
@@ -160,7 +168,7 @@
 
 
 def convolve_and_route(
-    window, stacked, responses, sums, early, late, late_copy, table_ref, totals
+    window, stacked, responses, sums, early, late, late_copy, table, table_copy, totals
 ):
     slots, span, width = window.shape
     history = span - BLOCK
@@ -214,24 +222,26 @@
     else:
         lax.fori_loop(0, chunks, one_chunk, 0)
 
-    per_kernel = table_ref.shape[1] // ker_count
+    table_copy.wait()
+    per_kernel = table.shape[1] // ker_count
     every = responses.reshape(ker_count * slots * span, width)
     for entry in range(per_kernel):
         for ker in range(ker_count):
             idx = ker * per_kernel + entry
-            place = pl.ds(pl.multiple_of(table_ref[0, idx], BLOCK), BLOCK)
-            sums[ker][place, :] = sums[ker][place, :] + every[pl.ds(table_ref[1, idx], BLOCK), :]
+            place = pl.ds(pl.multiple_of(table[0, idx], BLOCK), BLOCK)
+            sums[ker][place, :] = sums[ker][place, :] + every[pl.ds(table[1, idx], BLOCK), :]
     strips = totals[0].shape[0]
-    patches = totals[0].shape[1]
+    counts = totals[0].shape[1], totals[2].shape[1]
     for group in range(2):
-        for place in range(2 * strips * patches):
-            part, strip, patch = place // (strips * patches), place // patches % strips, place % patches
-            first = (part * strips + strip) * 2 * patches + group * patches + patch
-            rows = slice(first * BLOCK, (first + 1) * BLOCK)
-            total = sums[0][rows, :]
-            for ker in range(1, ker_count):
-                total = total + sums[ker][rows, :]
-            totals[2 * group + part][strip, patch] = total
+        for part in range(2):
+            for strip in range(strips):
+                for patch in range(counts[group]):
+                    place = (part * strips + strip) * sum(counts) + group * counts[0] + patch
+                    rows = slice(place * BLOCK, (place + 1) * BLOCK)
+                    total = sums[0][rows, :]
+                    for ker in range(1, ker_count):
+                        total = total + sums[ker][rows, :]
+                    totals[2 * group + part][strip, patch] = total
 
 
 def first_stress_kernel(
@@ -239,7 +249,9 @@
     *refs,
 ):
     totals, (rates_tail_ref, responses_tail_ref, late) = refs[:4], refs[4:7]
-    window, stacked, responses, late_sem, *sums = refs[7:]
+    window, stacked, responses, late_sem, table, table_sem, *sums = refs[7:]
+    table_copy = pltpu.make_async_copy(table_ref, table, table_sem)
+    table_copy.start()
     late_copy = pltpu.make_async_copy(late_ref.at[: late.shape[0]], late, late_sem)
     late_copy.start()
     slots, span, width = window.shape
@@ -269,7 +281,7 @@
     else:
         pl.loop(0, slots)(one_slot)
     convolve_and_route(
-        window, stacked, responses, sums, early, late, late_copy, table_ref, totals
+        window, stacked, responses, sums, early, late, late_copy, table, table_copy, totals
     )
     rates_tail_ref[...] = window[:, BLOCK:, :]
     responses_tail_ref[...] = responses[:, :, BLOCK:, :]
@@ -279,13 +291,15 @@
     table_ref, rates_ref, rates_tail_ref, responses_tail_ref, early, late,
     *refs,
 ):
-    totals, (window, stacked, responses, *sums) = refs[:4], refs[4:]
+    totals, (window, stacked, responses, table, table_sem, *sums) = refs[:4], refs[4:]
+    table_copy = pltpu.make_async_copy(table_ref, table, table_sem)
+    table_copy.start()
     history = window.shape[1] - BLOCK
     window[:, :history, :] = rates_tail_ref[...]
     window[:, history:, :] = rates_ref[...]
     responses[:, :, :history, :] = responses_tail_ref[...]
     convolve_and_route(
-        window, stacked, responses, sums, early, late, None, table_ref, totals
+        window, stacked, responses, sums, early, late, None, table, table_copy, totals
     )
 
 
@@ -300,29 +314,33 @@
 
 
 def solve_group_kernel(
-    block_idx, group, prestress_ref, friction_ref, load_ref, kept_ref, came_ref, rates_ref
-):
-    patches = rates_ref.shape[0]
-    for patch in range(patches):
+    block_idx, prestress_ref, friction_ref, load_ref, kept_ref, came_ref, rates_ref
+):
+    for patch in range(rates_ref.shape[0]):
         rates_ref[patch] = solve_patch(
-            block_idx, patch, group * patches, prestress_ref, friction_ref, load_ref,
-            kept_ref, came_ref,
+            block_idx, patch, 0, prestress_ref, friction_ref, load_ref, kept_ref, came_ref
         )
 
 
 def middle_block_kernel(
-    asked_ref, prestress_ref, friction_ref, load_ref, kept_ref, came_ref, others_ref,
+    received_ref, prestress_ref, friction_ref, load_ref, kept_ref, came_ref, others_ref,
     rates_ref, outgoing_ref,
 ):
-    patches = others_ref.shape[0]
-    for patch in range(patches):
-        rates_ref[patch] = others_ref[patch]
-        rates_ref[patches + patch] = solve_patch(
-            1, patch, patches, prestress_ref, friction_ref, load_ref, kept_ref, came_ref
+    known = others_ref.shape[0]
+    rates_ref[:known] = others_ref[...]
+    for patch in range(rates_ref.shape[0] - known):
+        rates_ref[known + patch] = solve_patch(
+            1, patch, known, prestress_ref, friction_ref, load_ref, kept_ref, came_ref
         )
 
+    asked_row = received_ref.shape[1] - 1
+
     def one_slot(slot):
-        outgoing_ref[slot] = rates_ref[asked_ref[slot]]
+        asked = jnp.broadcast_to(received_ref[slot, asked_row:, :], outgoing_ref.shape[1:])
+        chosen = rates_ref[0]
+        for patch in range(1, rates_ref.shape[0]):
+            chosen = jnp.where(asked == patch, rates_ref[patch], chosen)
+        outgoing_ref[slot] = chosen
 
     slots = outgoing_ref.shape[0]
     if slots <= 8:
@@ -333,18 +351,25 @@
 
 
 def last_block_kernel(
-    prestress_ref, friction_ref, load_ref, kept_ref, came_ref, others_ref, first_ref, second_ref,
-    out_ref,
-):
-    patches = others_ref.shape[0]
-    for patch in range(2 * patches):
-        out_ref[patch, :BLOCK, :] = first_ref[patch]
-        out_ref[patch, BLOCK : 2 * BLOCK, :] = second_ref[patch]
+    prestress_ref, friction_ref, load_ref, kept_ref, came_ref, others_ref, begun_ref, out_ref,
+    rates, sems,
+):
+    known, patches = others_ref.shape[0], rates.shape[0]
+    copies = [
+        pltpu.make_async_copy(
+            rates.at[patch], out_ref.at[known + patch, 2 * BLOCK :], sems.at[patch]
+        )
+        for patch in range(patches)
+    ]
+    others = pltpu.make_async_copy(others_ref, out_ref.at[:known, 2 * BLOCK :], sems.at[patches])
+    others.start()
     for patch in range(patches):
-        out_ref[patch, 2 * BLOCK :, :] = others_ref[patch]
-        out_ref[patches + patch, 2 * BLOCK :, :] = solve_patch(
-            2, patch, patches, prestress_ref, friction_ref, load_ref, kept_ref, came_ref
+        rates[patch] = solve_patch(
+            2, patch, known, prestress_ref, friction_ref, load_ref, kept_ref, came_ref
         )
+        copies[patch].start()
+    for copy in copies + [others]:
+        copy.wait()
 
 
 def local(interactions, list_lengths, kernels, prestress, friction, load_rate):
@@ -366,7 +391,6 @@
         name="pack",
     )(*map(in_hbm, (interactions, prestress, friction, load_rate)))
     received = lax.all_to_all(packed, "recv", split_axis=0, concat_axis=0, tiled=True)
-    asked = received[:, -1, 0].astype(jnp.int32)
 
     late_lags = lag_count // 4
     early = jax.ShapeDtypeStruct((2 * ker_count, width, (lag_count - late_lags) * width), bf16)
@@ -396,17 +420,13 @@
         name="prepare",
     )(list_lengths, in_hbm(interactions), kernels)
     late_shape, late = jax.ShapeDtypeStruct(late_shape, bf16), in_hbm(late)
-    first_rates = pl.pallas_call(
-        first_block_kernel,
-        in_specs=[VMEM] * 3,
-        out_specs=VMEM,
-        out_shape=jax.ShapeDtypeStruct((patch_count, BLOCK, width), f32),
-        compiler_params=grant(2),
-        name="first_block",
-    )(prestress, friction, load_rate)
-
-    group_patches = patch_count // 2
-    half = jax.ShapeDtypeStruct((n_src // 2, group_patches, BLOCK, width), f32)
+    last_patches = patch_count // 4
+    group_sizes = patch_count - last_patches, last_patches
+    halves = [
+        jax.ShapeDtypeStruct((n_src // 2, size, BLOCK, width), f32)
+        for size in group_sizes
+        for part in range(2)
+    ]
     rates_tail = jax.ShapeDtypeStruct((n_recv, lag_count, width), f32)
     responses_tail = jax.ShapeDtypeStruct((ker_count, n_recv, lag_count, width), f32)
     chunk = min(8, n_recv)
@@ -415,6 +435,8 @@
         pltpu.VMEM((n_recv, lag_count + BLOCK, width), f32),
         pltpu.VMEM((2 * chunk * BLOCK, lag_count * width), bf16),
         pltpu.VMEM((ker_count, n_recv, lag_count + BLOCK, width), f32),
+        pltpu.SMEM((2, interactions.shape[1]), jnp.int32),
+        pltpu.SemaphoreType.DMA,
     ] + [pltpu.VMEM(((group_rows + 1) * BLOCK, width), f32)] * ker_count
 
     def reduce_scatter(kept, sent):
@@ -427,11 +449,11 @@
             sent = kept[quarter:] + came[quarter:]
             kept = kept[:quarter] + came[:quarter]
 
-    rates_group = jax.ShapeDtypeStruct((group_patches, BLOCK, width), f32)
+    rates_group = jax.ShapeDtypeStruct((group_sizes[0], BLOCK, width), f32)
 
     def solve_first_group(block_idx, terms):
         return pl.pallas_call(
-            functools.partial(solve_group_kernel, block_idx, 0),
+            functools.partial(solve_group_kernel, block_idx),
             in_specs=[VMEM] * 5,
             out_specs=VMEM,
             out_shape=rates_group,
@@ -441,9 +463,9 @@
 
     *totals, rates_tail, responses_tail, late = pl.pallas_call(
         first_stress_kernel,
-        in_specs=[SMEM] + [VMEM] * 3 + [HBM],
+        in_specs=[VMEM] * 4 + [HBM],
         out_specs=[VMEM] * 7,
-        out_shape=[half] * 4 + [rates_tail, responses_tail, late_shape],
+        out_shape=halves + [rates_tail, responses_tail, late_shape],
         scratch_shapes=scratch[:3] + [pltpu.SemaphoreType.DMA] + scratch[3:],
         compiler_params=grant(stress_mib),
         name="first_stress",
@@ -451,7 +473,7 @@
     terms = [reduce_scatter(*totals[:2]), reduce_scatter(*totals[2:])]
     second_rates, outgoing = pl.pallas_call(
         middle_block_kernel,
-        in_specs=[SMEM] + [VMEM] * 6,
+        in_specs=[VMEM] * 7,
         out_specs=[VMEM] * 2,
         out_shape=[
             jax.ShapeDtypeStruct((patch_count, BLOCK, width), f32),
@@ -459,28 +481,45 @@
         ],
         compiler_params=grant(4),
         name="middle_block",
-    )(asked, prestress, friction, load_rate, *terms[1], solve_first_group(1, terms[0]))
+    )(received, prestress, friction, load_rate, *terms[1], solve_first_group(1, terms[0]))
     rates = lax.all_to_all(outgoing, "recv", split_axis=0, concat_axis=0, tiled=True)
     totals = pl.pallas_call(
         next_stress_kernel,
-        in_specs=[SMEM] + [VMEM] * 5,
+        in_specs=[VMEM] * 6,
         out_specs=[VMEM] * 4,
-        out_shape=[half] * 4,
+        out_shape=halves,
         scratch_shapes=scratch,
         compiler_params=grant(stress_mib),
         name="next_stress",
     )(table, rates, rates_tail, responses_tail, early, late)
     terms = [reduce_scatter(*totals[:2]), reduce_scatter(*totals[2:])]
+    output = pl.pallas_call(
+        first_blocks_kernel,
+        in_specs=[VMEM] * 4,
+        out_specs=HBM,
+        out_shape=jax.ShapeDtypeStruct((patch_count, BLOCKS * BLOCK, width), f32),
+        scratch_shapes=[
+            pltpu.VMEM((patch_count, BLOCK, width), f32),
+            pltpu.SemaphoreType.DMA((2,)),
+        ],
+        compiler_params=grant(4),
+        name="first_blocks",
+    )(prestress, friction, load_rate, second_rates)
     return pl.pallas_call(
         last_block_kernel,
-        in_specs=[VMEM] * 8,
-        out_specs=VMEM,
-        out_shape=jax.ShapeDtypeStruct((patch_count, BLOCKS * BLOCK, width), f32),
+        in_specs=[VMEM] * 6 + [HBM],
+        out_specs=HBM,
+        out_shape=jax.ShapeDtypeStruct(output.shape, f32),
+        scratch_shapes=[
+            pltpu.VMEM((last_patches, BLOCK, width), f32),
+            pltpu.SemaphoreType.DMA((last_patches + 1,)),
+        ],
+        input_output_aliases={6: 0},
         compiler_params=grant(4),
         name="last_block",
     )(
         prestress, friction, load_rate, *terms[1], solve_first_group(2, terms[0]),
-        first_rates, second_rates,
+        output,
     )
 
 

time: 48.5 us -> 46.5 us (0.959)
  Pallas kernels: 13 us -> 12.1 us
  waiting for transfers between devices: 11.5 us -> 10.7 us
    pallas_call x7, Pallas kernels: 8.37 us -> 7.4 us  [the longest x1 2.76 us: local(): pl.pallas_call(first_stress_kernel, in_specs=[VMEM] * 4 + [HBM], out_spec...]
    ppermute x8, waiting for transfers between devices: 8.05 us -> 7.22 us  [reduce_scatter(): came = lax.ppermute(sent, 'src', pairs)]
  transfers between devices with their start and end apart: 9 -> 9, of which waited for: 7 -> 7; matrix products, arithmetic and copies ran while one was open for 1% -> 0% of each run, Pallas kernels for 8% -> 10%
where the time goes in v3:
time: 46.5 us; the launch traced here: 46.1 us
  starting transfers between devices  12.7 us (27%)
  Pallas kernels  12.1 us (26%)
  waiting for transfers between devices  10.7 us (23%)
  blocking collectives  9.74 us (21%)
  between operations  0.74 us (2%)
    all_to_all x1, blocking collectives, local(): lax.all_to_all(outgoing, 'recv', split_axis=0, concat_axis=0, tiled=True)  9.74 us
    all_to_all x1, starting transfers between devices, local(): lax.all_to_all(packed, 'recv', split_axis=0, concat_axis=0, tiled=True)  7.28 us
    ppermute x8, waiting for transfers between devices, reduce_scatter(): came = lax.ppermute(sent, 'src', pairs)  7.22 us
    ppermute x8, starting transfers between devices, reduce_scatter(): came = lax.ppermute(sent, 'src', pairs)  5.45 us
    all_to_all x1, waiting for transfers between devices, local(): lax.all_to_all(packed, 'recv', split_axis=0, concat_axis=0, tiled=True)  3.49 us
    pallas_call x1, Pallas kernels, local(): pl.pallas_call(functools.partial(prepare_kernel, patch_count), in_specs=[...  3.2 us
    pallas_call x1, Pallas kernels, local(): pl.pallas_call(first_stress_kernel, in_specs=[VMEM] * 4 + [HBM], out_spec...  2.76 us
    pallas_call x1, Pallas kernels, local(): pl.pallas_call(next_stress_kernel, in_specs=[VMEM] * 6, out_specs=[VMEM]...  2.3 us
  transfers between devices with their start and end apart: 9, of which 7 were waited for; matrix products, arithmetic and copies ran while one was open for 0% of the time, Pallas kernels for 10%

profile of v3, /device:TPU:0, one launch (start us, length us, event | category | flops | bytes accessed | tf_op | source)
XLA Modules:
  0.0 46.1 jit_solution(1651723099251464547)
XLA Ops:
  0.0 1.5 %pack.1 = f32[8,25,128]{2,1,0:T(8,128)} custom-call(s32[3,96]{1,0:T(4,128)} %interactions_ref.3, f32[8,128]{1,0:T(8,128)} %prestress_ref.11, f32[8,128]{1,0:T(8,128)} %friction_ref.11, f32[8,128]{1,0:T(8,128)} %load_ref.11), custom_call_target="tpu_custom_call" | custom-call | tf_op jit(solution)/shard_map/pack/pallas_call | solution.py:385
  1.5 7.3 %all-to-all-start = ((f32[8,25,128]{2,1,0:T(8,128)}), f32[8,25,128]{2,1,0:T(8,128)S(1)}, u32[]{:S(2)}, u32[]{:S(2)}) async-start(f32[8,25,128]{2,1,0:T(8,128)} %pack.1), calls=%async_computation | async-start | bytes 262144 | tf_op jit(solution)/shard_map/all_to_all | solution.py:393
  9.4 3.2 %prepare.1 = (bf16[8,128,1536]{2,1,0:T(8,128)(2,1)S(1)}, bf16[96,128,512]{2,1,0:T(8,128)(2,1)}, s32[2,96]{1,0:T(2,128)S(1)}, f32[8,128]{1,0:T(8,128)S(1)}) custom-call(s32[1]{0:T(128)S(6)} %copy.9.lengths_ref, s32[3,96]{1,0:T(4,128)} %interactions_ref.3, f32[4,128,16,128]{3,2,1,0:T(8,128)} %kernel_ref.1), custom_call_target="tpu_custom_call" | custom-call | tf_op jit(solution)/shard_map/prepare/pallas_call | solution.py:400
  12.6 3.5 %all-to-all-done.params_ref.received_ref = f32[8,25,128]{2,1,0:T(8,128)S(1)} async-done(((f32[8,25,128]{2,1,0:T(8,128)}), f32[8,25,128]{2,1,0:T(8,128)S(1)}, u32[]{:S(2)}, u32[]{:S(2)}) %all-to-all-start) | async-done | bytes 102432 | tf_op jit(solution)/shard_map/all_to_all | solution.py:393
  16.1 2.8 %first_stress.1 = (f32[2,6,32,128]{3,2,1,0:T(8,128)S(1)}, f32[2,6,32,128]{3,2,1,0:T(8,128)S(1)}, f32[2,2,32,128]{3,2,1,0:T(8,128)S(1)}, f32[2,2,32,128]{3,2,1,0:...) custom-call(s32[2,96]{1,0:T(2,128)S(1)} %get-tuple-element.22.table_ref, ...), custom_call_target="tpu_custom_call" | custom-call | tf_op jit(solution)/shard_map/first_stress/pallas_call | solution.py:464
  19.0 0.5 %collective-permute-start = (f32[2,2,32,128]{3,2,1,0:T(8,128)S(1)}, f32[2,2,32,128]{3,2,1,0:T(8,128)S(1)}, u32[]{:S(2)}, u32[]{:S(2)}) collective-permute-start(f32[2,2,32,128]{3,2,1,0:T(8,128)S(1)} %get-tuple-element.27), channel_id=1, source_target_pairs={{0,1},{1,0},{2,3},{3,2},{4,5},{5,4},{6,7},{7,6},{8,9},{9,8},{10,11... | collective-permute-start | bytes 196616 | tf_op jit(solution)/shard_map/ppermute | solution.py:445
  19.5 0.9 %collective-permute-done.2 = f32[2,6,32,128]{3,2,1,0:T(8,128)S(1)} collective-permute-done((f32[2,6,32,128]{3,2,1,0:T(8,128)S(1)}, f32[2,6,32,128]{3,2,1,0:T(8,128)S(1)}, u32[]{:S(2)}, u32[]{:S(2)}) %collective-permute-start.2) | collective-permute-done | bytes 196640 | tf_op jit(solution)/shard_map/ppermute | solution.py:445
  20.4 1.6 %collective-permute-start.3 = (f32[1,6,32,128]{3,2,1,0:T(8,128)S(1)}, f32[1,6,32,128]{3,2,1,0:T(8,128)S(1)}, u32[]{:S(2)}, u32[]{:S(2)}) collective-permute-start(f32[1,6,32,128]{3,2,1,0:T(8,128)S(1)} %get-tuple-element.41), channel_id=1, source_target_pairs={{0,2},{1,3},{2,0},{3,1},{4,6},{5,7},{6,4},{7,5},{8,10},{9,11},{10,... | collective-permute-start | bytes 294920 | tf_op jit(solution)/shard_map/ppermute | solution.py:445
  22.0 0.6 %collective-permute-start.1 = (f32[1,2,32,128]{3,2,1,0:T(8,128)S(1)}, f32[1,2,32,128]{3,2,1,0:T(8,128)S(1)}, u32[]{:S(2)}, u32[]{:S(2)}) collective-permute-start(f32[1,2,32,128]{3,2,1,0:T(8,128)S(1)} %get-tuple-element.45), channel_id=1, source_target_pairs={{0,2},{1,3},{2,0},{3,1},{4,6},{5,7},{6,4},{7,5},{8,10},{9,11},{10,... | collective-permute-start | bytes 98312 | tf_op jit(solution)/shard_map/ppermute | solution.py:445
  22.6 3.1 %collective-permute-done.3.came_ref = f32[1,6,32,128]{3,2,1,0:T(8,128)S(1)} collective-permute-done((f32[1,6,32,128]{3,2,1,0:T(8,128)S(1)}, f32[1,6,32,128]{3,2,1,0:T(8,128)S(1)}, u32[]{:S(2)}, u32[]{:S(2)}) %collective-permute-start.3) | collective-permute-done | bytes 98336 | tf_op jit(solution)/shard_map/ppermute | solution.py:445
  25.7 0.2 solve_group.2.others_ref
  25.9 0.1 collective-permute-done.1.came_ref
  26.0 0.1 middle_block.1
  26.2 9.7 %all_to_all.10.rates_ref = f32[8,32,128]{2,1,0:T(8,128)S(1)} all-to-all(f32[8,32,128]{2,1,0:T(8,128)S(1)} %get-tuple-element.30), channel_id=1, replica_groups=mesh['recv'=8,'src'=4] {'recv'}, dimensions={0} | all-to-all | bytes 262144 | tf_op jit(solution)/shard_map/all_to_all | solution.py:485
  35.9 2.3 %next_stress.1 = (f32[2,6,32,128]{3,2,1,0:T(8,128)S(1)}, f32[2,6,32,128]{3,2,1,0:T(8,128)S(1)}, f32[2,2,32,128]{3,2,1,0:T(8,128)S(1)}, f32[2,2,32,128]{3,2,1,0:T(8,128)S(1)}) custom-call(s32[2,96]{1,0:T(2,128)S(1)} %get-tuple-element.22.table_ref, f32[8,32,128]{2,1,0:T(8,128)S(1)} %all_to_all.10.rates_ref, ...), custom_call_target="tpu_custom_call" | custom-call | tf_op jit(solution)/shard_map/next_stress/pallas_call | solution.py:486
  38.3 0.5 %collective-permute-start.4 = (f32[2,2,32,128]{3,2,1,0:T(8,128)S(1)}, f32[2,2,32,128]{3,2,1,0:T(8,128)S(1)}, u32[]{:S(2)}, u32[]{:S(2)}) collective-permute-start(f32[2,2,32,128]{3,2,1,0:T(8,128)S(1)} %get-tuple-element.35), channel_id=1, source_target_pairs={{0,1},{1,0},{2,3},{3,2},{4,5},{5,4},{6,7},{7,6},{8,9},{9,8},{10,11... | collective-permute-start | bytes 196616 | tf_op jit(solution)/shard_map/ppermute | solution.py:445
  38.8 0.9 %collective-permute-done.6 = f32[2,6,32,128]{3,2,1,0:T(8,128)S(1)} collective-permute-done((f32[2,6,32,128]{3,2,1,0:T(8,128)S(1)}, f32[2,6,32,128]{3,2,1,0:T(8,128)S(1)}, u32[]{:S(2)}, u32[]{:S(2)}) %collective-permute-start.6) | collective-permute-done | bytes 196640 | tf_op jit(solution)/shard_map/ppermute | solution.py:445
  39.7 1.6 %collective-permute-start.7 = (f32[1,6,32,128]{3,2,1,0:T(8,128)S(1)}, f32[1,6,32,128]{3,2,1,0:T(8,128)S(1)}, u32[]{:S(2)}, u32[]{:S(2)}) collective-permute-start(f32[1,6,32,128]{3,2,1,0:T(8,128)S(1)} %get-tuple-element.39), channel_id=1, source_target_pairs={{0,2},{1,3},{2,0},{3,1},{4,6},{5,7},{6,4},{7,5},{8,10},{9,11},{10,... | collective-permute-start | bytes 294920 | tf_op jit(solution)/shard_map/ppermute | solution.py:445
  41.4 0.6 %collective-permute-start.5 = (f32[1,2,32,128]{3,2,1,0:T(8,128)S(1)}, f32[1,2,32,128]{3,2,1,0:T(8,128)S(1)}, u32[]{:S(2)}, u32[]{:S(2)}) collective-permute-start(f32[1,2,32,128]{3,2,1,0:T(8,128)S(1)} %get-tuple-element.43), channel_id=1, source_target_pairs={{0,2},{1,3},{2,0},{3,1},{4,6},{5,7},{6,4},{7,5},{8,10},{9,11},{10,... | collective-permute-start | bytes 98312 | tf_op jit(solution)/shard_map/ppermute | solution.py:445
  41.9 1.0 %first_blocks.1.begun_ref = f32[8,96,128]{2,1,0:T(8,128)} custom-call(f32[8,128]{1,0:T(8,128)S(1)} %copy-done, f32[8,128]{1,0:T(8,128)S(1)} %copy-done.1, f32[8,128]{1,0:T(8,128)S(1)} %copy-done.2, f32[8,32,128]{2,1,0:T(8,128)S(1)} %get-tuple-element.38.second_ref), custom_call_target="tpu_custom_call" | custom-call | tf_op jit(solution)/shard_map/first_blocks/pallas_call | solution.py:496
  42.9 2.1 %collective-permute-done.7.came_ref = f32[1,6,32,128]{3,2,1,0:T(8,128)S(1)} collective-permute-done((f32[1,6,32,128]{3,2,1,0:T(8,128)S(1)}, f32[1,6,32,128]{3,2,1,0:T(8,128)S(1)}, u32[]{:S(2)}, u32[]{:S(2)}) %collective-permute-start.7) | collective-permute-done | bytes 98336 | tf_op jit(solution)/shard_map/ppermute | solution.py:445
  45.0 0.2 solve_group.3.others_ref
  45.3 0.1 collective-permute-done.5.came_ref
  45.4 0.7 %last_block.1 = f32[8,96,128]{2,1,0:T(8,128)} custom-call(f32[8,128]{1,0:T(8,128)S(1)} %copy-done, f32[8,128]{1,0:T(8,128)S(1)} %copy-done.1, f32[8,128]{1,0:T(8,128)S(1)} %copy-done.2, f32[1,2,32,128]{3,2,1,0:T(8,128)S(1)} %get-tuple-element.44.kept_ref, f32[1,2,32,128]{3,2,1,0:T(8,128)S(1)} %collective-permute-done.5.came_ref, ...), custom_call_target="tpu_custom_call", output_to_operand_aliasing={{}: (6, {})} | custom-call | tf_op jit(solution)/shard_map/last_block/pallas_call | solution.py:508
  (14 shorter events, 0.2 us)
Async XLA Ops:
  1.5 14.6 %all-to-all-start = ((f32[8,25,128]{2,1,0:T(8,128)}), f32[8,25,128]{2,1,0:T(8,128)S(1)}, u32[]{:S(2)}, u32[]{:S(2)}) async-start(f32[8,25,128]{2,1,0:T(8,128)} %pack.1), calls=%async_computation | async-start | bytes 262144 | tf_op jit(solution)/shard_map/all_to_all | solution.py:393
  16.1 9.6 %copy-start = (f32[8,128]{1,0:T(8,128)S(1)}, f32[8,128]{1,0:T(8,128)}, u32[]{:S(2)}) copy-start(f32[8,128]{1,0:T(8,128)} %prestress_ref.11) | copy-start | bytes 12292
  16.1 9.6 %copy-start.1 = (f32[8,128]{1,0:T(8,128)S(1)}, f32[8,128]{1,0:T(8,128)}, u32[]{:S(2)}) copy-start(f32[8,128]{1,0:T(8,128)} %friction_ref.11) | copy-start | bytes 12292
  16.1 9.6 %copy-start.2 = (f32[8,128]{1,0:T(8,128)S(1)}, f32[8,128]{1,0:T(8,128)}, u32[]{:S(2)}) copy-start(f32[8,128]{1,0:T(8,128)} %load_ref.11) | copy-start | bytes 12292
  18.9 1.5 %collective-permute-start.2 = (f32[2,6,32,128]{3,2,1,0:T(8,128)S(1)}, f32[2,6,32,128]{3,2,1,0:T(8,128)S(1)}, u32[]{:S(2)}, u32[]{:S(2)}) collective-permute-start(f32[2,6,32,128]{3,2,1,0:T(8,128)S(1)} %get-tuple-element.29), channel_id=1, source_target_pairs={{0,1},{1,0},{2,3},{3,2},{4,5},{5,4},{6,7},{7,6},{8,9},{9,8},{10,11... | collective-permute-start | bytes 589832 | tf_op jit(solution)/shard_map/ppermute | solution.py:445
  19.0 3.1 %collective-permute-start = (f32[2,2,32,128]{3,2,1,0:T(8,128)S(1)}, f32[2,2,32,128]{3,2,1,0:T(8,128)S(1)}, u32[]{:S(2)}, u32[]{:S(2)}) collective-permute-start(f32[2,2,32,128]{3,2,1,0:T(8,128)S(1)} %get-tuple-element.27), channel_id=1, source_target_pairs={{0,1},{1,0},{2,3},{3,2},{4,5},{5,4},{6,7},{7,6},{8,9},{9,8},{10,11... | collective-permute-start | bytes 196616 | tf_op jit(solution)/shard_map/ppermute | solution.py:445
  20.4 5.3 %collective-permute-start.3 = (f32[1,6,32,128]{3,2,1,0:T(8,128)S(1)}, f32[1,6,32,128]{3,2,1,0:T(8,128)S(1)}, u32[]{:S(2)}, u32[]{:S(2)}) collective-permute-start(f32[1,6,32,128]{3,2,1,0:T(8,128)S(1)} %get-tuple-element.41), channel_id=1, source_target_pairs={{0,2},{1,3},{2,0},{3,1},{4,6},{5,7},{6,4},{7,5},{8,10},{9,11},{10,... | collective-permute-start | bytes 294920 | tf_op jit(solution)/shard_map/ppermute | solution.py:445
  22.0 4.0 %collective-permute-start.1 = (f32[1,2,32,128]{3,2,1,0:T(8,128)S(1)}, f32[1,2,32,128]{3,2,1,0:T(8,128)S(1)}, u32[]{:S(2)}, u32[]{:S(2)}) collective-permute-start(f32[1,2,32,128]{3,2,1,0:T(8,128)S(1)} %get-tuple-element.45), channel_id=1, source_target_pairs={{0,2},{1,3},{2,0},{3,1},{4,6},{5,7},{6,4},{7,5},{8,10},{9,11},{10,... | collective-permute-start | bytes 98312 | tf_op jit(solution)/shard_map/ppermute | solution.py:445
  38.2 1.5 %collective-permute-start.6 = (f32[2,6,32,128]{3,2,1,0:T(8,128)S(1)}, f32[2,6,32,128]{3,2,1,0:T(8,128)S(1)}, u32[]{:S(2)}, u32[]{:S(2)}) collective-permute-start(f32[2,6,32,128]{3,2,1,0:T(8,128)S(1)} %get-tuple-element.37), channel_id=1, source_target_pairs={{0,1},{1,0},{2,3},{3,2},{4,5},{5,4},{6,7},{7,6},{8,9},{9,8},{10,11... | collective-permute-start | bytes 589832 | tf_op jit(solution)/shard_map/ppermute | solution.py:445
  38.3 3.1 %collective-permute-start.4 = (f32[2,2,32,128]{3,2,1,0:T(8,128)S(1)}, f32[2,2,32,128]{3,2,1,0:T(8,128)S(1)}, u32[]{:S(2)}, u32[]{:S(2)}) collective-permute-start(f32[2,2,32,128]{3,2,1,0:T(8,128)S(1)} %get-tuple-element.35), channel_id=1, source_target_pairs={{0,1},{1,0},{2,3},{3,2},{4,5},{5,4},{6,7},{7,6},{8,9},{9,8},{10,11... | collective-permute-start | bytes 196616 | tf_op jit(solution)/shard_map/ppermute | solution.py:445
  39.7 5.3 %collective-permute-start.7 = (f32[1,6,32,128]{3,2,1,0:T(8,128)S(1)}, f32[1,6,32,128]{3,2,1,0:T(8,128)S(1)}, u32[]{:S(2)}, u32[]{:S(2)}) collective-permute-start(f32[1,6,32,128]{3,2,1,0:T(8,128)S(1)} %get-tuple-element.39), channel_id=1, source_target_pairs={{0,2},{1,3},{2,0},{3,1},{4,6},{5,7},{6,4},{7,5},{8,10},{9,11},{10,... | collective-permute-start | bytes 294920 | tf_op jit(solution)/shard_map/ppermute | solution.py:445
  41.4 4.0 %collective-permute-start.5 = (f32[1,2,32,128]{3,2,1,0:T(8,128)S(1)}, f32[1,2,32,128]{3,2,1,0:T(8,128)S(1)}, u32[]{:S(2)}, u32[]{:S(2)}) collective-permute-start(f32[1,2,32,128]{3,2,1,0:T(8,128)S(1)} %get-tuple-element.43), channel_id=1, source_target_pairs={{0,2},{1,3},{2,0},{3,1},{4,6},{5,7},{6,4},{7,5},{8,10},{9,11},{10,... | collective-permute-start | bytes 98312 | tf_op jit(solution)/shard_map/ppermute | solution.py:445

commit v4 on v3

--- a/solution.py
+++ b/solution.py
@@ -179,8 +179,8 @@
     chunks = slots // chunk
 
     def clear():
-        for ker in range(ker_count):
-            sums[ker][...] = jnp.zeros_like(sums[ker])
+        for some in sums:
+            some[...] = jnp.zeros_like(some)
 
     if chunks > 1:
         clear()
@@ -229,7 +229,8 @@
         for ker in range(ker_count):
             idx = ker * per_kernel + entry
             place = pl.ds(pl.multiple_of(table[0, idx], BLOCK), BLOCK)
-            sums[ker][place, :] = sums[ker][place, :] + every[pl.ds(table[1, idx], BLOCK), :]
+            some = sums[ker % len(sums)]
+            some[place, :] = some[place, :] + every[pl.ds(table[1, idx], BLOCK), :]
     strips = totals[0].shape[0]
     counts = totals[0].shape[1], totals[2].shape[1]
     for group in range(2):
@@ -239,8 +240,8 @@
                     place = (part * strips + strip) * sum(counts) + group * counts[0] + patch
                     rows = slice(place * BLOCK, (place + 1) * BLOCK)
                     total = sums[0][rows, :]
-                    for ker in range(1, ker_count):
-                        total = total + sums[ker][rows, :]
+                    for some in sums[1:]:
+                        total = total + some[rows, :]
                     totals[2 * group + part][strip, patch] = total
 
 
@@ -420,7 +421,7 @@
         name="prepare",
     )(list_lengths, in_hbm(interactions), kernels)
     late_shape, late = jax.ShapeDtypeStruct(late_shape, bf16), in_hbm(late)
-    last_patches = patch_count // 4
+    last_patches = patch_count * 3 // 8
     group_sizes = patch_count - last_patches, last_patches
     halves = [
         jax.ShapeDtypeStruct((n_src // 2, size, BLOCK, width), f32)
@@ -437,7 +438,7 @@
         pltpu.VMEM((ker_count, n_recv, lag_count + BLOCK, width), f32),
         pltpu.SMEM((2, interactions.shape[1]), jnp.int32),
         pltpu.SemaphoreType.DMA,
-    ] + [pltpu.VMEM(((group_rows + 1) * BLOCK, width), f32)] * ker_count
+    ] + [pltpu.VMEM(((group_rows + 1) * BLOCK, width), f32)] * 2
 
     def reduce_scatter(kept, sent):
         for bit in range(bits):

time: 46.5 us -> 46.5 us (level)
  no operation moved by 1% of the time
where the time goes in v4:
time: 46.5 us; the launch traced here: 46.1 us
  starting transfers between devices  12.7 us (27%)
  Pallas kernels  12 us (26%)
  waiting for transfers between devices  10.8 us (23%)
  blocking collectives  9.74 us (21%)
  between operations  0.73 us (2%)
    all_to_all x1, blocking collectives, local(): lax.all_to_all(outgoing, 'recv', split_axis=0, concat_axis=0, tiled=True)  9.74 us
    ppermute x8, waiting for transfers between devices, reduce_scatter(): came = lax.ppermute(sent, 'src', pairs)  7.35 us
    all_to_all x1, starting transfers between devices, local(): lax.all_to_all(packed, 'recv', split_axis=0, concat_axis=0, tiled=True)  7.28 us
    ppermute x8, starting transfers between devices, reduce_scatter(): came = lax.ppermute(sent, 'src', pairs)  5.45 us
    all_to_all x1, waiting for transfers between devices, local(): lax.all_to_all(packed, 'recv', split_axis=0, concat_axis=0, tiled=True)  3.49 us
    pallas_call x1, Pallas kernels, local(): pl.pallas_call(functools.partial(prepare_kernel, patch_count), in_specs=[...  3.2 us
    pallas_call x1, Pallas kernels, local(): pl.pallas_call(first_stress_kernel, in_specs=[VMEM] * 4 + [HBM], out_spec...  2.7 us
    pallas_call x1, Pallas kernels, local(): pl.pallas_call(next_stress_kernel, in_specs=[VMEM] * 6, out_specs=[VMEM]...  2.23 us
  transfers between devices with their start and end apart: 9, of which 7 were waited for; matrix products, arithmetic and copies ran while one was open for 0% of the time, Pallas kernels for 10%

profile of v4, /device:TPU:0, one launch (start us, length us, event | category | flops | bytes accessed | tf_op | source)
XLA Modules:
  0.0 46.1 jit_solution(9159899110754567881)
XLA Ops:
  0.0 1.5 %pack.1 = f32[8,25,128]{2,1,0:T(8,128)} custom-call(s32[3,96]{1,0:T(4,128)} %interactions_ref.3, f32[8,128]{1,0:T(8,128)} %prestress_ref.11, f32[8,128]{1,0:T(8,128)} %friction_ref.11, f32[8,128]{1,0:T(8,128)} %load_ref.11), custom_call_target="tpu_custom_call" | custom-call | tf_op jit(solution)/shard_map/pack/pallas_call | solution.py:386
  1.5 7.3 %all-to-all-start = ((f32[8,25,128]{2,1,0:T(8,128)}), f32[8,25,128]{2,1,0:T(8,128)S(1)}, u32[]{:S(2)}, u32[]{:S(2)}) async-start(f32[8,25,128]{2,1,0:T(8,128)} %pack.1), calls=%async_computation | async-start | bytes 262144 | tf_op jit(solution)/shard_map/all_to_all | solution.py:394
  9.4 3.2 %prepare.1 = (bf16[8,128,1536]{2,1,0:T(8,128)(2,1)S(1)}, bf16[96,128,512]{2,1,0:T(8,128)(2,1)}, s32[2,96]{1,0:T(2,128)S(1)}, f32[8,128]{1,0:T(8,128)S(1)}) custom-call(s32[1]{0:T(128)S(6)} %copy.9.lengths_ref, s32[3,96]{1,0:T(4,128)} %interactions_ref.3, f32[4,128,16,128]{3,2,1,0:T(8,128)} %kernel_ref.1), custom_call_target="tpu_custom_call" | custom-call | tf_op jit(solution)/shard_map/prepare/pallas_call | solution.py:401
  12.6 3.5 %all-to-all-done.params_ref.received_ref = f32[8,25,128]{2,1,0:T(8,128)S(1)} async-done(((f32[8,25,128]{2,1,0:T(8,128)}), f32[8,25,128]{2,1,0:T(8,128)S(1)}, u32[]{:S(2)}, u32[]{:S(2)}) %all-to-all-start) | async-done | bytes 102432 | tf_op jit(solution)/shard_map/all_to_all | solution.py:394
  16.1 2.7 %first_stress.1 = (f32[2,5,32,128]{3,2,1,0:T(8,128)S(1)}, f32[2,5,32,128]{3,2,1,0:T(8,128)S(1)}, f32[2,3,32,128]{3,2,1,0:T(8,128)S(1)}, f32[2,3,32,128]{3,2,1,0:...) custom-call(s32[2,96]{1,0:T(2,128)S(1)} %get-tuple-element.22.table_ref, ...), custom_call_target="tpu_custom_call" | custom-call | tf_op jit(solution)/shard_map/first_stress/pallas_call | solution.py:465
  18.9 0.5 %collective-permute-start = (f32[2,3,32,128]{3,2,1,0:T(8,128)S(1)}, f32[2,3,32,128]{3,2,1,0:T(8,128)S(1)}, u32[]{:S(2)}, u32[]{:S(2)}) collective-permute-start(f32[2,3,32,128]{3,2,1,0:T(8,128)S(1)} %get-tuple-element.27), channel_id=1, source_target_pairs={{0,1},{1,0},{2,3},{3,2},{4,5},{5,4},{6,7},{7,6},{8,9},{9,8},{10,11... | collective-permute-start | bytes 294920 | tf_op jit(solution)/shard_map/ppermute | solution.py:446
  19.4 0.9 %collective-permute-done.2 = f32[2,5,32,128]{3,2,1,0:T(8,128)S(1)} collective-permute-done((f32[2,5,32,128]{3,2,1,0:T(8,128)S(1)}, f32[2,5,32,128]{3,2,1,0:T(8,128)S(1)}, u32[]{:S(2)}, u32[]{:S(2)}) %collective-permute-start.2) | collective-permute-done | bytes 163872 | tf_op jit(solution)/shard_map/ppermute | solution.py:446
  20.3 1.6 %collective-permute-start.3 = (f32[1,5,32,128]{3,2,1,0:T(8,128)S(1)}, f32[1,5,32,128]{3,2,1,0:T(8,128)S(1)}, u32[]{:S(2)}, u32[]{:S(2)}) collective-permute-start(f32[1,5,32,128]{3,2,1,0:T(8,128)S(1)} %get-tuple-element.41), channel_id=1, source_target_pairs={{0,2},{1,3},{2,0},{3,1},{4,6},{5,7},{6,4},{7,5},{8,10},{9,11},{10,... | collective-permute-start | bytes 245768 | tf_op jit(solution)/shard_map/ppermute | solution.py:446
  21.9 0.6 %collective-permute-start.1 = (f32[1,3,32,128]{3,2,1,0:T(8,128)S(1)}, f32[1,3,32,128]{3,2,1,0:T(8,128)S(1)}, u32[]{:S(2)}, u32[]{:S(2)}) collective-permute-start(f32[1,3,32,128]{3,2,1,0:T(8,128)S(1)} %get-tuple-element.45), channel_id=1, source_target_pairs={{0,2},{1,3},{2,0},{3,1},{4,6},{5,7},{6,4},{7,5},{8,10},{9,11},{10,... | collective-permute-start | bytes 147464 | tf_op jit(solution)/shard_map/ppermute | solution.py:446
  22.5 2.8 %collective-permute-done.3.came_ref = f32[1,5,32,128]{3,2,1,0:T(8,128)S(1)} collective-permute-done((f32[1,5,32,128]{3,2,1,0:T(8,128)S(1)}, f32[1,5,32,128]{3,2,1,0:T(8,128)S(1)}, u32[]{:S(2)}, u32[]{:S(2)}) %collective-permute-start.3) | collective-permute-done | bytes 81952 | tf_op jit(solution)/shard_map/ppermute | solution.py:446
  25.3 0.2 solve_group.2.others_ref
  25.5 0.5 %collective-permute-done.1.came_ref = f32[1,3,32,128]{3,2,1,0:T(8,128)S(1)} collective-permute-done((f32[1,3,32,128]{3,2,1,0:T(8,128)S(1)}, f32[1,3,32,128]{3,2,1,0:T(8,128)S(1)}, u32[]{:S(2)}, u32[]{:S(2)}) %collective-permute-start.1) | collective-permute-done | bytes 49184 | tf_op jit(solution)/shard_map/ppermute | solution.py:446
  26.1 0.2 middle_block.1
  26.2 9.7 %all_to_all.10.rates_ref = f32[8,32,128]{2,1,0:T(8,128)S(1)} all-to-all(f32[8,32,128]{2,1,0:T(8,128)S(1)} %get-tuple-element.30), channel_id=1, replica_groups=mesh['recv'=8,'src'=4] {'recv'}, dimensions={0} | all-to-all | bytes 262144 | tf_op jit(solution)/shard_map/all_to_all | solution.py:486
  36.0 2.2 %next_stress.1 = (f32[2,5,32,128]{3,2,1,0:T(8,128)S(1)}, f32[2,5,32,128]{3,2,1,0:T(8,128)S(1)}, f32[2,3,32,128]{3,2,1,0:T(8,128)S(1)}, f32[2,3,32,128]{3,2,1,0:T(8,128)S(1)}) custom-call(s32[2,96]{1,0:T(2,128)S(1)} %get-tuple-element.22.table_ref, f32[8,32,128]{2,1,0:T(8,128)S(1)} %all_to_all.10.rates_ref, ...), custom_call_target="tpu_custom_call" | custom-call | tf_op jit(solution)/shard_map/next_stress/pallas_call | solution.py:487
  38.3 0.5 %collective-permute-start.4 = (f32[2,3,32,128]{3,2,1,0:T(8,128)S(1)}, f32[2,3,32,128]{3,2,1,0:T(8,128)S(1)}, u32[]{:S(2)}, u32[]{:S(2)}) collective-permute-start(f32[2,3,32,128]{3,2,1,0:T(8,128)S(1)} %get-tuple-element.35), channel_id=1, source_target_pairs={{0,1},{1,0},{2,3},{3,2},{4,5},{5,4},{6,7},{7,6},{8,9},{9,8},{10,11... | collective-permute-start | bytes 294920 | tf_op jit(solution)/shard_map/ppermute | solution.py:446
  38.8 0.9 %collective-permute-done.6 = f32[2,5,32,128]{3,2,1,0:T(8,128)S(1)} collective-permute-done((f32[2,5,32,128]{3,2,1,0:T(8,128)S(1)}, f32[2,5,32,128]{3,2,1,0:T(8,128)S(1)}, u32[]{:S(2)}, u32[]{:S(2)}) %collective-permute-start.6) | collective-permute-done | bytes 163872 | tf_op jit(solution)/shard_map/ppermute | solution.py:446
  39.7 1.4 %collective-permute-start.7 = (f32[1,5,32,128]{3,2,1,0:T(8,128)S(1)}, f32[1,5,32,128]{3,2,1,0:T(8,128)S(1)}, u32[]{:S(2)}, u32[]{:S(2)}) collective-permute-start(f32[1,5,32,128]{3,2,1,0:T(8,128)S(1)} %get-tuple-element.39), channel_id=1, source_target_pairs={{0,2},{1,3},{2,0},{3,1},{4,6},{5,7},{6,4},{7,5},{8,10},{9,11},{10,... | collective-permute-start | bytes 245768 | tf_op jit(solution)/shard_map/ppermute | solution.py:446
  41.1 0.7 %collective-permute-start.5 = (f32[1,3,32,128]{3,2,1,0:T(8,128)S(1)}, f32[1,3,32,128]{3,2,1,0:T(8,128)S(1)}, u32[]{:S(2)}, u32[]{:S(2)}) collective-permute-start(f32[1,3,32,128]{3,2,1,0:T(8,128)S(1)} %get-tuple-element.43), channel_id=1, source_target_pairs={{0,2},{1,3},{2,0},{3,1},{4,6},{5,7},{6,4},{7,5},{8,10},{9,11},{10,... | collective-permute-start | bytes 147464 | tf_op jit(solution)/shard_map/ppermute | solution.py:446
  41.9 1.0 %first_blocks.1.begun_ref = f32[8,96,128]{2,1,0:T(8,128)} custom-call(f32[8,128]{1,0:T(8,128)S(1)} %copy-done, f32[8,128]{1,0:T(8,128)S(1)} %copy-done.1, f32[8,128]{1,0:T(8,128)S(1)} %copy-done.2, f32[8,32,128]{2,1,0:T(8,128)S(1)} %get-tuple-element.38.second_ref), custom_call_target="tpu_custom_call" | custom-call | tf_op jit(solution)/shard_map/first_blocks/pallas_call | solution.py:497
  42.9 1.9 %collective-permute-done.7.came_ref = f32[1,5,32,128]{3,2,1,0:T(8,128)S(1)} collective-permute-done((f32[1,5,32,128]{3,2,1,0:T(8,128)S(1)}, f32[1,5,32,128]{3,2,1,0:T(8,128)S(1)}, u32[]{:S(2)}, u32[]{:S(2)}) %collective-permute-start.7) | collective-permute-done | bytes 81952 | tf_op jit(solution)/shard_map/ppermute | solution.py:446
  44.8 0.2 solve_group.3.others_ref
  45.0 0.3 collective-permute-done.5.came_ref
  45.3 0.8 %last_block.1 = f32[8,96,128]{2,1,0:T(8,128)} custom-call(f32[8,128]{1,0:T(8,128)S(1)} %copy-done, f32[8,128]{1,0:T(8,128)S(1)} %copy-done.1, f32[8,128]{1,0:T(8,128)S(1)} %copy-done.2, f32[1,3,32,128]{3,2,1,0:T(8,128)S(1)} %get-tuple-element.44.kept_ref, f32[1,3,32,128]{3,2,1,0:T(8,128)S(1)} %collective-permute-done.5.came_ref, ...), custom_call_target="tpu_custom_call", output_to_operand_aliasing={{}: (6, {})} | custom-call | tf_op jit(solution)/shard_map/last_block/pallas_call | solution.py:509
  (14 shorter events, 0.2 us)
Async XLA Ops:
  1.5 14.6 %all-to-all-start = ((f32[8,25,128]{2,1,0:T(8,128)}), f32[8,25,128]{2,1,0:T(8,128)S(1)}, u32[]{:S(2)}, u32[]{:S(2)}) async-start(f32[8,25,128]{2,1,0:T(8,128)} %pack.1), calls=%async_computation | async-start | bytes 262144 | tf_op jit(solution)/shard_map/all_to_all | solution.py:394
  16.1 9.2 %copy-start = (f32[8,128]{1,0:T(8,128)S(1)}, f32[8,128]{1,0:T(8,128)}, u32[]{:S(2)}) copy-start(f32[8,128]{1,0:T(8,128)} %prestress_ref.11) | copy-start | bytes 12292
  16.1 9.2 %copy-start.1 = (f32[8,128]{1,0:T(8,128)S(1)}, f32[8,128]{1,0:T(8,128)}, u32[]{:S(2)}) copy-start(f32[8,128]{1,0:T(8,128)} %friction_ref.11) | copy-start | bytes 12292
  16.1 9.2 %copy-start.2 = (f32[8,128]{1,0:T(8,128)S(1)}, f32[8,128]{1,0:T(8,128)}, u32[]{:S(2)}) copy-start(f32[8,128]{1,0:T(8,128)} %load_ref.11) | copy-start | bytes 12292
  18.8 1.5 %collective-permute-start.2 = (f32[2,5,32,128]{3,2,1,0:T(8,128)S(1)}, f32[2,5,32,128]{3,2,1,0:T(8,128)S(1)}, u32[]{:S(2)}, u32[]{:S(2)}) collective-permute-start(f32[2,5,32,128]{3,2,1,0:T(8,128)S(1)} %get-tuple-element.29), channel_id=1, source_target_pairs={{0,1},{1,0},{2,3},{3,2},{4,5},{5,4},{6,7},{7,6},{8,9},{9,8},{10,11... | collective-permute-start | bytes 491528 | tf_op jit(solution)/shard_map/ppermute | solution.py:446
  18.9 3.0 %collective-permute-start = (f32[2,3,32,128]{3,2,1,0:T(8,128)S(1)}, f32[2,3,32,128]{3,2,1,0:T(8,128)S(1)}, u32[]{:S(2)}, u32[]{:S(2)}) collective-permute-start(f32[2,3,32,128]{3,2,1,0:T(8,128)S(1)} %get-tuple-element.27), channel_id=1, source_target_pairs={{0,1},{1,0},{2,3},{3,2},{4,5},{5,4},{6,7},{7,6},{8,9},{9,8},{10,11... | collective-permute-start | bytes 294920 | tf_op jit(solution)/shard_map/ppermute | solution.py:446
  20.3 5.0 %collective-permute-start.3 = (f32[1,5,32,128]{3,2,1,0:T(8,128)S(1)}, f32[1,5,32,128]{3,2,1,0:T(8,128)S(1)}, u32[]{:S(2)}, u32[]{:S(2)}) collective-permute-start(f32[1,5,32,128]{3,2,1,0:T(8,128)S(1)} %get-tuple-element.41), channel_id=1, source_target_pairs={{0,2},{1,3},{2,0},{3,1},{4,6},{5,7},{6,4},{7,5},{8,10},{9,11},{10,... | collective-permute-start | bytes 245768 | tf_op jit(solution)/shard_map/ppermute | solution.py:446
  21.9 4.2 %collective-permute-start.1 = (f32[1,3,32,128]{3,2,1,0:T(8,128)S(1)}, f32[1,3,32,128]{3,2,1,0:T(8,128)S(1)}, u32[]{:S(2)}, u32[]{:S(2)}) collective-permute-start(f32[1,3,32,128]{3,2,1,0:T(8,128)S(1)} %get-tuple-element.45), channel_id=1, source_target_pairs={{0,2},{1,3},{2,0},{3,1},{4,6},{5,7},{6,4},{7,5},{8,10},{9,11},{10,... | collective-permute-start | bytes 147464 | tf_op jit(solution)/shard_map/ppermute | solution.py:446
  38.2 1.5 %collective-permute-start.6 = (f32[2,5,32,128]{3,2,1,0:T(8,128)S(1)}, f32[2,5,32,128]{3,2,1,0:T(8,128)S(1)}, u32[]{:S(2)}, u32[]{:S(2)}) collective-permute-start(f32[2,5,32,128]{3,2,1,0:T(8,128)S(1)} %get-tuple-element.37), channel_id=1, source_target_pairs={{0,1},{1,0},{2,3},{3,2},{4,5},{5,4},{6,7},{7,6},{8,9},{9,8},{10,11... | collective-permute-start | bytes 491528 | tf_op jit(solution)/shard_map/ppermute | solution.py:446
  38.3 2.8 %collective-permute-start.4 = (f32[2,3,32,128]{3,2,1,0:T(8,128)S(1)}, f32[2,3,32,128]{3,2,1,0:T(8,128)S(1)}, u32[]{:S(2)}, u32[]{:S(2)}) collective-permute-start(f32[2,3,32,128]{3,2,1,0:T(8,128)S(1)} %get-tuple-element.35), channel_id=1, source_target_pairs={{0,1},{1,0},{2,3},{3,2},{4,5},{5,4},{6,7},{7,6},{8,9},{9,8},{10,11... | collective-permute-start | bytes 294920 | tf_op jit(solution)/shard_map/ppermute | solution.py:446
  39.7 5.1 %collective-permute-start.7 = (f32[1,5,32,128]{3,2,1,0:T(8,128)S(1)}, f32[1,5,32,128]{3,2,1,0:T(8,128)S(1)}, u32[]{:S(2)}, u32[]{:S(2)}) collective-permute-start(f32[1,5,32,128]{3,2,1,0:T(8,128)S(1)} %get-tuple-element.39), channel_id=1, source_target_pairs={{0,2},{1,3},{2,0},{3,1},{4,6},{5,7},{6,4},{7,5},{8,10},{9,11},{10,... | collective-permute-start | bytes 245768 | tf_op jit(solution)/shard_map/ppermute | solution.py:446
  41.1 4.2 %collective-permute-start.5 = (f32[1,3,32,128]{3,2,1,0:T(8,128)S(1)}, f32[1,3,32,128]{3,2,1,0:T(8,128)S(1)}, u32[]{:S(2)}, u32[]{:S(2)}) collective-permute-start(f32[1,3,32,128]{3,2,1,0:T(8,128)S(1)} %get-tuple-element.43), channel_id=1, source_target_pairs={{0,2},{1,3},{2,0},{3,1},{4,6},{5,7},{6,4},{7,5},{8,10},{9,11},{10,... | collective-permute-start | bytes 147464 | tf_op jit(solution)/shard_map/ppermute | solution.py:446

commit v5 on v3

--- a/solution.py
+++ b/solution.py
@@ -32,8 +32,9 @@
         inverse_root = lax.rsqrt(squares)
         magnitude = jnp.log(jnp.abs(rates) + squares * inverse_root)
         inverse_sinh = jnp.where(rates < 0, -magnitude, magnitude)
-        misfit = damping * rates + friction * inverse_sinh - drive
-        rates = rates - misfit / (damping + friction * inverse_root)
+        rates = (drive + friction * (rates * inverse_root - inverse_sinh)) / (
+            damping + friction * inverse_root
+        )
     return rates
 
 

time: 46.5 us -> 46.5 us (level)
  no operation moved by 1% of the time
where the time goes in v5:
time: 46.5 us; the launch traced here: 46.1 us
  starting transfers between devices  12.7 us (27%)
  Pallas kernels  12.1 us (26%)
  waiting for transfers between devices  10.8 us (23%)
  blocking collectives  9.74 us (21%)
  between operations  0.73 us (2%)
    all_to_all x1, blocking collectives, local(): lax.all_to_all(outgoing, 'recv', split_axis=0, concat_axis=0, tiled=True)  9.74 us
    all_to_all x1, starting transfers between devices, local(): lax.all_to_all(packed, 'recv', split_axis=0, concat_axis=0, tiled=True)  7.28 us
    ppermute x8, waiting for transfers between devices, reduce_scatter(): came = lax.ppermute(sent, 'src', pairs)  7.27 us
    ppermute x8, starting transfers between devices, reduce_scatter(): came = lax.ppermute(sent, 'src', pairs)  5.45 us
    all_to_all x1, waiting for transfers between devices, local(): lax.all_to_all(packed, 'recv', split_axis=0, concat_axis=0, tiled=True)  3.49 us
    pallas_call x1, Pallas kernels, local(): pl.pallas_call(functools.partial(prepare_kernel, patch_count), in_specs=[...  3.2 us
    pallas_call x1, Pallas kernels, local(): pl.pallas_call(first_stress_kernel, in_specs=[VMEM] * 4 + [HBM], out_spec...  2.77 us
    pallas_call x1, Pallas kernels, local(): pl.pallas_call(next_stress_kernel, in_specs=[VMEM] * 6, out_specs=[VMEM]...  2.31 us
  transfers between devices with their start and end apart: 9, of which 7 were waited for; matrix products, arithmetic and copies ran while one was open for 0% of the time, Pallas kernels for 10%

profile of v5, /device:TPU:0, one launch (start us, length us, event | category | flops | bytes accessed | tf_op | source)
XLA Modules:
  0.0 46.1 jit_solution(14593958365500191888)
XLA Ops:
  0.0 1.5 %pack.1 = f32[8,25,128]{2,1,0:T(8,128)} custom-call(s32[3,96]{1,0:T(4,128)} %interactions_ref.3, f32[8,128]{1,0:T(8,128)} %prestress_ref.11, f32[8,128]{1,0:T(8,128)} %friction_ref.11, f32[8,128]{1,0:T(8,128)} %load_ref.11), custom_call_target="tpu_custom_call" | custom-call | tf_op jit(solution)/shard_map/pack/pallas_call | solution.py:386
  1.5 7.3 %all-to-all-start = ((f32[8,25,128]{2,1,0:T(8,128)}), f32[8,25,128]{2,1,0:T(8,128)S(1)}, u32[]{:S(2)}, u32[]{:S(2)}) async-start(f32[8,25,128]{2,1,0:T(8,128)} %pack.1), calls=%async_computation | async-start | bytes 262144 | tf_op jit(solution)/shard_map/all_to_all | solution.py:394
  9.4 3.2 %prepare.1 = (bf16[8,128,1536]{2,1,0:T(8,128)(2,1)S(1)}, bf16[96,128,512]{2,1,0:T(8,128)(2,1)}, s32[2,96]{1,0:T(2,128)S(1)}, f32[8,128]{1,0:T(8,128)S(1)}) custom-call(s32[1]{0:T(128)S(6)} %copy.9.lengths_ref, s32[3,96]{1,0:T(4,128)} %interactions_ref.3, f32[4,128,16,128]{3,2,1,0:T(8,128)} %kernel_ref.1), custom_call_target="tpu_custom_call" | custom-call | tf_op jit(solution)/shard_map/prepare/pallas_call | solution.py:401
  12.6 3.5 %all-to-all-done.params_ref.received_ref = f32[8,25,128]{2,1,0:T(8,128)S(1)} async-done(((f32[8,25,128]{2,1,0:T(8,128)}), f32[8,25,128]{2,1,0:T(8,128)S(1)}, u32[]{:S(2)}, u32[]{:S(2)}) %all-to-all-start) | async-done | bytes 102432 | tf_op jit(solution)/shard_map/all_to_all | solution.py:394
  16.1 2.8 %first_stress.1 = (f32[2,6,32,128]{3,2,1,0:T(8,128)S(1)}, f32[2,6,32,128]{3,2,1,0:T(8,128)S(1)}, f32[2,2,32,128]{3,2,1,0:T(8,128)S(1)}, f32[2,2,32,128]{3,2,1,0:...) custom-call(s32[2,96]{1,0:T(2,128)S(1)} %get-tuple-element.22.table_ref, ...), custom_call_target="tpu_custom_call" | custom-call | tf_op jit(solution)/shard_map/first_stress/pallas_call | solution.py:465
  19.0 0.5 %collective-permute-start = (f32[2,2,32,128]{3,2,1,0:T(8,128)S(1)}, f32[2,2,32,128]{3,2,1,0:T(8,128)S(1)}, u32[]{:S(2)}, u32[]{:S(2)}) collective-permute-start(f32[2,2,32,128]{3,2,1,0:T(8,128)S(1)} %get-tuple-element.27), channel_id=1, source_target_pairs={{0,1},{1,0},{2,3},{3,2},{4,5},{5,4},{6,7},{7,6},{8,9},{9,8},{10,11... | collective-permute-start | bytes 196616 | tf_op jit(solution)/shard_map/ppermute | solution.py:446
  19.5 0.9 %collective-permute-done.2 = f32[2,6,32,128]{3,2,1,0:T(8,128)S(1)} collective-permute-done((f32[2,6,32,128]{3,2,1,0:T(8,128)S(1)}, f32[2,6,32,128]{3,2,1,0:T(8,128)S(1)}, u32[]{:S(2)}, u32[]{:S(2)}) %collective-permute-start.2) | collective-permute-done | bytes 196640 | tf_op jit(solution)/shard_map/ppermute | solution.py:446
  20.4 1.6 %collective-permute-start.3 = (f32[1,6,32,128]{3,2,1,0:T(8,128)S(1)}, f32[1,6,32,128]{3,2,1,0:T(8,128)S(1)}, u32[]{:S(2)}, u32[]{:S(2)}) collective-permute-start(f32[1,6,32,128]{3,2,1,0:T(8,128)S(1)} %get-tuple-element.41), channel_id=1, source_target_pairs={{0,2},{1,3},{2,0},{3,1},{4,6},{5,7},{6,4},{7,5},{8,10},{9,11},{10,... | collective-permute-start | bytes 294920 | tf_op jit(solution)/shard_map/ppermute | solution.py:446
  22.0 0.6 %collective-permute-start.1 = (f32[1,2,32,128]{3,2,1,0:T(8,128)S(1)}, f32[1,2,32,128]{3,2,1,0:T(8,128)S(1)}, u32[]{:S(2)}, u32[]{:S(2)}) collective-permute-start(f32[1,2,32,128]{3,2,1,0:T(8,128)S(1)} %get-tuple-element.45), channel_id=1, source_target_pairs={{0,2},{1,3},{2,0},{3,1},{4,6},{5,7},{6,4},{7,5},{8,10},{9,11},{10,... | collective-permute-start | bytes 98312 | tf_op jit(solution)/shard_map/ppermute | solution.py:446
  22.6 3.1 %collective-permute-done.3.came_ref = f32[1,6,32,128]{3,2,1,0:T(8,128)S(1)} collective-permute-done((f32[1,6,32,128]{3,2,1,0:T(8,128)S(1)}, f32[1,6,32,128]{3,2,1,0:T(8,128)S(1)}, u32[]{:S(2)}, u32[]{:S(2)}) %collective-permute-start.3) | collective-permute-done | bytes 98336 | tf_op jit(solution)/shard_map/ppermute | solution.py:446
  25.7 0.2 solve_group.2.others_ref
  25.9 0.1 collective-permute-done.1.came_ref
  26.0 0.1 middle_block.1
  26.2 9.7 %all_to_all.10.rates_ref = f32[8,32,128]{2,1,0:T(8,128)S(1)} all-to-all(f32[8,32,128]{2,1,0:T(8,128)S(1)} %get-tuple-element.30), channel_id=1, replica_groups=mesh['recv'=8,'src'=4] {'recv'}, dimensions={0} | all-to-all | bytes 262144 | tf_op jit(solution)/shard_map/all_to_all | solution.py:486
  35.9 2.3 %next_stress.1 = (f32[2,6,32,128]{3,2,1,0:T(8,128)S(1)}, f32[2,6,32,128]{3,2,1,0:T(8,128)S(1)}, f32[2,2,32,128]{3,2,1,0:T(8,128)S(1)}, f32[2,2,32,128]{3,2,1,0:T(8,128)S(1)}) custom-call(s32[2,96]{1,0:T(2,128)S(1)} %get-tuple-element.22.table_ref, f32[8,32,128]{2,1,0:T(8,128)S(1)} %all_to_all.10.rates_ref, ...), custom_call_target="tpu_custom_call" | custom-call | tf_op jit(solution)/shard_map/next_stress/pallas_call | solution.py:487
  38.3 0.5 %collective-permute-start.4 = (f32[2,2,32,128]{3,2,1,0:T(8,128)S(1)}, f32[2,2,32,128]{3,2,1,0:T(8,128)S(1)}, u32[]{:S(2)}, u32[]{:S(2)}) collective-permute-start(f32[2,2,32,128]{3,2,1,0:T(8,128)S(1)} %get-tuple-element.35), channel_id=1, source_target_pairs={{0,1},{1,0},{2,3},{3,2},{4,5},{5,4},{6,7},{7,6},{8,9},{9,8},{10,11... | collective-permute-start | bytes 196616 | tf_op jit(solution)/shard_map/ppermute | solution.py:446
  38.8 0.9 %collective-permute-done.6 = f32[2,6,32,128]{3,2,1,0:T(8,128)S(1)} collective-permute-done((f32[2,6,32,128]{3,2,1,0:T(8,128)S(1)}, f32[2,6,32,128]{3,2,1,0:T(8,128)S(1)}, u32[]{:S(2)}, u32[]{:S(2)}) %collective-permute-start.6) | collective-permute-done | bytes 196640 | tf_op jit(solution)/shard_map/ppermute | solution.py:446
  39.8 1.6 %collective-permute-start.7 = (f32[1,6,32,128]{3,2,1,0:T(8,128)S(1)}, f32[1,6,32,128]{3,2,1,0:T(8,128)S(1)}, u32[]{:S(2)}, u32[]{:S(2)}) collective-permute-start(f32[1,6,32,128]{3,2,1,0:T(8,128)S(1)} %get-tuple-element.39), channel_id=1, source_target_pairs={{0,2},{1,3},{2,0},{3,1},{4,6},{5,7},{6,4},{7,5},{8,10},{9,11},{10,... | collective-permute-start | bytes 294920 | tf_op jit(solution)/shard_map/ppermute | solution.py:446
  41.4 0.6 %collective-permute-start.5 = (f32[1,2,32,128]{3,2,1,0:T(8,128)S(1)}, f32[1,2,32,128]{3,2,1,0:T(8,128)S(1)}, u32[]{:S(2)}, u32[]{:S(2)}) collective-permute-start(f32[1,2,32,128]{3,2,1,0:T(8,128)S(1)} %get-tuple-element.43), channel_id=1, source_target_pairs={{0,2},{1,3},{2,0},{3,1},{4,6},{5,7},{6,4},{7,5},{8,10},{9,11},{10,... | collective-permute-start | bytes 98312 | tf_op jit(solution)/shard_map/ppermute | solution.py:446
  41.9 1.0 %first_blocks.1.begun_ref = f32[8,96,128]{2,1,0:T(8,128)} custom-call(f32[8,128]{1,0:T(8,128)S(1)} %copy-done, f32[8,128]{1,0:T(8,128)S(1)} %copy-done.1, f32[8,128]{1,0:T(8,128)S(1)} %copy-done.2, f32[8,32,128]{2,1,0:T(8,128)S(1)} %get-tuple-element.38.second_ref), custom_call_target="tpu_custom_call" | custom-call | tf_op jit(solution)/shard_map/first_blocks/pallas_call | solution.py:497
  42.9 2.1 %collective-permute-done.7.came_ref = f32[1,6,32,128]{3,2,1,0:T(8,128)S(1)} collective-permute-done((f32[1,6,32,128]{3,2,1,0:T(8,128)S(1)}, f32[1,6,32,128]{3,2,1,0:T(8,128)S(1)}, u32[]{:S(2)}, u32[]{:S(2)}) %collective-permute-start.7) | collective-permute-done | bytes 98336 | tf_op jit(solution)/shard_map/ppermute | solution.py:446
  45.0 0.2 solve_group.3.others_ref
  45.3 0.1 collective-permute-done.5.came_ref
  45.4 0.7 %last_block.1 = f32[8,96,128]{2,1,0:T(8,128)} custom-call(f32[8,128]{1,0:T(8,128)S(1)} %copy-done, f32[8,128]{1,0:T(8,128)S(1)} %copy-done.1, f32[8,128]{1,0:T(8,128)S(1)} %copy-done.2, f32[1,2,32,128]{3,2,1,0:T(8,128)S(1)} %get-tuple-element.44.kept_ref, f32[1,2,32,128]{3,2,1,0:T(8,128)S(1)} %collective-permute-done.5.came_ref, ...), custom_call_target="tpu_custom_call", output_to_operand_aliasing={{}: (6, {})} | custom-call | tf_op jit(solution)/shard_map/last_block/pallas_call | solution.py:509
  (14 shorter events, 0.2 us)
Async XLA Ops:
  1.5 14.6 %all-to-all-start = ((f32[8,25,128]{2,1,0:T(8,128)}), f32[8,25,128]{2,1,0:T(8,128)S(1)}, u32[]{:S(2)}, u32[]{:S(2)}) async-start(f32[8,25,128]{2,1,0:T(8,128)} %pack.1), calls=%async_computation | async-start | bytes 262144 | tf_op jit(solution)/shard_map/all_to_all | solution.py:394
  16.1 9.6 %copy-start = (f32[8,128]{1,0:T(8,128)S(1)}, f32[8,128]{1,0:T(8,128)}, u32[]{:S(2)}) copy-start(f32[8,128]{1,0:T(8,128)} %prestress_ref.11) | copy-start | bytes 12292
  16.1 9.6 %copy-start.1 = (f32[8,128]{1,0:T(8,128)S(1)}, f32[8,128]{1,0:T(8,128)}, u32[]{:S(2)}) copy-start(f32[8,128]{1,0:T(8,128)} %friction_ref.11) | copy-start | bytes 12292
  16.1 9.6 %copy-start.2 = (f32[8,128]{1,0:T(8,128)S(1)}, f32[8,128]{1,0:T(8,128)}, u32[]{:S(2)}) copy-start(f32[8,128]{1,0:T(8,128)} %load_ref.11) | copy-start | bytes 12292
  18.9 1.5 %collective-permute-start.2 = (f32[2,6,32,128]{3,2,1,0:T(8,128)S(1)}, f32[2,6,32,128]{3,2,1,0:T(8,128)S(1)}, u32[]{:S(2)}, u32[]{:S(2)}) collective-permute-start(f32[2,6,32,128]{3,2,1,0:T(8,128)S(1)} %get-tuple-element.29), channel_id=1, source_target_pairs={{0,1},{1,0},{2,3},{3,2},{4,5},{5,4},{6,7},{7,6},{8,9},{9,8},{10,11... | collective-permute-start | bytes 589832 | tf_op jit(solution)/shard_map/ppermute | solution.py:446
  19.0 3.0 %collective-permute-start = (f32[2,2,32,128]{3,2,1,0:T(8,128)S(1)}, f32[2,2,32,128]{3,2,1,0:T(8,128)S(1)}, u32[]{:S(2)}, u32[]{:S(2)}) collective-permute-start(f32[2,2,32,128]{3,2,1,0:T(8,128)S(1)} %get-tuple-element.27), channel_id=1, source_target_pairs={{0,1},{1,0},{2,3},{3,2},{4,5},{5,4},{6,7},{7,6},{8,9},{9,8},{10,11... | collective-permute-start | bytes 196616 | tf_op jit(solution)/shard_map/ppermute | solution.py:446
  20.4 5.3 %collective-permute-start.3 = (f32[1,6,32,128]{3,2,1,0:T(8,128)S(1)}, f32[1,6,32,128]{3,2,1,0:T(8,128)S(1)}, u32[]{:S(2)}, u32[]{:S(2)}) collective-permute-start(f32[1,6,32,128]{3,2,1,0:T(8,128)S(1)} %get-tuple-element.41), channel_id=1, source_target_pairs={{0,2},{1,3},{2,0},{3,1},{4,6},{5,7},{6,4},{7,5},{8,10},{9,11},{10,... | collective-permute-start | bytes 294920 | tf_op jit(solution)/shard_map/ppermute | solution.py:446
  22.0 4.0 %collective-permute-start.1 = (f32[1,2,32,128]{3,2,1,0:T(8,128)S(1)}, f32[1,2,32,128]{3,2,1,0:T(8,128)S(1)}, u32[]{:S(2)}, u32[]{:S(2)}) collective-permute-start(f32[1,2,32,128]{3,2,1,0:T(8,128)S(1)} %get-tuple-element.45), channel_id=1, source_target_pairs={{0,2},{1,3},{2,0},{3,1},{4,6},{5,7},{6,4},{7,5},{8,10},{9,11},{10,... | collective-permute-start | bytes 98312 | tf_op jit(solution)/shard_map/ppermute | solution.py:446
  38.2 1.5 %collective-permute-start.6 = (f32[2,6,32,128]{3,2,1,0:T(8,128)S(1)}, f32[2,6,32,128]{3,2,1,0:T(8,128)S(1)}, u32[]{:S(2)}, u32[]{:S(2)}) collective-permute-start(f32[2,6,32,128]{3,2,1,0:T(8,128)S(1)} %get-tuple-element.37), channel_id=1, source_target_pairs={{0,1},{1,0},{2,3},{3,2},{4,5},{5,4},{6,7},{7,6},{8,9},{9,8},{10,11... | collective-permute-start | bytes 589832 | tf_op jit(solution)/shard_map/ppermute | solution.py:446
  38.3 3.0 %collective-permute-start.4 = (f32[2,2,32,128]{3,2,1,0:T(8,128)S(1)}, f32[2,2,32,128]{3,2,1,0:T(8,128)S(1)}, u32[]{:S(2)}, u32[]{:S(2)}) collective-permute-start(f32[2,2,32,128]{3,2,1,0:T(8,128)S(1)} %get-tuple-element.35), channel_id=1, source_target_pairs={{0,1},{1,0},{2,3},{3,2},{4,5},{5,4},{6,7},{7,6},{8,9},{9,8},{10,11... | collective-permute-start | bytes 196616 | tf_op jit(solution)/shard_map/ppermute | solution.py:446
  39.8 5.3 %collective-permute-start.7 = (f32[1,6,32,128]{3,2,1,0:T(8,128)S(1)}, f32[1,6,32,128]{3,2,1,0:T(8,128)S(1)}, u32[]{:S(2)}, u32[]{:S(2)}) collective-permute-start(f32[1,6,32,128]{3,2,1,0:T(8,128)S(1)} %get-tuple-element.39), channel_id=1, source_target_pairs={{0,2},{1,3},{2,0},{3,1},{4,6},{5,7},{6,4},{7,5},{8,10},{9,11},{10,... | collective-permute-start | bytes 294920 | tf_op jit(solution)/shard_map/ppermute | solution.py:446
  41.4 4.0 %collective-permute-start.5 = (f32[1,2,32,128]{3,2,1,0:T(8,128)S(1)}, f32[1,2,32,128]{3,2,1,0:T(8,128)S(1)}, u32[]{:S(2)}, u32[]{:S(2)}) collective-permute-start(f32[1,2,32,128]{3,2,1,0:T(8,128)S(1)} %get-tuple-element.43), channel_id=1, source_target_pairs={{0,2},{1,3},{2,0},{3,1},{4,6},{5,7},{6,4},{7,5},{8,10},{9,11},{10,... | collective-permute-start | bytes 98312 | tf_op jit(solution)/shard_map/ppermute | solution.py:446

commit v6 on v4

--- a/solution.py
+++ b/solution.py
@@ -32,8 +32,9 @@
         inverse_root = lax.rsqrt(squares)
         magnitude = jnp.log(jnp.abs(rates) + squares * inverse_root)
         inverse_sinh = jnp.where(rates < 0, -magnitude, magnitude)
-        misfit = damping * rates + friction * inverse_sinh - drive
-        rates = rates - misfit / (damping + friction * inverse_root)
+        rates = (drive + friction * (rates * inverse_root - inverse_sinh)) / (
+            damping + friction * inverse_root
+        )
     return rates
 
 
@@ -421,7 +422,7 @@
         name="prepare",
     )(list_lengths, in_hbm(interactions), kernels)
     late_shape, late = jax.ShapeDtypeStruct(late_shape, bf16), in_hbm(late)
-    last_patches = patch_count * 3 // 8
+    last_patches = patch_count // 4
     group_sizes = patch_count - last_patches, last_patches
     halves = [
         jax.ShapeDtypeStruct((n_src // 2, size, BLOCK, width), f32)

time: 46.5 us -> 46.3 us (level)
  no operation moved by 1% of the time
where the time goes in v6:
time: 46.3 us; the launch traced here: 46 us
  starting transfers between devices  12.7 us (27%)
  Pallas kernels  11.9 us (26%)
  waiting for transfers between devices  10.8 us (23%)
  blocking collectives  9.74 us (21%)
  between operations  0.73 us (2%)
    all_to_all x1, blocking collectives, local(): lax.all_to_all(outgoing, 'recv', split_axis=0, concat_axis=0, tiled=True)  9.74 us
    all_to_all x1, starting transfers between devices, local(): lax.all_to_all(packed, 'recv', split_axis=0, concat_axis=0, tiled=True)  7.28 us
    ppermute x8, waiting for transfers between devices, reduce_scatter(): came = lax.ppermute(sent, 'src', pairs)  7.27 us
    ppermute x8, starting transfers between devices, reduce_scatter(): came = lax.ppermute(sent, 'src', pairs)  5.45 us
    all_to_all x1, waiting for transfers between devices, local(): lax.all_to_all(packed, 'recv', split_axis=0, concat_axis=0, tiled=True)  3.49 us
    pallas_call x1, Pallas kernels, local(): pl.pallas_call(functools.partial(prepare_kernel, patch_count), in_specs=[...  3.2 us
    pallas_call x1, Pallas kernels, local(): pl.pallas_call(first_stress_kernel, in_specs=[VMEM] * 4 + [HBM], out_spec...  2.7 us
    pallas_call x1, Pallas kernels, local(): pl.pallas_call(next_stress_kernel, in_specs=[VMEM] * 6, out_specs=[VMEM]...  2.24 us
  transfers between devices with their start and end apart: 9, of which 7 were waited for; matrix products, arithmetic and copies ran while one was open for 0% of the time, Pallas kernels for 10%

profile of v6, /device:TPU:0, one launch (start us, length us, event | category | flops | bytes accessed | tf_op | source)
XLA Modules:
  0.0 46.0 jit_solution(11259933483646928026)
XLA Ops:
  0.0 1.5 %pack.1 = f32[8,25,128]{2,1,0:T(8,128)} custom-call(s32[3,96]{1,0:T(4,128)} %interactions_ref.3, f32[8,128]{1,0:T(8,128)} %prestress_ref.11, f32[8,128]{1,0:T(8,128)} %friction_ref.11, f32[8,128]{1,0:T(8,128)} %load_ref.11), custom_call_target="tpu_custom_call" | custom-call | tf_op jit(solution)/shard_map/pack/pallas_call | solution.py:387
  1.5 7.3 %all-to-all-start = ((f32[8,25,128]{2,1,0:T(8,128)}), f32[8,25,128]{2,1,0:T(8,128)S(1)}, u32[]{:S(2)}, u32[]{:S(2)}) async-start(f32[8,25,128]{2,1,0:T(8,128)} %pack.1), calls=%async_computation | async-start | bytes 262144 | tf_op jit(solution)/shard_map/all_to_all | solution.py:395
  9.4 3.2 %prepare.1 = (bf16[8,128,1536]{2,1,0:T(8,128)(2,1)S(1)}, bf16[96,128,512]{2,1,0:T(8,128)(2,1)}, s32[2,96]{1,0:T(2,128)S(1)}, f32[8,128]{1,0:T(8,128)S(1)}) custom-call(s32[1]{0:T(128)S(6)} %copy.9.lengths_ref, s32[3,96]{1,0:T(4,128)} %interactions_ref.3, f32[4,128,16,128]{3,2,1,0:T(8,128)} %kernel_ref.1), custom_call_target="tpu_custom_call" | custom-call | tf_op jit(solution)/shard_map/prepare/pallas_call | solution.py:402
  12.6 3.5 %all-to-all-done.params_ref.received_ref = f32[8,25,128]{2,1,0:T(8,128)S(1)} async-done(((f32[8,25,128]{2,1,0:T(8,128)}), f32[8,25,128]{2,1,0:T(8,128)S(1)}, u32[]{:S(2)}, u32[]{:S(2)}) %all-to-all-start) | async-done | bytes 102432 | tf_op jit(solution)/shard_map/all_to_all | solution.py:395
  16.1 2.7 %first_stress.1 = (f32[2,6,32,128]{3,2,1,0:T(8,128)S(1)}, f32[2,6,32,128]{3,2,1,0:T(8,128)S(1)}, f32[2,2,32,128]{3,2,1,0:T(8,128)S(1)}, f32[2,2,32,128]{3,2,1,0:...) custom-call(s32[2,96]{1,0:T(2,128)S(1)} %get-tuple-element.22.table_ref, ...), custom_call_target="tpu_custom_call" | custom-call | tf_op jit(solution)/shard_map/first_stress/pallas_call | solution.py:466
  18.9 0.5 %collective-permute-start = (f32[2,2,32,128]{3,2,1,0:T(8,128)S(1)}, f32[2,2,32,128]{3,2,1,0:T(8,128)S(1)}, u32[]{:S(2)}, u32[]{:S(2)}) collective-permute-start(f32[2,2,32,128]{3,2,1,0:T(8,128)S(1)} %get-tuple-element.27), channel_id=1, source_target_pairs={{0,1},{1,0},{2,3},{3,2},{4,5},{5,4},{6,7},{7,6},{8,9},{9,8},{10,11... | collective-permute-start | bytes 196616 | tf_op jit(solution)/shard_map/ppermute | solution.py:447
  19.4 0.9 %collective-permute-done.2 = f32[2,6,32,128]{3,2,1,0:T(8,128)S(1)} collective-permute-done((f32[2,6,32,128]{3,2,1,0:T(8,128)S(1)}, f32[2,6,32,128]{3,2,1,0:T(8,128)S(1)}, u32[]{:S(2)}, u32[]{:S(2)}) %collective-permute-start.2) | collective-permute-done | bytes 196640 | tf_op jit(solution)/shard_map/ppermute | solution.py:447
  20.4 1.6 %collective-permute-start.3 = (f32[1,6,32,128]{3,2,1,0:T(8,128)S(1)}, f32[1,6,32,128]{3,2,1,0:T(8,128)S(1)}, u32[]{:S(2)}, u32[]{:S(2)}) collective-permute-start(f32[1,6,32,128]{3,2,1,0:T(8,128)S(1)} %get-tuple-element.41), channel_id=1, source_target_pairs={{0,2},{1,3},{2,0},{3,1},{4,6},{5,7},{6,4},{7,5},{8,10},{9,11},{10,... | collective-permute-start | bytes 294920 | tf_op jit(solution)/shard_map/ppermute | solution.py:447
  22.0 0.6 %collective-permute-start.1 = (f32[1,2,32,128]{3,2,1,0:T(8,128)S(1)}, f32[1,2,32,128]{3,2,1,0:T(8,128)S(1)}, u32[]{:S(2)}, u32[]{:S(2)}) collective-permute-start(f32[1,2,32,128]{3,2,1,0:T(8,128)S(1)} %get-tuple-element.45), channel_id=1, source_target_pairs={{0,2},{1,3},{2,0},{3,1},{4,6},{5,7},{6,4},{7,5},{8,10},{9,11},{10,... | collective-permute-start | bytes 98312 | tf_op jit(solution)/shard_map/ppermute | solution.py:447
  22.5 3.1 %collective-permute-done.3.came_ref = f32[1,6,32,128]{3,2,1,0:T(8,128)S(1)} collective-permute-done((f32[1,6,32,128]{3,2,1,0:T(8,128)S(1)}, f32[1,6,32,128]{3,2,1,0:T(8,128)S(1)}, u32[]{:S(2)}, u32[]{:S(2)}) %collective-permute-start.3) | collective-permute-done | bytes 98336 | tf_op jit(solution)/shard_map/ppermute | solution.py:447
  25.6 0.2 solve_group.2.others_ref
  25.9 0.1 collective-permute-done.1.came_ref
  26.0 0.1 middle_block.1
  26.1 9.7 %all_to_all.10.rates_ref = f32[8,32,128]{2,1,0:T(8,128)S(1)} all-to-all(f32[8,32,128]{2,1,0:T(8,128)S(1)} %get-tuple-element.30), channel_id=1, replica_groups=mesh['recv'=8,'src'=4] {'recv'}, dimensions={0} | all-to-all | bytes 262144 | tf_op jit(solution)/shard_map/all_to_all | solution.py:487
  35.8 2.2 %next_stress.1 = (f32[2,6,32,128]{3,2,1,0:T(8,128)S(1)}, f32[2,6,32,128]{3,2,1,0:T(8,128)S(1)}, f32[2,2,32,128]{3,2,1,0:T(8,128)S(1)}, f32[2,2,32,128]{3,2,1,0:T(8,128)S(1)}) custom-call(s32[2,96]{1,0:T(2,128)S(1)} %get-tuple-element.22.table_ref, f32[8,32,128]{2,1,0:T(8,128)S(1)} %all_to_all.10.rates_ref, ...), custom_call_target="tpu_custom_call" | custom-call | tf_op jit(solution)/shard_map/next_stress/pallas_call | solution.py:488
  38.2 0.5 %collective-permute-start.4 = (f32[2,2,32,128]{3,2,1,0:T(8,128)S(1)}, f32[2,2,32,128]{3,2,1,0:T(8,128)S(1)}, u32[]{:S(2)}, u32[]{:S(2)}) collective-permute-start(f32[2,2,32,128]{3,2,1,0:T(8,128)S(1)} %get-tuple-element.35), channel_id=1, source_target_pairs={{0,1},{1,0},{2,3},{3,2},{4,5},{5,4},{6,7},{7,6},{8,9},{9,8},{10,11... | collective-permute-start | bytes 196616 | tf_op jit(solution)/shard_map/ppermute | solution.py:447
  38.7 0.9 %collective-permute-done.6 = f32[2,6,32,128]{3,2,1,0:T(8,128)S(1)} collective-permute-done((f32[2,6,32,128]{3,2,1,0:T(8,128)S(1)}, f32[2,6,32,128]{3,2,1,0:T(8,128)S(1)}, u32[]{:S(2)}, u32[]{:S(2)}) %collective-permute-start.6) | collective-permute-done | bytes 196640 | tf_op jit(solution)/shard_map/ppermute | solution.py:447
  39.6 1.6 %collective-permute-start.7 = (f32[1,6,32,128]{3,2,1,0:T(8,128)S(1)}, f32[1,6,32,128]{3,2,1,0:T(8,128)S(1)}, u32[]{:S(2)}, u32[]{:S(2)}) collective-permute-start(f32[1,6,32,128]{3,2,1,0:T(8,128)S(1)} %get-tuple-element.39), channel_id=1, source_target_pairs={{0,2},{1,3},{2,0},{3,1},{4,6},{5,7},{6,4},{7,5},{8,10},{9,11},{10,... | collective-permute-start | bytes 294920 | tf_op jit(solution)/shard_map/ppermute | solution.py:447
  41.2 0.6 %collective-permute-start.5 = (f32[1,2,32,128]{3,2,1,0:T(8,128)S(1)}, f32[1,2,32,128]{3,2,1,0:T(8,128)S(1)}, u32[]{:S(2)}, u32[]{:S(2)}) collective-permute-start(f32[1,2,32,128]{3,2,1,0:T(8,128)S(1)} %get-tuple-element.43), channel_id=1, source_target_pairs={{0,2},{1,3},{2,0},{3,1},{4,6},{5,7},{6,4},{7,5},{8,10},{9,11},{10,... | collective-permute-start | bytes 98312 | tf_op jit(solution)/shard_map/ppermute | solution.py:447
  41.8 1.0 %first_blocks.1.begun_ref = f32[8,96,128]{2,1,0:T(8,128)} custom-call(f32[8,128]{1,0:T(8,128)S(1)} %copy-done, f32[8,128]{1,0:T(8,128)S(1)} %copy-done.1, f32[8,128]{1,0:T(8,128)S(1)} %copy-done.2, f32[8,32,128]{2,1,0:T(8,128)S(1)} %get-tuple-element.38.second_ref), custom_call_target="tpu_custom_call" | custom-call | tf_op jit(solution)/shard_map/first_blocks/pallas_call | solution.py:498
  42.8 2.1 %collective-permute-done.7.came_ref = f32[1,6,32,128]{3,2,1,0:T(8,128)S(1)} collective-permute-done((f32[1,6,32,128]{3,2,1,0:T(8,128)S(1)}, f32[1,6,32,128]{3,2,1,0:T(8,128)S(1)}, u32[]{:S(2)}, u32[]{:S(2)}) %collective-permute-start.7) | collective-permute-done | bytes 98336 | tf_op jit(solution)/shard_map/ppermute | solution.py:447
  44.9 0.2 solve_group.3.others_ref
  45.1 0.1 collective-permute-done.5.came_ref
  45.2 0.7 %last_block.1 = f32[8,96,128]{2,1,0:T(8,128)} custom-call(f32[8,128]{1,0:T(8,128)S(1)} %copy-done, f32[8,128]{1,0:T(8,128)S(1)} %copy-done.1, f32[8,128]{1,0:T(8,128)S(1)} %copy-done.2, f32[1,2,32,128]{3,2,1,0:T(8,128)S(1)} %get-tuple-element.44.kept_ref, f32[1,2,32,128]{3,2,1,0:T(8,128)S(1)} %collective-permute-done.5.came_ref, ...), custom_call_target="tpu_custom_call", output_to_operand_aliasing={{}: (6, {})} | custom-call | tf_op jit(solution)/shard_map/last_block/pallas_call | solution.py:510
  (14 shorter events, 0.2 us)
Async XLA Ops:
  1.5 14.6 %all-to-all-start = ((f32[8,25,128]{2,1,0:T(8,128)}), f32[8,25,128]{2,1,0:T(8,128)S(1)}, u32[]{:S(2)}, u32[]{:S(2)}) async-start(f32[8,25,128]{2,1,0:T(8,128)} %pack.1), calls=%async_computation | async-start | bytes 262144 | tf_op jit(solution)/shard_map/all_to_all | solution.py:395
  16.1 9.5 %copy-start = (f32[8,128]{1,0:T(8,128)S(1)}, f32[8,128]{1,0:T(8,128)}, u32[]{:S(2)}) copy-start(f32[8,128]{1,0:T(8,128)} %prestress_ref.11) | copy-start | bytes 12292
  16.1 9.5 %copy-start.1 = (f32[8,128]{1,0:T(8,128)S(1)}, f32[8,128]{1,0:T(8,128)}, u32[]{:S(2)}) copy-start(f32[8,128]{1,0:T(8,128)} %friction_ref.11) | copy-start | bytes 12292
  16.1 9.5 %copy-start.2 = (f32[8,128]{1,0:T(8,128)S(1)}, f32[8,128]{1,0:T(8,128)}, u32[]{:S(2)}) copy-start(f32[8,128]{1,0:T(8,128)} %load_ref.11) | copy-start | bytes 12292
  18.8 1.5 %collective-permute-start.2 = (f32[2,6,32,128]{3,2,1,0:T(8,128)S(1)}, f32[2,6,32,128]{3,2,1,0:T(8,128)S(1)}, u32[]{:S(2)}, u32[]{:S(2)}) collective-permute-start(f32[2,6,32,128]{3,2,1,0:T(8,128)S(1)} %get-tuple-element.29), channel_id=1, source_target_pairs={{0,1},{1,0},{2,3},{3,2},{4,5},{5,4},{6,7},{7,6},{8,9},{9,8},{10,11... | collective-permute-start | bytes 589832 | tf_op jit(solution)/shard_map/ppermute | solution.py:447
  18.9 3.0 %collective-permute-start = (f32[2,2,32,128]{3,2,1,0:T(8,128)S(1)}, f32[2,2,32,128]{3,2,1,0:T(8,128)S(1)}, u32[]{:S(2)}, u32[]{:S(2)}) collective-permute-start(f32[2,2,32,128]{3,2,1,0:T(8,128)S(1)} %get-tuple-element.27), channel_id=1, source_target_pairs={{0,1},{1,0},{2,3},{3,2},{4,5},{5,4},{6,7},{7,6},{8,9},{9,8},{10,11... | collective-permute-start | bytes 196616 | tf_op jit(solution)/shard_map/ppermute | solution.py:447
  20.4 5.3 %collective-permute-start.3 = (f32[1,6,32,128]{3,2,1,0:T(8,128)S(1)}, f32[1,6,32,128]{3,2,1,0:T(8,128)S(1)}, u32[]{:S(2)}, u32[]{:S(2)}) collective-permute-start(f32[1,6,32,128]{3,2,1,0:T(8,128)S(1)} %get-tuple-element.41), channel_id=1, source_target_pairs={{0,2},{1,3},{2,0},{3,1},{4,6},{5,7},{6,4},{7,5},{8,10},{9,11},{10,... | collective-permute-start | bytes 294920 | tf_op jit(solution)/shard_map/ppermute | solution.py:447
  22.0 4.0 %collective-permute-start.1 = (f32[1,2,32,128]{3,2,1,0:T(8,128)S(1)}, f32[1,2,32,128]{3,2,1,0:T(8,128)S(1)}, u32[]{:S(2)}, u32[]{:S(2)}) collective-permute-start(f32[1,2,32,128]{3,2,1,0:T(8,128)S(1)} %get-tuple-element.45), channel_id=1, source_target_pairs={{0,2},{1,3},{2,0},{3,1},{4,6},{5,7},{6,4},{7,5},{8,10},{9,11},{10,... | collective-permute-start | bytes 98312 | tf_op jit(solution)/shard_map/ppermute | solution.py:447
  38.1 1.5 %collective-permute-start.6 = (f32[2,6,32,128]{3,2,1,0:T(8,128)S(1)}, f32[2,6,32,128]{3,2,1,0:T(8,128)S(1)}, u32[]{:S(2)}, u32[]{:S(2)}) collective-permute-start(f32[2,6,32,128]{3,2,1,0:T(8,128)S(1)} %get-tuple-element.37), channel_id=1, source_target_pairs={{0,1},{1,0},{2,3},{3,2},{4,5},{5,4},{6,7},{7,6},{8,9},{9,8},{10,11... | collective-permute-start | bytes 589832 | tf_op jit(solution)/shard_map/ppermute | solution.py:447
  38.2 3.0 %collective-permute-start.4 = (f32[2,2,32,128]{3,2,1,0:T(8,128)S(1)}, f32[2,2,32,128]{3,2,1,0:T(8,128)S(1)}, u32[]{:S(2)}, u32[]{:S(2)}) collective-permute-start(f32[2,2,32,128]{3,2,1,0:T(8,128)S(1)} %get-tuple-element.35), channel_id=1, source_target_pairs={{0,1},{1,0},{2,3},{3,2},{4,5},{5,4},{6,7},{7,6},{8,9},{9,8},{10,11... | collective-permute-start | bytes 196616 | tf_op jit(solution)/shard_map/ppermute | solution.py:447
  39.6 5.3 %collective-permute-start.7 = (f32[1,6,32,128]{3,2,1,0:T(8,128)S(1)}, f32[1,6,32,128]{3,2,1,0:T(8,128)S(1)}, u32[]{:S(2)}, u32[]{:S(2)}) collective-permute-start(f32[1,6,32,128]{3,2,1,0:T(8,128)S(1)} %get-tuple-element.39), channel_id=1, source_target_pairs={{0,2},{1,3},{2,0},{3,1},{4,6},{5,7},{6,4},{7,5},{8,10},{9,11},{10,... | collective-permute-start | bytes 294920 | tf_op jit(solution)/shard_map/ppermute | solution.py:447
  41.2 4.0 %collective-permute-start.5 = (f32[1,2,32,128]{3,2,1,0:T(8,128)S(1)}, f32[1,2,32,128]{3,2,1,0:T(8,128)S(1)}, u32[]{:S(2)}, u32[]{:S(2)}) collective-permute-start(f32[1,2,32,128]{3,2,1,0:T(8,128)S(1)} %get-tuple-element.43), channel_id=1, source_target_pairs={{0,2},{1,3},{2,0},{3,1},{4,6},{5,7},{6,4},{7,5},{8,10},{9,11},{10,... | collective-permute-start | bytes 98312 | tf_op jit(solution)/shard_map/ppermute | solution.py:447
